TPU v7x, 1024 devices: a whole 8x8x8 slice. The times are simulated.
1024 devices in a mesh: pp: 4 (over y_hi), fsdp: 64 (over x, z), tp: 4 (over y_lo, core).
Axes of the slice: x: 8, y: 8 (y_hi: 4, y_lo: 2; y = y_hi * 2 + y_lo), z: 8, core: 2. Of those that a mesh axis runs over, the one named last changes fastest.
Arguments:
- saved_inputs: bfloat16 [4, 8192, 8192], P('pp', 'fsdp', 'tp'), may hold values from -6 to 6
- returned: bfloat16 [4, 8192, 8192], P('pp', 'fsdp', 'tp'), may hold values from -6 to 6
- proj_weight: bfloat16 [4, 8192, 640], P('pp', 'tp', 'fsdp'), may hold values from -0.03125 to 0.03125
- log_rate: float32 [4, 128], P('pp', 'tp'), may hold values from -4.6 to -1.2
- step_bias: float32 [4, 128], P('pp', 'tp'), may hold values from -3 to -1
- skip_gain: float32 [4, 128], P('pp', 'tp'), may hold values from 0.5 to 1.5
Outputs:
- grad_out: bfloat16 [4, 8192, 8192], P('pp', 'fsdp', 'tp')
- weight_grad: float32 [4, 8192, 640], P('pp', 'tp', 'fsdp')
All inputs are finite; a program needn't handle non-finite values.
Results may differ from a plain program's by a relative error of at most 0.0044.
Values may be sent and summed in bfloat16 or wider, within the bound.
No kernel may reach another device: no remote copies, remote signals or barrier semaphores. Data moves between devices by JAX's collectives and lax.ppermute only.
A program may use at most 64 MiB of HBM per device.

v0:
```python
import jax
import jax.numpy as jnp
from jax import lax
from jax.sharding import PartitionSpec as P

HEAD_DIM = 64
STATE = 256
BLOCK = 128


def shifted(value, axis, by):
    count = lax.axis_size(axis)
    return lax.ppermute(value, axis, [(i, (i + by) % count) for i in range(count)])


def state_space(head_input, b_values, c_values, raw_step, log_rate, step_bias, skip_gain):
    length, head_count, head_size = head_input.shape
    blocks = length // BLOCK
    highest = lax.Precision.HIGHEST
    step_size = jax.nn.softplus(raw_step + step_bias[None, :])
    log_decay = -step_size * jnp.exp(log_rate)[None, :]
    block_values = head_input.reshape(blocks, BLOCK, head_count, head_size)
    b_blocks = b_values.reshape(blocks, BLOCK, b_values.shape[1])
    c_blocks = c_values.reshape(blocks, BLOCK, c_values.shape[1])
    cumulative = jnp.cumsum(log_decay.reshape(blocks, BLOCK, head_count), axis=1)
    scaled = block_values * step_size.reshape(blocks, BLOCK, head_count)[..., None]
    scores = jnp.einsum("kin,kjn->kij", c_blocks, b_blocks, precision=highest)
    causal = (jnp.arange(BLOCK)[:, None] >= jnp.arange(BLOCK)[None, :])[None, :, :, None]
    log_gaps = cumulative[:, :, None, :] - cumulative[:, None, :, :]
    mixing = jnp.where(causal, jnp.exp(jnp.where(causal, log_gaps, 0.0)), 0.0) * scores[..., None]
    within = jnp.einsum("kijh,kjhp->kihp", mixing, scaled, precision=highest)
    to_end = jnp.exp(cumulative[:, -1:, :] - cumulative)
    states = jnp.einsum("kjn,kjhp->khnp", b_blocks, scaled * to_end[..., None], precision=highest)
    totals = jnp.exp(cumulative[:, -1, :])

    def advance(running, inputs_pair):
        block_state, block_total = inputs_pair
        return (block_total[:, None, None] * running + block_state, running)

    start_state = jnp.zeros((head_count, b_values.shape[1], head_size), head_input.dtype)
    _, entering = lax.scan(advance, start_state, (states, totals))
    across = (
        jnp.einsum("kin,khnp->kihp", c_blocks, entering, precision=highest)
        * jnp.exp(cumulative)[..., None]
    )
    output = (within + across).reshape(length, head_count, head_size)
    return output + skip_gain[None, :, None] * head_input


def head_share(partial_sums):
    return lax.psum_scatter(partial_sums, "tp", scatter_dimension=0, tiled=True)


def per_device(saved_inputs, returned, proj_weight, log_rate, step_bias, skip_gain):
    inputs = saved_inputs[0]
    row_count, inner_here = inputs.shape
    heads_here = log_rate.shape[1]
    weight_local = proj_weight[0]
    arrived = shifted(returned, "pp", -1)[0]
    weight_full = lax.all_gather(weight_local, "fsdp", axis=1, tiled=True)
    partial_proj = jnp.dot(inputs, weight_full, preferred_element_type=jnp.float32)
    projected = lax.all_gather(head_share(partial_proj), "tp", axis=0, tiled=True)
    head_total = projected.shape[1] - 2 * STATE
    offset = lax.axis_index("tp") * heads_here
    raw_step = lax.dynamic_slice_in_dim(projected, 2 * STATE + offset, heads_here, 1)
    values = inputs.astype(jnp.float32).reshape(row_count, heads_here, HEAD_DIM)

    def local_core(head_input, b_values, c_values, step_raw):
        return state_space(
            head_input, b_values, c_values, step_raw, log_rate[0], step_bias[0], skip_gain[0]
        )

    _, backward = jax.vjp(
        local_core, values, projected[:, :STATE], projected[:, STATE : 2 * STATE], raw_step
    )
    upstream = arrived.astype(jnp.float32)
    grad_x, grad_b, grad_c, grad_raw = backward(upstream.reshape(row_count, heads_here, HEAD_DIM))
    placed = lax.dynamic_update_slice_in_dim(
        jnp.zeros((row_count, head_total), jnp.float32), grad_raw, offset, 1
    )
    grad_share = head_share(jnp.concatenate([grad_b, grad_c, placed], axis=1)).astype(jnp.bfloat16)
    proj_grad = lax.all_gather(grad_share, "tp", axis=0, tiled=True)
    back_proj = lax.dot_general(
        proj_grad, weight_full, (((1,), (1,)), ((), ())), preferred_element_type=jnp.float32
    )
    grad_inputs = (upstream + grad_x.reshape(row_count, inner_here) + back_proj).astype(
        jnp.bfloat16
    )
    share = lax.psum_scatter(
        lax.dot_general(
            proj_grad, inputs, (((0,), (0,)), ((), ())), preferred_element_type=jnp.float32
        ),
        "fsdp",
        scatter_dimension=0,
        tiled=True,
    )
    section_wgrad = share.T
    return (grad_inputs[None], section_wgrad[None])


def solution(mesh):
    placed = (
        P("pp", "fsdp", "tp"),
        P("pp", "fsdp", "tp"),
        P("pp", "tp", "fsdp"),
        P("pp", "tp"),
        P("pp", "tp"),
        P("pp", "tp"),
    )
    return jax.shard_map(
        per_device,
        mesh=mesh,
        in_specs=placed,
        out_specs=(P("pp", "fsdp", "tp"), P("pp", "tp", "fsdp")),
        check_vma=False,
    )
```

profile of v0, /device:TPU:16, one launch (start us, length us, event | category | flops | bytes accessed | tf_op | source)
XLA Modules:
  0.0 461.1 jit_solution(17458775247638793704)
XLA Ops:
  7.2 1.5 copy.113
  8.8 110.5 %all-gather.3.cloned.1.call-done = bf16[1,2048,640]{1,0,2:T(2,128)(2,1)} async-done(((bf16[1,2048,10]{1,0,2:T(2,128)(2,1)}), bf16[1,2048,640]{1,0,2:T(2,128)(2,1)}) %all-gather.3.cloned.1.call-update) | async-done | bytes 2621456 | tf_op jit(solution)/shard_map/all_gather | solution.py:60
  119.3 9.6 %copy.114 = bf16[1,2048,640]{2,1,0:T(8,128)(2,1)S(1)} copy(bf16[1,2048,640]{1,0,2:T(2,128)(2,1)} %all-gather.3.cloned.1.call-done) | data formatting | bytes 5242880 | tf_op jit(solution)/shard_map/all_gather | solution.py:60
  128.9 1.3 fusion.2
  130.3 4.9 %collective-permute-start = (bf16[1,128,2048]{2,1,0:T(8,128)(2,1)}, bf16[1,128,2048]{2,1,0:T(8,128)(2,1)S(1)}, u32[]{:S(2)}, u32[]{:S(2)}) collective-permute-start(bf16[1,128,2048]{2,1,0:T(8,128)(2,1)} %param.7), channel_id=1, source_target_pairs={{0,768},{256,0},{512,256},{768,512},{1,769},{257,1},{513,257},{769... | collective-permute-start | bytes 1572872 | tf_op jit(solution)/shard_map/ppermute | solution.py:13
  135.2 2.0 copy.120
  137.2 2.1 convert_element_type.57
  140.1 15.3 %collective-permute-done = bf16[1,128,2048]{2,1,0:T(8,128)(2,1)S(1)} collective-permute-done((bf16[1,128,2048]{2,1,0:T(8,128)(2,1)}, bf16[1,128,2048]{2,1,0:T(8,128)(2,1)S(1)}, u32[]{:S(2)}, u32[]{:S(2)}) %collective-permute-start) | collective-permute-done | bytes 524320 | tf_op jit(solution)/shard_map/ppermute | solution.py:13
  155.4 1.0 copy.117
  156.4 1.2 copy.127
  157.6 1.1 reduce-scatter.5.cloned.1.call-done
  158.7 7.1 %all_gather.10 = f32[128,640]{1,0:T(8,128)S(1)} all-gather(f32[32,640]{1,0:T(8,128)} %reduce-scatter.5.cloned.1.call-done), channel_id=1, replica_groups=mesh['pp'=4,'fsdp'=64,'tp'=4] {'tp'}, dimensions={0}, use_global_device_ids=true | all-gather | bytes 409600 | tf_op jit(solution)/shard_map/all_gather | solution.py:62
  165.8 2.8 convolution_bitcast_fusion
  168.6 0.9 fusion.47
  170.3 1.6 reduce_window_sum.26
  171.9 1.5 copy.115
  173.4 1.3 exponential_multiply_fusion
  174.7 2.8 fusion.24
  178.1 1.6 copy.130
  179.7 1.3 bitcast_exponential_fusion
  181.0 5.1 %multiply_reduce_fusion = (f32[128,32]{0,1:T(8,128)}, f32[128,32]{0,1:T(8,128)}, f32[1,128,32,64]{1,3,2,0:T(8,128)}) fusion(f32[1,128,32,64]{1,3,2,0:T(8,128)} %convolution_bitcast_fusion, f32[1,128,32,64]{1,3,2,0:T(8,128)} %bitcast.151, f32[128,32]{0,1:T(8,128)} %copy.118, bf16[32,64,128]{2,1,0:T(8,128)(2,1)} %bitcast.155, f32[128,128]{1,0:T(8,128)} %fusion.47, ...), kind=kOutput, calls=%fused_computation.37 | convolution fusion | flops 406839296 | bytes 3833856 | tf_op jit(solution)/shard_map/transpose(jvp(kijh,kjhp->kihp))/dot_general | solution.py:31
  186.1 1.4 copy.129
  187.6 1.3 multiply_reduce_fusion.3
  188.9 2.2 bitcast_multiply_fusion.2
  191.0 1.4 copy.133
  192.5 5.1 %fusion.21 = (f32[128,32]{0,1:T(8,128)}, f32[128,32]{0,1:T(8,128)}, f32[128,128]{0,1:T(8,128)}) fusion(f32[128,128]{0,1:T(8,128)} %copy.130, f32[128,32]{0,1:T(8,128)} %bitcast.158, pred[128,128]{0,1:T(8,128)(4,1)} %copy-done.4, bf16[32,64,128]{2,1,0:T(8,128)(2,1)} %bitcast.156, f32[128,32,64]{0,2,1:T(8,128)} %bitcast.152, f32[128,32]{0,1:T(8,128)} %copy.118), kind=kOutput, calls=%fused_computation.21 | convolution fusion | flops 408657920 | bytes 1785856 | tf_op jit(solution)/shard_map/transpose(jvp(kijh,kjhp->kihp))/dot_general | solution.py:31
  197.5 1.5 copy.132
  199.0 2.3 multiply_reduce_fusion.1
  201.3 1.4 copy.128
  202.8 1.4 copy.131
  204.2 1.6 fusion.55
  205.8 2.6 reduce_window_sum.29
  208.4 1.6 fusion.54
  210.0 1.5 copy.134
  211.5 1.1 mul.223
  212.6 2.5 copy.123
  215.2 2.3 convert_multiply_fusion
  217.5 2.6 copy.124
  220.1 3.2 convolution_bitcast_fusion.1
  224.2 3.0 fusion.23
  228.2 23.5 %reduce-scatter.7.cloned.1.call-done = f32[32,640]{1,0:T(8,128)} async-done(((f32[128,640]{1,0:T(8,128)}), f32[32,640]{1,0:T(8,128)}) %reduce-scatter.7.cloned.1.call-update) | async-done | bytes 81936 | tf_op jit(solution)/shard_map/reduce_scatter | solution.py:51
  252.6 6.6 %all_gather.11 = bf16[128,640]{1,0:T(8,128)(2,1)S(1)} all-gather(bf16[32,640]{1,0:T(8,128)(2,1)S(1)} %convert_element_type.65), channel_id=1, replica_groups=mesh['pp'=4,'fsdp'=64,'tp'=4] {'tp'}, dimensions={0}, use_global_device_ids=true | all-gather | bytes 204800 | tf_op jit(solution)/shard_map/all_gather | solution.py:82
  259.2 4.3 fusion.40
  264.2 1.3 dynamic-slice
  266.2 2.5 copy.119
  268.7 3.0 fusion.39
  271.7 181.2 %all-reduce.5.cloned.1.call-done = f32[640,2048]{1,0:T(8,128)} async-done(((f32[640,2048]{1,0:T(8,128)}), f32[640,2048]{1,0:T(8,128)}) %all-reduce.5.cloned.1.call-update) | async-done | bytes 5242896
  452.9 0.9 dynamic-slice_bitcast_fusion
  (41 shorter events, 6.5 us)
Async XLA Ops:
  7.2 112.2 %all-gather.3.cloned.1.call-start = ((), (), s32[]{:S(2)}) async-start(), calls=%async_computation.3 | async-start | bytes 5324800 | tf_op jit(solution)/shard_map/all_gather | solution.py:60
  8.8 120.2 %copy-start = (bf16[1,128,2048]{2,1,0:T(8,128)(2,1)S(1)}, bf16[1,128,2048]{2,1,0:T(8,128)(2,1)}, u32[]{:S(2)}) copy-start(bf16[1,128,2048]{2,1,0:T(8,128)(2,1)} %param.6) | copy-start | bytes 1572868
  8.8 149.9 %reduce-scatter.5.cloned.1.call-start = ((), (), s32[]{:S(2)}) async-start(), calls=%async_computation.2 | async-start | bytes 409600 | tf_op jit(solution)/shard_map/reduce_scatter | solution.py:51
  130.2 9.8 %copy-start.8 = (f32[1,32]{1,0:T(1,128)S(1)}, f32[1,32]{1,0:T(1,128)}, u32[]{:S(2)}) copy-start(f32[1,32]{1,0:T(1,128)} %param.9) | copy-start | bytes 388
  130.3 121.4 %reduce-scatter.7.cloned.1.call-start = ((), (), s32[]{:S(2)}) async-start(), calls=%async_computation.4 | async-start | bytes 409600 | tf_op jit(solution)/shard_map/reduce_scatter | solution.py:51
  130.3 25.1 %collective-permute-start = (bf16[1,128,2048]{2,1,0:T(8,128)(2,1)}, bf16[1,128,2048]{2,1,0:T(8,128)(2,1)S(1)}, u32[]{:S(2)}, u32[]{:S(2)}) collective-permute-start(bf16[1,128,2048]{2,1,0:T(8,128)(2,1)} %param.7), channel_id=1, source_target_pairs={{0,768},{256,0},{512,256},{768,512},{1,769},{257,1},{513,257},{769... | collective-permute-start | bytes 1572872 | tf_op jit(solution)/shard_map/ppermute | solution.py:13
  139.3 18.3 %copy-start.4 = (pred[128,128]{0,1:T(8,128)(4,1)}, pred[128,128]{0,1:T(8,128)(4,1)S(1)}, u32[]{:S(2)}) copy-start(pred[128,128]{0,1:T(8,128)(4,1)S(1)} %iota_compare_fusion) | copy-start | bytes 49156
  140.1 29.5 %copy-start.6 = (f32[32]{0:T(128)}, f32[32]{0:T(128)S(1)}, u32[]{:S(2)}) copy-start(f32[32]{0:T(128)S(1)} %exponential_bitcast_fusion) | copy-start | bytes 388
  140.1 29.4 %copy-start.5 = (f32[1,32]{1,0:T(1,128)S(1)}, f32[1,32]{1,0:T(1,128)}, u32[]{:S(2)}) copy-start(f32[1,32]{1,0:T(1,128)} %param.10) | copy-start | bytes 388
  197.5 14.0 %copy-start.2 = (f32[128,32]{0,1:T(8,128)S(1)}, f32[128,32]{0,1:T(8,128)}, u32[]{:S(2)}) copy-start(f32[128,32]{0,1:T(8,128)} %get-tuple-element.61) | copy-start | bytes 49156
  217.5 5.9 %copy-start.1 = (f32[128,128]{0,1:T(8,128)S(1)}, f32[128,128]{0,1:T(8,128)}, u32[]{:S(2)}) copy-start(f32[128,128]{0,1:T(8,128)} %get-tuple-element.53) | copy-start | bytes 196612
  220.1 7.1 %copy-start.3 = (f32[128,32]{0,1:T(8,128)S(1)}, f32[128,32]{0,1:T(8,128)}, u32[]{:S(2)}) copy-start(f32[128,32]{0,1:T(8,128)} %copy.134) | copy-start | bytes 49156
  228.2 224.7 %all-reduce.5.cloned.1.call-start = ((), (), s32[]{:S(2)}) async-start(), calls=%async_computation.5 | async-start | bytes 10485760
  263.4 0.7 copy-start.7
Sparse Core Ops, SparseCore 0:
  12.8 106.5 all-gather.2
  130.4 28.2 reduce-scatter.4
  228.3 23.3 reduce-scatter.6
  263.6 189.2 all-reduce.4
where the time goes:
time: 463 us; the launch traced here: 461 us
  waiting for transfers between devices  332 us (72%)
  local copies, waits for them, and re-layouts  42 us (9%)
  matrix products  32.2 us (7%)
  other arithmetic  21.9 us (5%)
  between operations  14.6 us (3%)
  blocking collectives  13.7 us (3%)
  starting transfers between devices  5.02 us (1%)
    unnamed x5, waiting for transfers between devices  181 us
    all_gather x1, waiting for transfers between devices, per_device(): weight_full = lax.all_gather(weight_local, 'fsdp', axis=1, tiled=True)  110 us
    reduce_scatter x2, waiting for transfers between devices, head_share(): return lax.psum_scatter(partial_sums, 'tp', scatter_dimension=0, tiled=True)  24.5 us
    ppermute x1, waiting for transfers between devices, shifted(): lax.ppermute(value, axis, [(i, (i + by) % count) for i in range(count)])  15.3 us
    dot_general x2, matrix products, state_space(): within = jnp.einsum('kijh,kjhp->kihp', mixing, scaled, precision=highest)  10.2 us
    all_gather x1, local copies, waits for them, and re-layouts, per_device(): weight_full = lax.all_gather(weight_local, 'fsdp', axis=1, tiled=True)  9.6 us
  transfers between devices with their start and end apart: 5, of which 5 were waited for; matrix products, arithmetic and copies ran while one was open for 3% of the time, Pallas kernels for 0%

commit v1 on v0

v1 whole, which is shorter than its diff:
```python
import jax
import jax.numpy as jnp
from jax import lax
from jax.experimental import pallas as pl
from jax.experimental.pallas import tpu as pltpu
from jax.sharding import PartitionSpec as P

HEAD_DIM = 64
STATE = 256
F32 = jnp.float32
BF16 = jnp.bfloat16
HIGHEST = lax.Precision.HIGHEST
NT = (((1,), (1,)), ((), ()))
NN = (((1,), (0,)), ((), ()))
VMEM_LIMIT = 56 * 1024 * 1024


def dot(a, b, dims=NN, precision=None):
    return lax.dot_general(a, b, dims, precision=precision, preferred_element_type=F32)


def call(kernel, outs, scratch=(), smem=(), inputs=0, name=None):
    specs = [
        pl.BlockSpec(memory_space=pltpu.SMEM if i in smem else pltpu.VMEM) for i in range(inputs)
    ]
    return pl.pallas_call(
        kernel,
        out_shape=outs,
        in_specs=specs,
        out_specs=jax.tree.map(lambda _: pl.BlockSpec(memory_space=pltpu.VMEM), outs),
        scratch_shapes=list(scratch),
        compiler_params=pltpu.CompilerParams(vmem_limit_bytes=VMEM_LIMIT),
        name=name,
    )


def project_kernel(w_ref, x_ref, out_ref, tail_ref):
    groups = w_ref.shape[0] // 8
    inner = x_ref.shape[1]
    quarter = inner // 4
    main = dot(w_ref[:, :inner], x_ref[...], NT)
    tail = None
    for q in range(4):
        tail_ref[...] = dot(w_ref[:, inner:], x_ref[:, q * quarter : (q + 1) * quarter], NT)
        part = tail_ref[pl.ds(q, 2 * groups, 4), :]
        tail = part if tail is None else tail + part
    for g in range(groups):
        out_ref[10 * g : 10 * g + 8, :] = main[8 * g : 8 * g + 8, :]
        out_ref[10 * g + 8 : 10 * g + 10, :] = tail[2 * g : 2 * g + 2, :]


def as_column(row):
    n = row.shape[1]
    at = lax.broadcasted_iota(jnp.int32, (n, n), 0) == lax.broadcasted_iota(jnp.int32, (n, n), 1)
    return jnp.sum(jnp.where(at, jnp.broadcast_to(row, (n, n)), 0.0), axis=1, keepdims=True)


def core_kernel(
    tp_ref, gain_ref, proj_ref, rate_ref, bias_ref, g_ref, x_ref,
    pack_ref, gx_ref,
    cum_ref, cols_ref, row_ref, col_ref, scores_ref,
):
    heads = rate_ref.shape[1]
    t = g_ref.shape[0]
    raw = proj_ref[pl.ds(pl.multiple_of(2 * STATE + tp_ref[0] * heads, heads), heads), :]
    z = raw + as_column(bias_ref[...])
    rate = as_column(jnp.exp(rate_ref[...]))
    step = jnp.maximum(z, 0.0) + jnp.log1p(jnp.exp(-jnp.abs(z)))
    first = lax.broadcasted_iota(jnp.int32, (t, t), 0)
    second = lax.broadcasted_iota(jnp.int32, (t, t), 1)
    cum = dot(-step * rate, jnp.where(first <= second, 1.0, 0.0), NN, HIGHEST)
    cum_ref[...] = cum
    cols_ref[...] = jnp.transpose(
        jnp.concatenate([cum, step, jnp.zeros((t - 2 * heads, t), F32)], axis=0)
    )
    scores = dot(jnp.transpose(proj_ref[:STATE, :]), proj_ref[STATE : 2 * STATE, :], NN, HIGHEST)
    causal = first <= second
    scores_ref[...] = jnp.where(causal, scores, 0.0)
    pack_ref[:t, :] = jnp.zeros((t, t), F32)
    left = second < HEAD_DIM

    def pair(k, carry):
        lanes = pl.ds(pl.multiple_of(k * 2 * HEAD_DIM, 2 * HEAD_DIM), 2 * HEAD_DIM)
        g = g_ref[:, lanes]
        x = x_ref[:, lanes]
        cols = cols_ref[...]
        none = jnp.zeros_like(g)
        gs = (jnp.where(left, g, none), jnp.where(left, none, g))
        moved = jnp.zeros((t, 2 * HEAD_DIM), F32)
        for a in range(2):
            h = 2 * k + a
            product = dot(x, gs[a], NT)
            step_col = cols[:, heads + a : heads + a + 1]
            decay = jnp.exp(jnp.minimum(cum_ref[pl.ds(h, 1), :] - cols[:, a : a + 1], 0.0))
            faded = product * decay
            stepped = faded * step_col
            pack_ref[:t, :] += stepped
            col_ref[...] = jnp.where(
                second == h,
                jnp.sum(faded * scores_ref[...], axis=1, keepdims=True),
                col_ref[...],
            )
            row_ref[pl.ds(h, 1), :] = jnp.sum(stepped * scores_ref[...], axis=0, keepdims=True)
            moved += dot((decay * scores_ref[...]).astype(BF16), gs[a], NN)
        step_both = jnp.where(left, cols[:, heads : heads + 1], cols[:, heads + 1 : heads + 2])
        gain = jnp.where(left, gain_ref[0, 2 * k], gain_ref[0, 2 * k + 1])
        up = g.astype(F32)
        gx_ref[:, lanes] = up + (moved * step_both + gain * up)
        cols_ref[...] = pltpu.roll(cols, t - 2, 1)
        return carry

    lax.fori_loop(0, heads // 2, pair, 0)
    pack_ref[:t, :] = jnp.where(causal, pack_ref[:t, :], 0.0)
    col = jnp.transpose(col_ref[...])[:heads, :]
    dcum = row_ref[...] - step * col
    decayed = dot(dcum, jnp.where(first >= second, 1.0, 0.0), NN, HIGHEST)
    pack_ref[t:, :] = (col - rate * decayed) * (1.0 / (1.0 + jnp.exp(-z)))


def grads_kernel(pack_ref, proj_ref, x_ref, out_ref, main_ref, tail_ref, wide_ref, grad_ref, rows_ref):
    parts, rows, t = pack_ref.shape
    heads = rows - t
    inner = x_ref.shape[1]
    quarter = inner // 4
    groups = out_ref.shape[0] // 8
    scores = pack_ref[0, :t, :]
    for p in range(1, parts):
        scores = scores + pack_ref[p, :t, :]
    grad_ref[:STATE, :] = dot(proj_ref[STATE : 2 * STATE, :], scores, NT, HIGHEST)
    grad_ref[STATE : 2 * STATE, :] = dot(proj_ref[:STATE, :], scores, NN, HIGHEST)
    for p in range(parts):
        grad_ref[2 * STATE + p * heads : 2 * STATE + (p + 1) * heads, :] = pack_ref[p, t:, :]
    for g in range(groups):
        rows_ref[8 * g : 8 * g + 8, :] = grad_ref[10 * g : 10 * g + 8, :]
        rows_ref[8 * groups + 2 * g : 8 * groups + 2 * g + 2, :] = grad_ref[10 * g + 8 : 10 * g + 10, :]
    main = rows_ref[: 8 * groups, :].astype(BF16)
    main_ref[...] = main
    out_ref[:, :inner] = dot(main, x_ref[...]).astype(BF16)
    for q in range(4):
        wide_ref[pl.ds(q, 2 * groups, 4), :] = rows_ref[8 * groups :, :]
    wide = wide_ref[...]
    quarter_of = lax.broadcasted_iota(jnp.int32, wide.shape, 0) % 4
    total = None
    for q in range(4):
        piece = jnp.where(quarter_of == q, wide, 0.0).astype(BF16)
        part = dot(piece, x_ref[:, q * quarter : (q + 1) * quarter])
        total = part if total is None else total + part
    out_ref[:, inner:] = total.astype(BF16)
    tail_ref[...] = wide.astype(BF16)


def back_kernel(main_ref, tail_ref, w_ref, gx_ref, out_ref):
    inner = gx_ref.shape[1]
    quarter = inner // 4
    main = jnp.transpose(main_ref[...].astype(F32)).astype(BF16)
    tail = jnp.transpose(tail_ref[...].astype(F32))
    quarter_of = lax.broadcasted_iota(jnp.int32, tail.shape, 1) % 4
    for q in range(4):
        lanes = slice(q * quarter, (q + 1) * quarter)
        piece = jnp.where(quarter_of == q, tail, 0.0).astype(BF16)
        back = dot(main, w_ref[:, lanes]) + dot(piece, w_ref[:, inner:])
        out_ref[:, lanes] = (gx_ref[:, lanes] + back).astype(BF16)


def per_device(saved_inputs, returned, proj_weight, log_rate, step_bias, skip_gain):
    x = saved_inputs[0]
    t, inner = x.shape
    heads = log_rate.shape[1]
    sections = lax.axis_size("pp")
    groups = lax.axis_size("fsdp")
    tps = lax.axis_size("tp")
    columns = proj_weight.shape[2]
    pcols = columns * groups
    wide = inner + 2 * inner // 8
    arrived = lax.ppermute(
        returned, "pp", [(i, (i - 1) % sections) for i in range(sections)]
    )[0]

    w = proj_weight[0].T
    shard = jnp.concatenate([w[:8], w[8:].reshape(8, inner // 4)], axis=1)
    gathered = lax.all_to_all(
        jnp.broadcast_to(shard[None], (groups, 8, wide)), "fsdp", 0, 0
    ).reshape(groups * 8, wide)

    partial = call(
        project_kernel,
        jax.ShapeDtypeStruct((pcols, t), F32),
        scratch=[pltpu.VMEM((groups * 8, t), F32)],
        inputs=2,
        name="project",
    )(gathered, x)
    share = lax.all_to_all(partial.reshape(tps, pcols // tps, t), "tp", 0, 0).sum(axis=0)
    proj = lax.all_gather(share, "tp", axis=0, tiled=True)

    pack, gx = call(
        core_kernel,
        (
            jax.ShapeDtypeStruct((t + heads, t), F32),
            jax.ShapeDtypeStruct((t, inner), F32),
        ),
        scratch=[
            pltpu.VMEM((heads, t), F32),
            pltpu.VMEM((t, t), F32),
            pltpu.VMEM((heads, t), F32),
            pltpu.VMEM((t, t), F32),
            pltpu.VMEM((t, t), F32),
        ],
        smem=(0, 1),
        inputs=7,
        name="core",
    )(lax.axis_index("tp").reshape(1), skip_gain, proj, log_rate, step_bias, arrived, x)

    packs = lax.all_gather(pack, "tp", axis=0)
    contrib, main, tail = call(
        grads_kernel,
        (
            jax.ShapeDtypeStruct((groups * 8, wide), BF16),
            jax.ShapeDtypeStruct((groups * 8, t), BF16),
            jax.ShapeDtypeStruct((groups * 8, t), BF16),
        ),
        scratch=[
            pltpu.VMEM((groups * 8, t), F32),
            pltpu.VMEM((pcols, t), F32),
            pltpu.VMEM((pcols, t), F32),
        ],
        inputs=3,
        name="grads",
    )(packs, proj, x)
    pieces = lax.all_to_all(contrib.reshape(groups, 8, wide), "fsdp", 0, 0)
    grad_inputs = call(
        back_kernel,
        jax.ShapeDtypeStruct((t, inner), BF16),
        inputs=4,
        name="back",
    )(main, tail, gathered, gx)
    total = pieces.astype(F32).sum(axis=0)
    wgrad = jnp.concatenate([total[:, :inner], total[:, inner:].reshape(2, inner)], axis=0)
    return (grad_inputs[None], wgrad.T[None])


def solution(mesh):
    placed = (
        P("pp", "fsdp", "tp"),
        P("pp", "fsdp", "tp"),
        P("pp", "tp", "fsdp"),
        P("pp", "tp"),
        P("pp", "tp"),
        P("pp", "tp"),
    )
    return jax.shard_map(
        per_device,
        mesh=mesh,
        in_specs=placed,
        out_specs=(P("pp", "fsdp", "tp"), P("pp", "tp", "fsdp")),
        check_vma=False,
    )
```

time: 463 us -> 237 us (0.51)
  the two profiles are of different devices: /device:TPU:16 before, /device:TPU:84 now
where the time goes in v1:
time: 237 us
  blocking collectives  110 us (46%)
  waiting for transfers between devices  85.4 us (36%)
  Pallas kernels  19.4 us (8%)
  starting transfers between devices  18 us (8%)
  local copies, waits for them, and re-layouts  3.23 us (1%)
    all_to_all x1, blocking collectives, per_device(): lax.all_to_all(jnp.broadcast_to(shard[None], (groups, 8, wide)), 'fsdp',...  86.4 us
    all_to_all x1, waiting for transfers between devices, per_device(): pieces = lax.all_to_all(contrib.reshape(groups, 8, wide), 'fsdp', 0, 0)  71.9 us
    all_to_all x1, waiting for transfers between devices, per_device(): lax.all_to_all(partial.reshape(tps, pcols // tps, t), 'tp', 0, 0)  13.6 us
    all_gather x1, blocking collectives, per_device(): proj = lax.all_gather(share, 'tp', axis=0, tiled=True)  12.9 us
    all_to_all x1, starting transfers between devices, per_device(): pieces = lax.all_to_all(contrib.reshape(groups, 8, wide), 'fsdp', 0, 0)  11.3 us
    all_gather x1, blocking collectives, per_device(): packs = lax.all_gather(pack, 'tp', axis=0)  10.4 us
    pallas_call x1, Pallas kernels, per_device(): call(core_kernel, (jax.ShapeDtypeStruct((t + heads, t), F32), jax.ShapeDt...  7.4 us
  transfers between devices with their start and end apart: 3, of which 2 were waited for; matrix products, arithmetic and copies ran while one was open for 0% of the time, Pallas kernels for 2%

profile of v1, /device:TPU:84, one launch (start us, length us, event | category | flops | bytes accessed | tf_op | source)
XLA Modules:
  0.0 236.7 jit_solution(8861525970252021697)
XLA Ops:
  0.6 0.8 slice.17
  1.4 0.8 slice.16
  2.2 0.2 broadcast_in_dim.12
  2.4 86.4 %all_to_all.15 = bf16[64,8,2560]{2,1,0:T(8,128)(2,1)} all-to-all(bf16[64,8,2560]{2,1,0:T(8,128)(2,1)S(1)} %broadcast_in_dim.12), channel_id=1, replica_groups=mesh['pp'=4,'fsdp'=64,'tp'=4] {'fsdp'}, dimensions={0} | all-to-all | bytes 5242880 | tf_op jit(solution)/shard_map/all_to_all | solution.py:181
  88.7 0.0 copy-start.1
  88.7 3.9 %project.1 = f32[640,128]{1,0:T(8,128)} custom-call(bf16[512,2560]{1,0:T(8,128)(2,1)} %bitcast.15, bf16[128,2048]{1,0:T(8,128)(2,1)} %bitcast.17), custom_call_target="tpu_custom_call" | custom-call | tf_op jit(solution)/shard_map/project/pallas_call | solution.py:185
  92.6 4.7 %all-to-all-start.1 = ((f32[4,160,128]{2,1,0:T(8,128)}), f32[4,160,128]{2,1,0:T(8,128)S(1)}, u32[]{:S(2)}, u32[]{:S(2)}) async-start(f32[4,160,128]{2,1,0:T(8,128)} %bitcast.22), calls=%async_computation.1 | async-start | bytes 655360 | tf_op jit(solution)/shard_map/all_to_all | solution.py:192
  97.3 0.0 copy-done.1
  97.3 2.0 collective-permute-start
  99.3 13.6 %all-to-all-done.1 = f32[4,160,128]{2,1,0:T(8,128)S(1)} async-done(((f32[4,160,128]{2,1,0:T(8,128)}), f32[4,160,128]{2,1,0:T(8,128)S(1)}, u32[]{:S(2)}, u32[]{:S(2)}) %all-to-all-start.1) | async-done | bytes 327712 | tf_op jit(solution)/shard_map/all_to_all | solution.py:192
  112.9 12.9 %all_gather.9.proj_ref = f32[640,128]{1,0:T(8,128)} all-gather(f32[160,128]{1,0:T(8,128)S(1)} %reduce_sum.18), channel_id=1, replica_groups=mesh['pp'=4,'fsdp'=64,'tp'=4] {'tp'}, dimensions={0}, use_global_device_ids=true | all-gather | bytes 409600 | tf_op jit(solution)/shard_map/all_gather | solution.py:193
  125.7 0.0 collective-permute-done
  125.7 0.0 copy-start
  125.7 0.8 copy-done
  126.5 7.4 %core.1 = (f32[160,128]{1,0:T(8,128)}, f32[128,2048]{1,0:T(8,128)}) custom-call(s32[1]{0:T(128)} %bitcast.tp_ref, f32[1,32]{1,0:T(1,128)} %gain_ref.1, f32[640,128]{1,0:T(8,128)} %all_gather.9.proj_ref, f32[1,32]{1,0:T(1,128)} %rate_ref.1, f32[1,32]{1,0:T(1,128)} %bias_ref.1, bf16[128,2048]{1,0:T(8,128)(2,1)} %bitcast.24, bf16[128,2048]{1,0:T(8,128)(2,1)} %bitcast.18), custom_call_target="tpu_custom_call" | custom-call | tf_op jit(solution)/shard_map/core/pallas_call | solution.py:195
  133.9 10.4 %all-gather = f32[640,128]{1,0:T(8,128)} all-gather(f32[160,128]{1,0:T(8,128)} %get-tuple-element.7), channel_id=2, replica_groups=mesh['pp'=4,'fsdp'=64,'tp'=4] {'tp'}, dimensions={0}, use_global_device_ids=true | all-gather | bytes 409600 | tf_op jit(solution)/shard_map/all_gather | solution.py:213
  144.3 4.4 %grads.1 = (bf16[512,2560]{1,0:T(8,128)(2,1)}, bf16[512,128]{1,0:T(8,128)(2,1)}, bf16[512,128]{1,0:T(8,128)(2,1)}) custom-call(f32[4,160,128]{2,1,0:T(8,128)} %bitcast.21, f32[640,128]{1,0:T(8,128)} %all_gather.9.proj_ref, bf16[128,2048]{1,0:T(8,128)(2,1)} %bitcast.19), custom_call_target="tpu_custom_call" | custom-call | tf_op jit(solution)/shard_map/grads/pallas_call | solution.py:214
  148.7 11.3 %all-to-all-start.2 = ((bf16[64,8,2560]{2,1,0:T(8,128)(2,1)}), bf16[64,8,2560]{2,1,0:T(8,128)(2,1)S(1)}, u32[]{:S(2)}, u32[]{:S(2)}) async-start(bf16[64,8,2560]{2,1,0:T(8,128)(2,1)} %bitcast.20), calls=%async_computation.2 | async-start | bytes 5242880 | tf_op jit(solution)/shard_map/all_to_all | solution.py:229
  160.0 3.7 %back.1 = bf16[128,2048]{1,0:T(8,128)(2,1)} custom-call(bf16[512,128]{1,0:T(8,128)(2,1)} %get-tuple-element.8.main_ref, bf16[512,128]{1,0:T(8,128)(2,1)} %get-tuple-element.9.tail_ref, bf16[512,2560]{1,0:T(8,128)(2,1)} %bitcast.16, f32[128,2048]{1,0:T(8,128)} %get-tuple-element.10.gx_ref), custom_call_target="tpu_custom_call" | custom-call | tf_op jit(solution)/shard_map/back/pallas_call | solution.py:230
  163.7 71.9 %all-to-all-done.2 = bf16[64,8,2560]{2,1,0:T(8,128)(2,1)S(1)} async-done(((bf16[64,8,2560]{2,1,0:T(8,128)(2,1)}), bf16[64,8,2560]{2,1,0:T(8,128)(2,1)S(1)}, u32[]{:S(2)}, u32[]{:S(2)}) %all-to-all-start.2) | async-done | bytes 2621472 | tf_op jit(solution)/shard_map/all_to_all | solution.py:229
  235.6 0.4 convert_reduce_fusion
  236.0 0.7 broadcast_in_dim.14
  (7 shorter events, 0.1 us)
Async XLA Ops:
  88.7 8.5 %copy-start.1 = (bf16[1,128,2048]{2,1,0:T(8,128)(2,1)S(1)}, bf16[1,128,2048]{2,1,0:T(8,128)(2,1)}, u32[]{:S(2)}) copy-start(bf16[1,128,2048]{2,1,0:T(8,128)(2,1)} %param.7) | copy-start | bytes 1572868
  92.6 20.2 %all-to-all-start.1 = ((f32[4,160,128]{2,1,0:T(8,128)}), f32[4,160,128]{2,1,0:T(8,128)S(1)}, u32[]{:S(2)}, u32[]{:S(2)}) async-start(f32[4,160,128]{2,1,0:T(8,128)} %bitcast.22), calls=%async_computation.1 | async-start | bytes 655360 | tf_op jit(solution)/shard_map/all_to_all | solution.py:192
  97.3 28.5 %collective-permute-start = (bf16[1,128,2048]{2,1,0:T(8,128)(2,1)S(1)}, bf16[1,128,2048]{2,1,0:T(8,128)(2,1)S(1)}, u32[]{:S(2)}, u32[]{:S(2)}) collective-permute-start(bf16[1,128,2048]{2,1,0:T(8,128)(2,1)S(1)} %copy-done.1), channel_id=1, source_target_pairs={{0,768},{256,0},{512,256},{768,512},{1,769},{257,1},{513,257},{769... | collective-permute-start | bytes 1572872 | tf_op jit(solution)/shard_map/ppermute | solution.py:175
  125.7 0.8 copy-start
  148.7 86.9 %all-to-all-start.2 = ((bf16[64,8,2560]{2,1,0:T(8,128)(2,1)}), bf16[64,8,2560]{2,1,0:T(8,128)(2,1)S(1)}, u32[]{:S(2)}, u32[]{:S(2)}) async-start(bf16[64,8,2560]{2,1,0:T(8,128)(2,1)} %bitcast.20), calls=%async_computation.2 | async-start | bytes 5242880 | tf_op jit(solution)/shard_map/all_to_all | solution.py:229

commit v2 on v1

v2 whole, which is shorter than its diff:
```python
import functools

import jax
import jax.numpy as jnp
from jax import lax
from jax.experimental import pallas as pl
from jax.experimental.pallas import tpu as pltpu
from jax.sharding import Mesh, PartitionSpec as P


HEAD_DIM = 64
STATE = 256
F32 = jnp.float32
BF16 = jnp.bfloat16
HIGHEST = lax.Precision.HIGHEST
NT = (((1,), (1,)), ((), ()))
NN = (((1,), (0,)), ((), ()))
VMEM_LIMIT = 20 * 1024 * 1024


def dot(a, b, dims=NN, precision=None):
    return lax.dot_general(a, b, dims, precision=precision, preferred_element_type=F32)


def call(kernel, outs, scratch=(), smem=(), inputs=0):
    specs = [
        pl.BlockSpec(memory_space=pltpu.SMEM if i in smem else pltpu.VMEM) for i in range(inputs)
    ]
    return pl.pallas_call(
        kernel,
        out_shape=outs,
        in_specs=specs,
        out_specs=jax.tree.map(lambda _: pl.BlockSpec(memory_space=pltpu.VMEM), outs),
        scratch_shapes=list(scratch),
        compiler_params=pltpu.CompilerParams(vmem_limit_bytes=VMEM_LIMIT),
    )


def natural(side, m, f):
    half = side // 2
    return 10 * ((2 * (f // half) + m // 2) * side + 2 * (f % half) + m % 2)


def project_kernel(w_ref, x0_ref, x1_ref, x2_ref, x3_ref, out_ref, tail_ref):
    far = w_ref.shape[0] // 8
    inner = x0_ref.shape[1]
    quarter = inner // 4
    for r, x_ref in enumerate((x0_ref, x1_ref, x2_ref, x3_ref)):
        out_ref[r, : 8 * far, :] = dot(w_ref[:, :inner], x_ref[...], NT)
        tail = None
        for q in range(4):
            tail_ref[r, q] = dot(w_ref[:, inner:], x_ref[:, q * quarter : (q + 1) * quarter], NT)
            part = tail_ref[r, q, pl.ds(q, 2 * far, 4), :]
            tail = part if tail is None else tail + part
        out_ref[r, 8 * far :, :] = tail


def as_column(row):
    n = row.shape[1]
    at = lax.broadcasted_iota(jnp.int32, (n, n), 0) == lax.broadcasted_iota(jnp.int32, (n, n), 1)
    return jnp.sum(jnp.where(at, jnp.broadcast_to(row, (n, n)), 0.0), axis=1, keepdims=True)


def prepare_kernel(rate_ref, bias_ref, out_ref):
    _, heads, t = out_ref.shape
    out_ref[0] = jnp.broadcast_to(as_column(jnp.exp(rate_ref[...])), (heads, t))
    out_ref[1] = jnp.broadcast_to(as_column(bias_ref[...]), (heads, t))


def core_kernel(
    side, tp_ref, gain_ref, group_ref, head_ref, g_ref, x_ref,
    pack_ref, gx_ref, proj_ref,
    cum_ref, cols_ref, row_ref, col_ref, scores_ref,
):
    heads = head_ref.shape[1]
    t = g_ref.shape[0]
    near, rows, _ = group_ref.shape
    far = rows // 10
    for m in range(near):
        for f in range(far):
            at = natural(side, m, f)
            proj_ref[at : at + 8, :] = group_ref[m, 8 * f : 8 * f + 8, :]
            last = 8 * far + 2 * f
            proj_ref[at + 8 : at + 10, :] = group_ref[m, last : last + 2, :]
    raw = proj_ref[pl.ds(pl.multiple_of(2 * STATE + tp_ref[0] * heads, heads), heads), :]
    z = raw + head_ref[1]
    rate = head_ref[0]
    step = jnp.maximum(z, 0.0) + jnp.log1p(jnp.exp(-jnp.abs(z)))
    first = lax.broadcasted_iota(jnp.int32, (t, t), 0)
    second = lax.broadcasted_iota(jnp.int32, (t, t), 1)
    cum = dot(-step * rate, jnp.where(first <= second, 1.0, 0.0), NN, HIGHEST)
    cum_ref[...] = cum
    cols_ref[...] = jnp.transpose(
        jnp.concatenate([cum, step, jnp.zeros((t - 2 * heads, t), F32)], axis=0)
    )
    scores = dot(jnp.transpose(proj_ref[:STATE, :]), proj_ref[STATE : 2 * STATE, :], NN, HIGHEST)
    causal = first <= second
    scores_ref[...] = jnp.where(causal, scores, 0.0)
    pack_ref[:t, :] = jnp.zeros((t, t), F32)
    left = second < HEAD_DIM

    def pair(k, carry):
        lanes = pl.ds(pl.multiple_of(k * 2 * HEAD_DIM, 2 * HEAD_DIM), 2 * HEAD_DIM)
        g = g_ref[:, lanes]
        x = x_ref[:, lanes]
        cols = cols_ref[...]
        none = jnp.zeros_like(g)
        gs = (jnp.where(left, g, none), jnp.where(left, none, g))
        moved = jnp.zeros((t, 2 * HEAD_DIM), F32)
        for a in range(2):
            h = 2 * k + a
            product = dot(x, gs[a], NT)
            step_col = cols[:, heads + a : heads + a + 1]
            decay = jnp.exp(jnp.minimum(cum_ref[pl.ds(h, 1), :] - cols[:, a : a + 1], 0.0))
            faded = product * decay
            stepped = faded * step_col
            pack_ref[:t, :] += stepped
            col_ref[...] = jnp.where(
                second == h,
                jnp.sum(faded * scores_ref[...], axis=1, keepdims=True),
                col_ref[...],
            )
            row_ref[pl.ds(h, 1), :] = jnp.sum(stepped * scores_ref[...], axis=0, keepdims=True)
            moved += dot((decay * scores_ref[...]).astype(BF16), gs[a], NN)
        step_both = jnp.where(left, cols[:, heads : heads + 1], cols[:, heads + 1 : heads + 2])
        gain = jnp.where(left, gain_ref[0, 2 * k], gain_ref[0, 2 * k + 1])
        up = g.astype(F32)
        gx_ref[:, lanes] = up + (moved * step_both + gain * up)
        cols_ref[...] = pltpu.roll(cols, t - 2, 1)
        return carry

    lax.fori_loop(0, heads // 2, pair, 0)
    pack_ref[:t, :] = jnp.where(causal, pack_ref[:t, :], 0.0)
    col = jnp.transpose(col_ref[...])[:heads, :]
    dcum = row_ref[...] - step * col
    decayed = dot(dcum, jnp.where(first >= second, 1.0, 0.0), NN, HIGHEST)
    pack_ref[t:, :] = (col - rate * decayed) * (1.0 / (1.0 + jnp.exp(-z)))


def grads_kernel(side, pack_ref, proj_ref, send_ref, grad_ref, rows_ref):
    parts, rows, t = pack_ref.shape
    heads = rows - t
    scores = pack_ref[0, :t, :]
    for p in range(1, parts):
        scores = scores + pack_ref[p, :t, :]
    grad_ref[:STATE, :] = dot(proj_ref[STATE : 2 * STATE, :], scores, NT, HIGHEST)
    grad_ref[STATE : 2 * STATE, :] = dot(proj_ref[:STATE, :], scores, NN, HIGHEST)
    for p in range(parts):
        grad_ref[2 * STATE + p * heads : 2 * STATE + (p + 1) * heads, :] = pack_ref[p, t:, :]
    near, rows, _ = send_ref.shape
    far = rows // 10
    for m in range(near):
        for f in range(far):
            at = natural(side, m, f)
            rows_ref[m, 8 * f : 8 * f + 8, :] = grad_ref[at : at + 8, :]
            last = 8 * far + 2 * f
            rows_ref[m, last : last + 2, :] = grad_ref[at + 8 : at + 10, :]
    send_ref[...] = rows_ref[...].astype(BF16)


def weight_kernel(who_ref, grad_ref, x0_ref, x1_ref, x2_ref, x3_ref, out_ref, wide_ref):
    far = grad_ref.shape[1] // 10
    inner = x0_ref.shape[1]
    quarter = inner // 4
    main = tail = 0.0
    for r, x_ref in enumerate((x0_ref, x1_ref, x2_ref, x3_ref)):
        grad = grad_ref[who_ref[r]]
        main = main + dot(grad[: 8 * far, :], x_ref[...])
        for q in range(4):
            wide_ref[r, pl.ds(q, 2 * far, 4), :] = grad[8 * far :, :].astype(F32)
        wide = wide_ref[r]
        quarter_of = lax.broadcasted_iota(jnp.int32, wide.shape, 0) % 4
        for q in range(4):
            piece = jnp.where(quarter_of == q, wide, 0.0).astype(BF16)
            tail = tail + dot(piece, x_ref[:, q * quarter : (q + 1) * quarter])
    out_ref[:, :inner] = main.astype(BF16)
    out_ref[:, inner:] = tail.astype(BF16)


def back_kernel(who_ref, grad_ref, w0_ref, w1_ref, w2_ref, w3_ref, gx_ref, out_ref, wide_ref):
    far = grad_ref.shape[1] // 10
    inner = gx_ref.shape[1]
    quarter = inner // 4
    w_refs = (w0_ref, w1_ref, w2_ref, w3_ref)
    mains, tails = [], []
    for r in range(4):
        grad = grad_ref[who_ref[r]].astype(F32)
        mains.append(jnp.transpose(grad[: 8 * far, :]).astype(BF16))
        for q in range(4):
            wide_ref[r, pl.ds(q, 2 * far, 4), :] = grad[8 * far :, :]
        tails.append(jnp.transpose(wide_ref[r]))
    quarter_of = lax.broadcasted_iota(jnp.int32, tails[0].shape, 1) % 4
    for q in range(4):
        lanes = slice(q * quarter, (q + 1) * quarter)
        back = 0.0
        for r in range(4):
            piece = jnp.where(quarter_of == q, tails[r], 0.0).astype(BF16)
            back = back + (dot(mains[r], w_refs[r][:, lanes]) + dot(piece, w_refs[r][:, inner:]))
        out_ref[:, lanes] = (gx_ref[:, lanes] + back).astype(BF16)


NEAR = ("xl", "zl")
FAR = ("xh", "zh")
ROWS = ("xh", "xl", "zh", "zl")


def from_near(value):
    count = lax.axis_size(NEAR)
    return [value] + [
        lax.ppermute(value, NEAR, [(m, m ^ r) for m in range(count)]) for r in range(1, count)
    ]


def per_device(saved_inputs, returned, proj_weight, log_rate, step_bias, skip_gain):
    x = saved_inputs[0]
    t, inner = x.shape
    heads = log_rate.shape[1]
    sections = lax.axis_size("pp")
    near = lax.axis_size(NEAR)
    far = lax.axis_size(FAR)
    side = lax.axis_size(("xh", "xl"))
    tps = lax.axis_size("tp")
    pcols = proj_weight.shape[2] * near * far
    rows = pcols // near
    wide = inner + 2 * inner // 8
    who = lax.axis_index(NEAR) ^ jnp.arange(near, dtype=jnp.int32)
    xs = from_near(x)
    arrived = lax.ppermute(returned, "pp", [(i, (i - 1) % sections) for i in range(sections)])[0]
    of_heads = call(
        prepare_kernel, jax.ShapeDtypeStruct((2, heads, t), F32), inputs=2
    )(log_rate, step_bias)

    w = proj_weight[0].T
    shard = jnp.concatenate([w[:8], w[8:].reshape(8, inner // 4)], axis=1)
    weight = lax.all_to_all(
        jnp.broadcast_to(shard[None], (far, 8, wide)), FAR, 0, 0
    ).reshape(far * 8, wide)
    weights = from_near(weight)

    partial = call(
        project_kernel,
        jax.ShapeDtypeStruct((near, rows, t), F32),
        scratch=[pltpu.VMEM((near, 4, far * 8, t), F32)],
        inputs=5,
    )(weight, *xs)
    share = lax.all_to_all(partial, "tp", 0, 0).sum(axis=0)
    own = lax.ppermute(
        share,
        NEAR + ("tp",),
        [(m * tps + k, (m ^ k) * tps + m) for m in range(near) for k in range(tps)],
    )
    proj = lax.all_gather(own, "tp", axis=0)

    pack, gx, proj = call(
        functools.partial(core_kernel, side),
        (
            jax.ShapeDtypeStruct((t + heads, t), F32),
            jax.ShapeDtypeStruct((t, inner), F32),
            jax.ShapeDtypeStruct((pcols, t), F32),
        ),
        scratch=[
            pltpu.VMEM((heads, t), F32),
            pltpu.VMEM((t, t), F32),
            pltpu.VMEM((heads, t), F32),
            pltpu.VMEM((t, t), F32),
            pltpu.VMEM((t, t), F32),
        ],
        smem=(0, 1),
        inputs=6,
    )(lax.axis_index("tp").reshape(1), skip_gain, proj, of_heads, arrived, x)

    packs = lax.all_gather(pack, "tp", axis=0)
    send = call(
        functools.partial(grads_kernel, side),
        jax.ShapeDtypeStruct((near, rows, t), BF16),
        scratch=[pltpu.VMEM((pcols, t), F32), pltpu.VMEM((near, rows, t), F32)],
        inputs=2,
    )(packs, proj)
    grads = lax.all_to_all(send, NEAR, 0, 0)
    contrib = call(
        weight_kernel,
        jax.ShapeDtypeStruct((far * 8, wide), BF16),
        scratch=[pltpu.VMEM((near, far * 8, t), F32)],
        smem=(0,),
        inputs=6,
    )(who, grads, *xs)
    pieces = lax.all_to_all(contrib.reshape(far, 8, wide), FAR, 0, 0)
    grad_inputs = call(
        back_kernel,
        jax.ShapeDtypeStruct((t, inner), BF16),
        scratch=[pltpu.VMEM((near, far * 8, t), F32)],
        smem=(0,),
        inputs=7,
    )(who, send, *weights, gx)
    total = pieces.astype(F32).sum(axis=0)
    wgrad = jnp.concatenate([total[:, :inner], total[:, inner:].reshape(2, inner)], axis=0)
    return (grad_inputs[None], wgrad.T[None])


def solution(mesh):
    side = 8
    fine = Mesh(
        mesh.devices.reshape(mesh.shape["pp"], side // 2, 2, side // 2, 2, mesh.shape["tp"]),
        ("pp", "xh", "xl", "zh", "zl", "tp"),
    )
    rows = ROWS
    placed = (
        P("pp", rows, "tp"),
        P("pp", rows, "tp"),
        P("pp", "tp", rows),
        P("pp", "tp"),
        P("pp", "tp"),
        P("pp", "tp"),
    )
    return jax.shard_map(
        per_device,
        mesh=fine,
        in_specs=placed,
        out_specs=(P("pp", rows, "tp"), P("pp", "tp", rows)),
        check_vma=False,
    )
```

time: 237 us -> 190 us (0.80)
  the two profiles are of different devices: /device:TPU:84 before, /device:TPU:65 now
where the time goes in v2:
time: 190 us; the launch traced here: 189 us
  waiting for transfers between devices  81.2 us (43%)
  starting transfers between devices  67.8 us (36%)
  blocking collectives  19.4 us (10%)
  Pallas kernels  14.6 us (8%)
  local copies, waits for them, and re-layouts  4.15 us (2%)
    ppermute x6, waiting for transfers between devices, from_near(): lax.ppermute(value, NEAR, [(m, m ^ r) for m in range(count)])  71.9 us
    all_to_all x1, starting transfers between devices, per_device(): lax.all_to_all(jnp.broadcast_to(shard[None], (far, 8, wide)), FAR, 0, 0)  20.5 us
    ppermute x6, starting transfers between devices, from_near(): lax.ppermute(value, NEAR, [(m, m ^ r) for m in range(count)])  17.4 us
    all_gather x1, blocking collectives, per_device(): proj = lax.all_gather(own, 'tp', axis=0)  13.2 us
    ppermute x1, starting transfers between devices, per_device(): lax.ppermute(share, NEAR + ('tp',), [(m * tps + k, (m ^ k) * tps + m) for...  10.1 us
    all_to_all x1, starting transfers between devices, per_device(): pieces = lax.all_to_all(contrib.reshape(far, 8, wide), FAR, 0, 0)  8.71 us
    all_gather x1, blocking collectives, per_device(): packs = lax.all_gather(pack, 'tp', axis=0)  6.19 us
    pallas_call x1, Pallas kernels, per_device(): call(functools.partial(core_kernel, side), (jax.ShapeDtypeStruct((t + hea...  5.81 us
  transfers between devices with their start and end apart: 12, of which 9 were waited for; matrix products, arithmetic and copies ran while one was open for 1% of the time, Pallas kernels for 2%

profile of v2, /device:TPU:65, one launch (start us, length us, event | category | flops | bytes accessed | tf_op | source)
XLA Modules:
  0.0 189.1 jit_solution(9578265664946112026)
XLA Ops:
  0.6 0.8 slice.17
  1.4 0.8 slice.16
  2.2 0.0 copy-start
  2.2 0.9 broadcast_in_dim.12
  3.1 20.5 %all-to-all-start = ((bf16[16,8,2560]{2,1,0:T(8,128)(2,1)}), bf16[16,8,2560]{2,1,0:T(8,128)(2,1)S(1)}, u32[]{:S(2)}, u32[]{:S(2)}) async-start(bf16[16,8,2560]{2,1,0:T(8,128)(2,1)} %broadcast_in_dim.12), calls=%async_computation | async-start | bytes 1310720 | tf_op jit(solution)/shard_map/all_to_all | solution.py:235
  23.6 0.0 copy-done
  23.6 4.0 %collective-permute-start.2 = (bf16[128,2048]{1,0:T(8,128)(2,1)S(1)}, bf16[128,2048]{1,0:T(8,128)(2,1)S(1)}, u32[]{:S(2)}, u32[]{:S(2)}) collective-permute-start(bf16[128,2048]{1,0:T(8,128)(2,1)S(1)} %bitcast.20), channel_id=1, source_target_pairs={{0,36},{4,32},{32,4},{36,0},{1,37},{5,33},{33,5},{37,1},{2,38},{6,... | collective-permute-start | bytes 1572872 | tf_op jit(solution)/shard_map/ppermute | solution.py:210
  27.6 3.1 %collective-permute-start.1 = (bf16[128,2048]{1,0:T(8,128)(2,1)S(1)}, bf16[128,2048]{1,0:T(8,128)(2,1)S(1)}, u32[]{:S(2)}, u32[]{:S(2)}) collective-permute-start(bf16[128,2048]{1,0:T(8,128)(2,1)S(1)} %bitcast.21), channel_id=1, source_target_pairs={{0,32},{4,36},{32,0},{36,4},{1,33},{5,37},{33,1},{37,5},{2,34},{6,... | collective-permute-start | bytes 1572872 | tf_op jit(solution)/shard_map/ppermute | solution.py:210
  30.7 1.9 %collective-permute-start = (bf16[128,2048]{1,0:T(8,128)(2,1)S(1)}, bf16[128,2048]{1,0:T(8,128)(2,1)S(1)}, u32[]{:S(2)}, u32[]{:S(2)}) collective-permute-start(bf16[128,2048]{1,0:T(8,128)(2,1)S(1)} %bitcast.22), channel_id=1, source_target_pairs={{0,4},{4,0},{32,36},{36,32},{1,5},{5,1},{33,37},{37,33},{2,6},{6,2... | collective-permute-start | bytes 1572872 | tf_op jit(solution)/shard_map/ppermute | solution.py:210
  32.6 22.7 %collective-permute-done.2.x3_ref = bf16[128,2048]{1,0:T(8,128)(2,1)S(1)} collective-permute-done((bf16[128,2048]{1,0:T(8,128)(2,1)S(1)}, bf16[128,2048]{1,0:T(8,128)(2,1)S(1)}, u32[]{:S(2)}, u32[]{:S(2)}) %collective-permute-start.2) | collective-permute-done | bytes 524320 | tf_op jit(solution)/shard_map/ppermute | solution.py:210
  55.3 10.2 %collective-permute-done.1.x2_ref = bf16[128,2048]{1,0:T(8,128)(2,1)S(1)} collective-permute-done((bf16[128,2048]{1,0:T(8,128)(2,1)S(1)}, bf16[128,2048]{1,0:T(8,128)(2,1)S(1)}, u32[]{:S(2)}, u32[]{:S(2)}) %collective-permute-start.1) | collective-permute-done | bytes 524320 | tf_op jit(solution)/shard_map/ppermute | solution.py:210
  65.5 1.0 collective-permute-done.x1_ref
  66.5 0.0 all-to-all-done
  66.5 2.0 %shard_map.77 = f32[4,160,128]{2,1,0:T(8,128)} custom-call(bf16[128,2560]{1,0:T(8,128)(2,1)S(1)} %bitcast.15, bf16[128,2048]{1,0:T(8,128)(2,1)S(1)} %bitcast.23, bf16[128,2048]{1,0:T(8,128)(2,1)S(1)} %collective-permute-done.x1_ref, bf16[128,2048]{1,0:T(8,128)(2,1)S(1)} %collective-permute-done.1.x2_ref, bf16[128,2048]{1,0:T(8,128)(2,1)S(1)} %collective-permute-done.2.x3_ref), custom_call_target="tpu_custom_call" | custom-call | tf_op jit(solution)/shard_map/pallas_call | solution.py:240
  68.5 0.0 copy-start.3
  68.5 0.0 copy-start.4
  68.5 4.9 %all-to-all-start.1 = ((f32[4,160,128]{2,1,0:T(8,128)}), f32[4,160,128]{2,1,0:T(8,128)}, u32[]{:S(2)}, u32[]{:S(2)}) async-start(f32[4,160,128]{2,1,0:T(8,128)} %shard_map.77), calls=%async_computation.1 | async-start | bytes 655360 | tf_op jit(solution)/shard_map/all_to_all | solution.py:246
  73.4 1.9 %collective-permute-start.4 = (bf16[1,128,2048]{2,1,0:T(8,128)(2,1)}, bf16[1,128,2048]{2,1,0:T(8,128)(2,1)S(1)}, u32[]{:S(2)}, u32[]{:S(2)}) collective-permute-start(bf16[1,128,2048]{2,1,0:T(8,128)(2,1)} %param.7), channel_id=1, source_target_pairs={{0,768},{256,0},{512,256},{768,512},{1,769},{257,1},{513,257},{769... | collective-permute-start | bytes 1572872 | tf_op jit(solution)/shard_map/ppermute | solution.py:228
  75.3 3.9 %all-to-all-done.1 = f32[4,160,128]{2,1,0:T(8,128)} async-done(((f32[4,160,128]{2,1,0:T(8,128)}), f32[4,160,128]{2,1,0:T(8,128)}, u32[]{:S(2)}, u32[]{:S(2)}) %all-to-all-start.1) | async-done | bytes 327712 | tf_op jit(solution)/shard_map/all_to_all | solution.py:246
  79.2 1.0 reduce_sum.18
  80.3 10.1 %collective-permute-start.3 = (f32[160,128]{1,0:T(8,128)S(1)}, f32[160,128]{1,0:T(8,128)S(1)}, u32[]{:S(2)}, u32[]{:S(2)}) collective-permute-start(f32[160,128]{1,0:T(8,128)S(1)} %reduce_sum.18), channel_id=1, source_target_pairs={{0,0},{1,4},{2,32},{3,36},{4,5},{5,1},{6,37},{7,33},{32,34},{33,38... | collective-permute-start | bytes 245768 | tf_op jit(solution)/shard_map/ppermute | solution.py:247
  90.3 0.0 copy-done.3
  90.4 0.0 copy-done.4
  90.4 0.1 shard_map.78.head_ref
  90.5 1.4 collective-permute-done.3
  91.8 13.2 %all-gather = f32[640,128]{1,0:T(8,128)S(1)} all-gather(f32[160,128]{1,0:T(8,128)S(1)} %collective-permute-done.3), channel_id=2, replica_groups=mesh['pp'=4,'xh'=4,'xl'=2,'zh'=4,'zl'=2,'tp'=4] {'tp'}, dimensions={0}, use_global_device_ids=true | all-gather | bytes 409600 | tf_op jit(solution)/shard_map/all_gather | solution.py:252
  105.0 0.0 collective-permute-done.4
  105.0 0.0 copy-done.5
  105.0 5.8 %shard_map.79 = (f32[160,128]{1,0:T(8,128)S(1)}, f32[128,2048]{1,0:T(8,128)S(1)}, f32[640,128]{1,0:T(8,128)S(1)}) custom-call(s32[1]{0:T(128)} %bitcast.tp_ref, f32[1,32]{1,0:T(1,128)S(1)} %copy-done.5, f32[4,160,128]{2,1,0:T(8,128)S(1)} %bitcast.27, f32[2,32,128]{2,1,0:T(8,128)S(1)} %shard_map.78.head_ref, bf16[128,2048]{1,0:T(8,128)(2,1)S(1)} %bitcast.28, ...), custom_call_target="tpu_custom_call" | custom-call | tf_op jit(solution)/shard_map/pallas_call | solution.py:254
  110.8 0.0 copy-start.1
  110.8 1.0 copy-done.1
  111.8 6.2 %all-gather.1 = f32[640,128]{1,0:T(8,128)S(1)} all-gather(f32[160,128]{1,0:T(8,128)S(1)} %get-tuple-element.5), channel_id=3, replica_groups=mesh['pp'=4,'xh'=4,'xl'=2,'zh'=4,'zl'=2,'tp'=4] {'tp'}, dimensions={0}, use_global_device_ids=true | all-gather | bytes 409600 | tf_op jit(solution)/shard_map/all_gather | solution.py:272
  118.0 1.1 shard_map.80.grad_ref
  119.1 4.3 %all-to-all-start.2 = ((bf16[4,160,128]{2,1,0:T(8,128)(2,1)}), bf16[4,160,128]{2,1,0:T(8,128)(2,1)S(1)}, u32[]{:S(2)}, u32[]{:S(2)}) async-start(bf16[4,160,128]{2,1,0:T(8,128)(2,1)} %shard_map.80.grad_ref), calls=%async_computation.2 | async-start | bytes 327680 | tf_op jit(solution)/shard_map/all_to_all | solution.py:279
  123.4 4.0 %all-to-all-done.2.grad_ref = bf16[4,160,128]{2,1,0:T(8,128)(2,1)S(1)} async-done(((bf16[4,160,128]{2,1,0:T(8,128)(2,1)}), bf16[4,160,128]{2,1,0:T(8,128)(2,1)S(1)}, u32[]{:S(2)}, u32[]{:S(2)}) %all-to-all-start.2) | async-done | bytes 163872 | tf_op jit(solution)/shard_map/all_to_all | solution.py:279
  127.4 2.6 %shard_map.82 = bf16[128,2560]{1,0:T(8,128)(2,1)} custom-call(s32[4]{0:T(128)S(1)} %iota_xor_fusion.who_ref, bf16[4,160,128]{2,1,0:T(8,128)(2,1)S(1)} %all-to-all-done.2.grad_ref, bf16[128,2048]{1,0:T(8,128)(2,1)S(1)} %bitcast.25, bf16[128,2048]{1,0:T(8,128)(2,1)S(1)} %collective-permute-done.x1_ref, bf16[128,2048]{1,0:T(8,128)(2,1)S(1)} %collective-permute-done.1.x2_ref, ...), custom_call_target="tpu_custom_call" | custom-call | tf_op jit(solution)/shard_map/pallas_call | solution.py:280
  130.0 8.7 %all-to-all-start.3 = ((bf16[16,8,2560]{2,1,0:T(8,128)(2,1)}), bf16[16,8,2560]{2,1,0:T(8,128)(2,1)S(1)}, u32[]{:S(2)}, u32[]{:S(2)}) async-start(bf16[16,8,2560]{2,1,0:T(8,128)(2,1)} %bitcast.10), calls=%async_computation.3 | async-start | bytes 1310720 | tf_op jit(solution)/shard_map/all_to_all | solution.py:287
  138.8 2.9 %collective-permute-start.7 = (bf16[128,2560]{1,0:T(8,128)(2,1)S(1)}, bf16[128,2560]{1,0:T(8,128)(2,1)S(1)}, u32[]{:S(2)}, u32[]{:S(2)}) collective-permute-start(bf16[128,2560]{1,0:T(8,128)(2,1)S(1)} %bitcast.16), channel_id=1, source_target_pairs={{0,36},{4,32},{32,4},{36,0},{1,37},{5,33},{33,5},{37,1},{2,38},{6,... | collective-permute-start | bytes 1966088 | tf_op jit(solution)/shard_map/ppermute | solution.py:210
  141.6 2.8 %collective-permute-start.6 = (bf16[128,2560]{1,0:T(8,128)(2,1)S(1)}, bf16[128,2560]{1,0:T(8,128)(2,1)S(1)}, u32[]{:S(2)}, u32[]{:S(2)}) collective-permute-start(bf16[128,2560]{1,0:T(8,128)(2,1)S(1)} %bitcast.17), channel_id=1, source_target_pairs={{0,32},{4,36},{32,0},{36,4},{1,33},{5,37},{33,1},{37,5},{2,34},{6,... | collective-permute-start | bytes 1966088 | tf_op jit(solution)/shard_map/ppermute | solution.py:210
  144.4 2.7 %collective-permute-start.5 = (bf16[128,2560]{1,0:T(8,128)(2,1)S(1)}, bf16[128,2560]{1,0:T(8,128)(2,1)S(1)}, u32[]{:S(2)}, u32[]{:S(2)}) collective-permute-start(bf16[128,2560]{1,0:T(8,128)(2,1)S(1)} %bitcast.18), channel_id=1, source_target_pairs={{0,4},{4,0},{32,36},{36,32},{1,5},{5,1},{33,37},{37,33},{2,6},{6,2... | collective-permute-start | bytes 1966088 | tf_op jit(solution)/shard_map/ppermute | solution.py:210
  147.2 22.9 %collective-permute-done.7.w3_ref = bf16[128,2560]{1,0:T(8,128)(2,1)S(1)} collective-permute-done((bf16[128,2560]{1,0:T(8,128)(2,1)S(1)}, bf16[128,2560]{1,0:T(8,128)(2,1)S(1)}, u32[]{:S(2)}, u32[]{:S(2)}) %collective-permute-start.7) | collective-permute-done | bytes 655392 | tf_op jit(solution)/shard_map/ppermute | solution.py:210
  170.1 13.5 %collective-permute-done.6.w2_ref = bf16[128,2560]{1,0:T(8,128)(2,1)S(1)} collective-permute-done((bf16[128,2560]{1,0:T(8,128)(2,1)S(1)}, bf16[128,2560]{1,0:T(8,128)(2,1)S(1)}, u32[]{:S(2)}, u32[]{:S(2)}) %collective-permute-start.6) | collective-permute-done | bytes 655392 | tf_op jit(solution)/shard_map/ppermute | solution.py:210
  183.6 1.6 collective-permute-done.5.w1_ref
  185.2 0.0 copy-done.2
  185.2 3.0 %shard_map.81 = bf16[128,2048]{1,0:T(8,128)(2,1)} custom-call(s32[4]{0:T(128)S(1)} %iota_xor_fusion.who_ref, bf16[4,160,128]{2,1,0:T(8,128)(2,1)} %shard_map.80.grad_ref, bf16[128,2560]{1,0:T(8,128)(2,1)S(1)} %bitcast.19, bf16[128,2560]{1,0:T(8,128)(2,1)S(1)} %collective-permute-done.5.w1_ref, bf16[128,2560]{1,0:T(8,128)(2,1)S(1)} %collective-permute-done.6.w2_ref, ...), custom_call_target="tpu_custom_call" | custom-call | tf_op jit(solution)/shard_map/pallas_call | solution.py:288
  188.3 0.0 all-to-all-done.3
  188.3 0.1 convert_reduce_fusion
  188.4 0.7 broadcast_in_dim.14
  (9 shorter events, 0.1 us)
Async XLA Ops:
  2.2 21.4 %copy-start = (bf16[1,128,2048]{2,1,0:T(8,128)(2,1)S(1)}, bf16[1,128,2048]{2,1,0:T(8,128)(2,1)}, u32[]{:S(2)}) copy-start(bf16[1,128,2048]{2,1,0:T(8,128)(2,1)} %param.6) | copy-start | bytes 1572868
  3.1 63.4 %all-to-all-start = ((bf16[16,8,2560]{2,1,0:T(8,128)(2,1)}), bf16[16,8,2560]{2,1,0:T(8,128)(2,1)S(1)}, u32[]{:S(2)}, u32[]{:S(2)}) async-start(bf16[16,8,2560]{2,1,0:T(8,128)(2,1)} %broadcast_in_dim.12), calls=%async_computation | async-start | bytes 1310720 | tf_op jit(solution)/shard_map/all_to_all | solution.py:235
  23.6 31.7 %collective-permute-start.2 = (bf16[128,2048]{1,0:T(8,128)(2,1)S(1)}, bf16[128,2048]{1,0:T(8,128)(2,1)S(1)}, u32[]{:S(2)}, u32[]{:S(2)}) collective-permute-start(bf16[128,2048]{1,0:T(8,128)(2,1)S(1)} %bitcast.20), channel_id=1, source_target_pairs={{0,36},{4,32},{32,4},{36,0},{1,37},{5,33},{33,5},{37,1},{2,38},{6,... | collective-permute-start | bytes 1572872 | tf_op jit(solution)/shard_map/ppermute | solution.py:210
  27.6 37.9 %collective-permute-start.1 = (bf16[128,2048]{1,0:T(8,128)(2,1)S(1)}, bf16[128,2048]{1,0:T(8,128)(2,1)S(1)}, u32[]{:S(2)}, u32[]{:S(2)}) collective-permute-start(bf16[128,2048]{1,0:T(8,128)(2,1)S(1)} %bitcast.21), channel_id=1, source_target_pairs={{0,32},{4,36},{32,0},{36,4},{1,33},{5,37},{33,1},{37,5},{2,34},{6,... | collective-permute-start | bytes 1572872 | tf_op jit(solution)/shard_map/ppermute | solution.py:210
  30.7 35.8 %collective-permute-start = (bf16[128,2048]{1,0:T(8,128)(2,1)S(1)}, bf16[128,2048]{1,0:T(8,128)(2,1)S(1)}, u32[]{:S(2)}, u32[]{:S(2)}) collective-permute-start(bf16[128,2048]{1,0:T(8,128)(2,1)S(1)} %bitcast.22), channel_id=1, source_target_pairs={{0,4},{4,0},{32,36},{36,32},{1,5},{5,1},{33,37},{37,33},{2,6},{6,2... | collective-permute-start | bytes 1572872 | tf_op jit(solution)/shard_map/ppermute | solution.py:210
  68.5 21.8 %copy-start.3 = (f32[1,32]{1,0:T(1,128)S(1)}, f32[1,32]{1,0:T(1,128)}, u32[]{:S(2)}) copy-start(f32[1,32]{1,0:T(1,128)} %rate_ref.1) | copy-start | bytes 388
  68.5 21.8 %copy-start.4 = (f32[1,32]{1,0:T(1,128)S(1)}, f32[1,32]{1,0:T(1,128)}, u32[]{:S(2)}) copy-start(f32[1,32]{1,0:T(1,128)} %bias_ref.1) | copy-start | bytes 388
  68.5 36.5 %copy-start.5 = (f32[1,32]{1,0:T(1,128)S(1)}, f32[1,32]{1,0:T(1,128)}, u32[]{:S(2)}) copy-start(f32[1,32]{1,0:T(1,128)} %gain_ref.1) | copy-start | bytes 388
  68.5 10.7 %all-to-all-start.1 = ((f32[4,160,128]{2,1,0:T(8,128)}), f32[4,160,128]{2,1,0:T(8,128)}, u32[]{:S(2)}, u32[]{:S(2)}) async-start(f32[4,160,128]{2,1,0:T(8,128)} %shard_map.77), calls=%async_computation.1 | async-start | bytes 655360 | tf_op jit(solution)/shard_map/all_to_all | solution.py:246
  73.4 31.6 %collective-permute-start.4 = (bf16[1,128,2048]{2,1,0:T(8,128)(2,1)}, bf16[1,128,2048]{2,1,0:T(8,128)(2,1)S(1)}, u32[]{:S(2)}, u32[]{:S(2)}) collective-permute-start(bf16[1,128,2048]{2,1,0:T(8,128)(2,1)} %param.7), channel_id=1, source_target_pairs={{0,768},{256,0},{512,256},{768,512},{1,769},{257,1},{513,257},{769... | collective-permute-start | bytes 1572872 | tf_op jit(solution)/shard_map/ppermute | solution.py:228
  80.3 11.6 %collective-permute-start.3 = (f32[160,128]{1,0:T(8,128)S(1)}, f32[160,128]{1,0:T(8,128)S(1)}, u32[]{:S(2)}, u32[]{:S(2)}) collective-permute-start(f32[160,128]{1,0:T(8,128)S(1)} %reduce_sum.18), channel_id=1, source_target_pairs={{0,0},{1,4},{2,32},{3,36},{4,5},{5,1},{6,37},{7,33},{32,34},{33,38... | collective-permute-start | bytes 245768 | tf_op jit(solution)/shard_map/ppermute | solution.py:247
  110.8 1.0 copy-start.1
  119.1 8.3 %all-to-all-start.2 = ((bf16[4,160,128]{2,1,0:T(8,128)(2,1)}), bf16[4,160,128]{2,1,0:T(8,128)(2,1)S(1)}, u32[]{:S(2)}, u32[]{:S(2)}) async-start(bf16[4,160,128]{2,1,0:T(8,128)(2,1)} %shard_map.80.grad_ref), calls=%async_computation.2 | async-start | bytes 327680 | tf_op jit(solution)/shard_map/all_to_all | solution.py:279
  130.0 55.2 %copy-start.2 = (f32[128,2048]{1,0:T(8,128)S(1)}, f32[128,2048]{1,0:T(8,128)}, u32[]{:S(2)}) copy-start(f32[128,2048]{1,0:T(8,128)} %copy-done.1) | copy-start | bytes 3145732
  130.0 58.2 %all-to-all-start.3 = ((bf16[16,8,2560]{2,1,0:T(8,128)(2,1)}), bf16[16,8,2560]{2,1,0:T(8,128)(2,1)S(1)}, u32[]{:S(2)}, u32[]{:S(2)}) async-start(bf16[16,8,2560]{2,1,0:T(8,128)(2,1)} %bitcast.10), calls=%async_computation.3 | async-start | bytes 1310720 | tf_op jit(solution)/shard_map/all_to_all | solution.py:287
  138.8 31.3 %collective-permute-start.7 = (bf16[128,2560]{1,0:T(8,128)(2,1)S(1)}, bf16[128,2560]{1,0:T(8,128)(2,1)S(1)}, u32[]{:S(2)}, u32[]{:S(2)}) collective-permute-start(bf16[128,2560]{1,0:T(8,128)(2,1)S(1)} %bitcast.16), channel_id=1, source_target_pairs={{0,36},{4,32},{32,4},{36,0},{1,37},{5,33},{33,5},{37,1},{2,38},{6,... | collective-permute-start | bytes 1966088 | tf_op jit(solution)/shard_map/ppermute | solution.py:210
  141.6 42.0 %collective-permute-start.6 = (bf16[128,2560]{1,0:T(8,128)(2,1)S(1)}, bf16[128,2560]{1,0:T(8,128)(2,1)S(1)}, u32[]{:S(2)}, u32[]{:S(2)}) collective-permute-start(bf16[128,2560]{1,0:T(8,128)(2,1)S(1)} %bitcast.17), channel_id=1, source_target_pairs={{0,32},{4,36},{32,0},{36,4},{1,33},{5,37},{33,1},{37,5},{2,34},{6,... | collective-permute-start | bytes 1966088 | tf_op jit(solution)/shard_map/ppermute | solution.py:210
  144.4 40.8 %collective-permute-start.5 = (bf16[128,2560]{1,0:T(8,128)(2,1)S(1)}, bf16[128,2560]{1,0:T(8,128)(2,1)S(1)}, u32[]{:S(2)}, u32[]{:S(2)}) collective-permute-start(bf16[128,2560]{1,0:T(8,128)(2,1)S(1)} %bitcast.18), channel_id=1, source_target_pairs={{0,4},{4,0},{32,36},{36,32},{1,5},{5,1},{33,37},{37,33},{2,6},{6,2... | collective-permute-start | bytes 1966088 | tf_op jit(solution)/shard_map/ppermute | solution.py:210

commit v3 on v2

--- a/solution.py
+++ b/solution.py
@@ -15,7 +15,7 @@
 HIGHEST = lax.Precision.HIGHEST
 NT = (((1,), (1,)), ((), ()))
 NN = (((1,), (0,)), ((), ()))
-VMEM_LIMIT = 20 * 1024 * 1024
+VMEM_LIMIT = 8 * 1024 * 1024
 
 
 def dot(a, b, dims=NN, precision=None):
@@ -41,17 +41,26 @@
     return 10 * ((2 * (f // half) + m // 2) * side + 2 * (f % half) + m % 2)
 
 
-def project_kernel(w_ref, x0_ref, x1_ref, x2_ref, x3_ref, out_ref, tail_ref):
+def lanes_of(parts, start, count):
+    width = parts[0].shape[1]
+    at = start % width
+    return parts[start // width][:, at : at + count]
+
+
+def project_kernel(w_ref, x0_ref, x1_ref, x2_ref, xa_ref, xb_ref, out_ref, tail_ref):
     far = w_ref.shape[0] // 8
     inner = x0_ref.shape[1]
     quarter = inner // 4
-    for r, x_ref in enumerate((x0_ref, x1_ref, x2_ref, x3_ref)):
-        out_ref[r, : 8 * far, :] = dot(w_ref[:, :inner], x_ref[...], NT)
-        tail = None
+    for r, parts in enumerate(((x0_ref,), (x1_ref,), (x2_ref,), (xa_ref, xb_ref))):
+        width = inner // len(parts)
+        main = 0.0
+        for i, part in enumerate(parts):
+            main = main + dot(w_ref[:, i * width : (i + 1) * width], part[...], NT)
+        out_ref[r, : 8 * far, :] = main
+        tail = 0.0
         for q in range(4):
-            tail_ref[r, q] = dot(w_ref[:, inner:], x_ref[:, q * quarter : (q + 1) * quarter], NT)
-            part = tail_ref[r, q, pl.ds(q, 2 * far, 4), :]
-            tail = part if tail is None else tail + part
+            tail_ref[r, q] = dot(w_ref[:, inner:], lanes_of(parts, q * quarter, quarter), NT)
+            tail = tail + tail_ref[r, q, pl.ds(q, 2 * far, 4), :]
         out_ref[r, 8 * far :, :] = tail
 
 
@@ -61,18 +70,20 @@
     return jnp.sum(jnp.where(at, jnp.broadcast_to(row, (n, n)), 0.0), axis=1, keepdims=True)
 
 
-def prepare_kernel(rate_ref, bias_ref, out_ref):
-    _, heads, t = out_ref.shape
-    out_ref[0] = jnp.broadcast_to(as_column(jnp.exp(rate_ref[...])), (heads, t))
-    out_ref[1] = jnp.broadcast_to(as_column(bias_ref[...]), (heads, t))
+def bias_kernel(bias_ref, out_ref):
+    out_ref[...] = jnp.broadcast_to(as_column(bias_ref[...]), out_ref.shape)
+
+
+def rate_kernel(rate_ref, out_ref):
+    out_ref[...] = jnp.broadcast_to(as_column(jnp.exp(rate_ref[...])), out_ref.shape)
 
 
 def core_kernel(
-    side, tp_ref, gain_ref, group_ref, head_ref, g_ref, x_ref,
+    side, tp_ref, gain_ref, group_ref, rate_ref, bias_ref, g_ref, x_ref,
     pack_ref, gx_ref, proj_ref,
     cum_ref, cols_ref, row_ref, col_ref, scores_ref,
 ):
-    heads = head_ref.shape[1]
+    heads = rate_ref.shape[0]
     t = g_ref.shape[0]
     near, rows, _ = group_ref.shape
     far = rows // 10
@@ -83,8 +94,8 @@
             last = 8 * far + 2 * f
             proj_ref[at + 8 : at + 10, :] = group_ref[m, last : last + 2, :]
     raw = proj_ref[pl.ds(pl.multiple_of(2 * STATE + tp_ref[0] * heads, heads), heads), :]
-    z = raw + head_ref[1]
-    rate = head_ref[0]
+    z = raw + bias_ref[...]
+    rate = rate_ref[...]
     step = jnp.maximum(z, 0.0) + jnp.log1p(jnp.exp(-jnp.abs(z)))
     first = lax.broadcasted_iota(jnp.int32, (t, t), 0)
     second = lax.broadcasted_iota(jnp.int32, (t, t), 1)
@@ -158,22 +169,26 @@
     send_ref[...] = rows_ref[...].astype(BF16)
 
 
-def weight_kernel(who_ref, grad_ref, x0_ref, x1_ref, x2_ref, x3_ref, out_ref, wide_ref):
+def weight_kernel(who_ref, grad_ref, x0_ref, x1_ref, x2_ref, xa_ref, xb_ref, out_ref, wide_ref):
     far = grad_ref.shape[1] // 10
     inner = x0_ref.shape[1]
     quarter = inner // 4
-    main = tail = 0.0
-    for r, x_ref in enumerate((x0_ref, x1_ref, x2_ref, x3_ref)):
+    half = inner // 2
+    mains = [0.0, 0.0]
+    tail = 0.0
+    for r, parts in enumerate(((x0_ref,), (x1_ref,), (x2_ref,), (xa_ref, xb_ref))):
         grad = grad_ref[who_ref[r]]
-        main = main + dot(grad[: 8 * far, :], x_ref[...])
+        for i in range(2):
+            mains[i] = mains[i] + dot(grad[: 8 * far, :], lanes_of(parts, i * half, half))
         for q in range(4):
             wide_ref[r, pl.ds(q, 2 * far, 4), :] = grad[8 * far :, :].astype(F32)
         wide = wide_ref[r]
         quarter_of = lax.broadcasted_iota(jnp.int32, wide.shape, 0) % 4
         for q in range(4):
             piece = jnp.where(quarter_of == q, wide, 0.0).astype(BF16)
-            tail = tail + dot(piece, x_ref[:, q * quarter : (q + 1) * quarter])
-    out_ref[:, :inner] = main.astype(BF16)
+            tail = tail + dot(piece, lanes_of(parts, q * quarter, quarter))
+    out_ref[:, :half] = mains[0].astype(BF16)
+    out_ref[:, half:inner] = mains[1].astype(BF16)
     out_ref[:, inner:] = tail.astype(BF16)
 
 
@@ -204,11 +219,8 @@
 ROWS = ("xh", "xl", "zh", "zl")
 
 
-def from_near(value):
-    count = lax.axis_size(NEAR)
-    return [value] + [
-        lax.ppermute(value, NEAR, [(m, m ^ r) for m in range(count)]) for r in range(1, count)
-    ]
+def from_near(value, r):
+    return lax.ppermute(value, NEAR, [(m, m ^ r) for m in range(lax.axis_size(NEAR))])
 
 
 def per_device(saved_inputs, returned, proj_weight, log_rate, step_bias, skip_gain):
@@ -224,24 +236,31 @@
     rows = pcols // near
     wide = inner + 2 * inner // 8
     who = lax.axis_index(NEAR) ^ jnp.arange(near, dtype=jnp.int32)
-    xs = from_near(x)
+    along_z, along_x = from_near(x, 1), from_near(x, 2)
+    xs = [
+        x,
+        along_z,
+        along_x,
+        from_near(along_z[:, : inner // 2], 2),
+        from_near(along_x[:, inner // 2 :], 1),
+    ]
     arrived = lax.ppermute(returned, "pp", [(i, (i - 1) % sections) for i in range(sections)])[0]
-    of_heads = call(
-        prepare_kernel, jax.ShapeDtypeStruct((2, heads, t), F32), inputs=2
-    )(log_rate, step_bias)
+    rates = call(rate_kernel, jax.ShapeDtypeStruct((heads, t), F32), inputs=1)(log_rate)
+    biases = call(bias_kernel, jax.ShapeDtypeStruct((heads, t), F32), inputs=1)(step_bias)
 
     w = proj_weight[0].T
     shard = jnp.concatenate([w[:8], w[8:].reshape(8, inner // 4)], axis=1)
     weight = lax.all_to_all(
         jnp.broadcast_to(shard[None], (far, 8, wide)), FAR, 0, 0
     ).reshape(far * 8, wide)
-    weights = from_near(weight)
+    weights = [weight, from_near(weight, 1), from_near(weight, 2)]
+    weights.append(from_near(weight, 3))
 
     partial = call(
         project_kernel,
         jax.ShapeDtypeStruct((near, rows, t), F32),
         scratch=[pltpu.VMEM((near, 4, far * 8, t), F32)],
-        inputs=5,
+        inputs=6,
     )(weight, *xs)
     share = lax.all_to_all(partial, "tp", 0, 0).sum(axis=0)
     own = lax.ppermute(
@@ -266,8 +285,8 @@
             pltpu.VMEM((t, t), F32),
         ],
         smem=(0, 1),
-        inputs=6,
-    )(lax.axis_index("tp").reshape(1), skip_gain, proj, of_heads, arrived, x)
+        inputs=7,
+    )(lax.axis_index("tp").reshape(1), skip_gain, proj, rates, biases, arrived, x)
 
     packs = lax.all_gather(pack, "tp", axis=0)
     send = call(
@@ -282,7 +301,7 @@
         jax.ShapeDtypeStruct((far * 8, wide), BF16),
         scratch=[pltpu.VMEM((near, far * 8, t), F32)],
         smem=(0,),
-        inputs=6,
+        inputs=7,
     )(who, grads, *xs)
     pieces = lax.all_to_all(contrib.reshape(far, 8, wide), FAR, 0, 0)
     grad_inputs = call(

time: 190 us -> 194 us (1.021)
  the two profiles are of different devices: /device:TPU:65 before, /device:TPU:1 now
where the time goes in v3:
time: 194 us; the launch traced here: 193 us
  starting transfers between devices  75 us (39%)
  waiting for transfers between devices  69.1 us (36%)
  blocking collectives  25.7 us (13%)
  Pallas kernels  15.1 us (8%)
  local copies, waits for them, and re-layouts  5.99 us (3%)
    ppermute x7, waiting for transfers between devices, from_near(): lax.ppermute(value, NEAR, [(m, m ^ r) for m in range(lax.axis_size(NEAR))])  62.1 us
    ppermute x7, starting transfers between devices, from_near(): lax.ppermute(value, NEAR, [(m, m ^ r) for m in range(lax.axis_size(NEAR))])  21.8 us
    all_to_all x1, starting transfers between devices, per_device(): lax.all_to_all(jnp.broadcast_to(shard[None], (far, 8, wide)), FAR, 0, 0)  21.3 us
    all_gather x1, blocking collectives, per_device(): proj = lax.all_gather(own, 'tp', axis=0)  19.5 us
    all_to_all x1, starting transfers between devices, per_device(): pieces = lax.all_to_all(contrib.reshape(far, 8, wide), FAR, 0, 0)  10.5 us
    ppermute x1, starting transfers between devices, per_device(): lax.ppermute(returned, 'pp', [(i, (i - 1) % sections) for i in range(sect...  6.56 us
    all_gather x1, blocking collectives, per_device(): packs = lax.all_gather(pack, 'tp', axis=0)  6.21 us
    all_to_all x1, starting transfers between devices, per_device(): share = lax.all_to_all(partial, 'tp', 0, 0).sum(axis=0)  6.18 us
  transfers between devices with their start and end apart: 13, of which 8 were waited for; matrix products, arithmetic and copies ran while one was open for 0% of the time, Pallas kernels for 2%

profile of v3, /device:TPU:1, one launch (start us, length us, event | category | flops | bytes accessed | tf_op | source)
XLA Modules:
  0.0 192.9 jit_solution(463838436506872794)
XLA Ops:
  0.6 0.8 slice.25
  1.4 0.8 slice.24
  2.2 0.9 broadcast_in_dim.12
  3.1 21.3 %all-to-all-start = ((bf16[16,8,2560]{2,1,0:T(8,128)(2,1)}), bf16[16,8,2560]{2,1,0:T(8,128)(2,1)S(1)}, u32[]{:S(2)}, u32[]{:S(2)}) async-start(bf16[16,8,2560]{2,1,0:T(8,128)(2,1)} %broadcast_in_dim.12), calls=%async_computation | async-start | bytes 1310720 | tf_op jit(solution)/shard_map/all_to_all | solution.py:253
  24.4 0.0 copy-done
  24.4 2.2 %collective-permute-start.1 = (bf16[128,2048]{1,0:T(8,128)(2,1)S(1)}, bf16[128,2048]{1,0:T(8,128)(2,1)S(1)}, u32[]{:S(2)}, u32[]{:S(2)}) collective-permute-start(bf16[128,2048]{1,0:T(8,128)(2,1)S(1)} %bitcast.20), channel_id=1, source_target_pairs={{0,32},{4,36},{32,0},{36,4},{1,33},{5,37},{33,1},{37,5},{2,34},{6,... | collective-permute-start | bytes 1572872 | tf_op jit(solution)/shard_map/ppermute | solution.py:223
  26.6 4.0 %collective-permute-start = (bf16[128,2048]{1,0:T(8,128)(2,1)S(1)}, bf16[128,2048]{1,0:T(8,128)(2,1)S(1)}, u32[]{:S(2)}, u32[]{:S(2)}) collective-permute-start(bf16[128,2048]{1,0:T(8,128)(2,1)S(1)} %bitcast.21), channel_id=1, source_target_pairs={{0,4},{4,0},{32,36},{36,32},{1,5},{5,1},{33,37},{37,33},{2,6},{6,2... | collective-permute-start | bytes 1572872 | tf_op jit(solution)/shard_map/ppermute | solution.py:223
  30.7 19.6 %collective-permute-done.1.x2_ref = bf16[128,2048]{1,0:T(8,128)(2,1)S(1)} collective-permute-done((bf16[128,2048]{1,0:T(8,128)(2,1)S(1)}, bf16[128,2048]{1,0:T(8,128)(2,1)S(1)}, u32[]{:S(2)}, u32[]{:S(2)}) %collective-permute-start.1) | collective-permute-done | bytes 524320 | tf_op jit(solution)/shard_map/ppermute | solution.py:223
  50.3 4.0 %collective-permute-start.3 = (bf16[128,1024]{1,0:T(8,128)(2,1)S(1)}, bf16[128,1024]{1,0:T(8,128)(2,1)S(1)}, u32[]{:S(2)}, u32[]{:S(2)}) collective-permute-start(bf16[128,1024]{1,0:T(8,128)(2,1)S(1)} %slice.27), channel_id=1, source_target_pairs={{0,4},{4,0},{32,36},{36,32},{1,5},{5,1},{33,37},{37,33},{2,6},{6,2... | collective-permute-start | bytes 786440 | tf_op jit(solution)/shard_map/ppermute | solution.py:223
  54.4 0.0 collective-permute-done.x1_ref
  54.4 3.1 %collective-permute-start.2 = (bf16[128,1024]{1,0:T(8,128)(2,1)S(1)}, bf16[128,1024]{1,0:T(8,128)(2,1)S(1)}, u32[]{:S(2)}, u32[]{:S(2)}) collective-permute-start(bf16[128,1024]{1,0:T(8,128)(2,1)S(1)} %slice.26), channel_id=1, source_target_pairs={{0,32},{4,36},{32,0},{36,4},{1,33},{5,37},{33,1},{37,5},{2,34},{6,... | collective-permute-start | bytes 786440 | tf_op jit(solution)/shard_map/ppermute | solution.py:223
  57.5 2.0 %collective-permute-done.3.xb_ref = bf16[128,1024]{1,0:T(8,128)(2,1)S(1)} collective-permute-done((bf16[128,1024]{1,0:T(8,128)(2,1)S(1)}, bf16[128,1024]{1,0:T(8,128)(2,1)S(1)}, u32[]{:S(2)}, u32[]{:S(2)}) %collective-permute-start.3) | collective-permute-done | bytes 262176 | tf_op jit(solution)/shard_map/ppermute | solution.py:223
  59.5 2.8 %collective-permute-done.2.xa_ref = bf16[128,1024]{1,0:T(8,128)(2,1)S(1)} collective-permute-done((bf16[128,1024]{1,0:T(8,128)(2,1)S(1)}, bf16[128,1024]{1,0:T(8,128)(2,1)S(1)}, u32[]{:S(2)}, u32[]{:S(2)}) %collective-permute-start.2) | collective-permute-done | bytes 262176 | tf_op jit(solution)/shard_map/ppermute | solution.py:223
  62.4 0.0 all-to-all-done
  62.4 2.0 %shard_map.77 = f32[4,160,128]{2,1,0:T(8,128)} custom-call(bf16[128,2560]{1,0:T(8,128)(2,1)S(1)} %bitcast.15, bf16[128,2048]{1,0:T(8,128)(2,1)S(1)} %bitcast.22, bf16[128,2048]{1,0:T(8,128)(2,1)S(1)} %collective-permute-done.x1_ref, bf16[128,2048]{1,0:T(8,128)(2,1)S(1)} %collective-permute-done.1.x2_ref, ...), custom_call_target="tpu_custom_call" | custom-call | tf_op jit(solution)/shard_map/pallas_call | solution.py:259
  64.4 0.0 copy-done.1
  64.4 6.2 %all-to-all-start.1 = ((f32[4,160,128]{2,1,0:T(8,128)}), f32[4,160,128]{2,1,0:T(8,128)S(1)}, u32[]{:S(2)}, u32[]{:S(2)}) async-start(f32[4,160,128]{2,1,0:T(8,128)} %shard_map.77), calls=%async_computation.1 | async-start | bytes 655360 | tf_op jit(solution)/shard_map/all_to_all | solution.py:265
  70.6 6.6 %collective-permute-start.5 = (bf16[1,128,2048]{2,1,0:T(8,128)(2,1)}, bf16[1,128,2048]{2,1,0:T(8,128)(2,1)S(1)}, u32[]{:S(2)}, u32[]{:S(2)}) collective-permute-start(bf16[1,128,2048]{2,1,0:T(8,128)(2,1)} %param.7), channel_id=1, source_target_pairs={{0,768},{256,0},{512,256},{768,512},{1,769},{257,1},{513,257},{769... | collective-permute-start | bytes 1572872 | tf_op jit(solution)/shard_map/ppermute | solution.py:247
  77.2 0.0 all-to-all-done.1
  77.2 4.4 %collective-permute-start.4 = (f32[160,128]{1,0:T(8,128)S(1)}, f32[160,128]{1,0:T(8,128)S(1)}, u32[]{:S(2)}, u32[]{:S(2)}) collective-permute-start(f32[160,128]{1,0:T(8,128)S(1)} %reduce_sum.18), channel_id=1, source_target_pairs={{0,0},{1,4},{2,32},{3,36},{4,5},{5,1},{6,37},{7,33},{32,34},{33,38... | collective-permute-start | bytes 245768 | tf_op jit(solution)/shard_map/ppermute | solution.py:266
  81.6 0.0 copy-done.6
  81.6 0.1 shard_map.78.rate_ref
  81.7 0.0 copy-done.7
  81.7 0.1 shard_map.79.bias_ref
  81.8 1.3 collective-permute-done.4
  83.1 19.5 %all-gather = f32[640,128]{1,0:T(8,128)S(1)} all-gather(f32[160,128]{1,0:T(8,128)S(1)} %collective-permute-done.4), channel_id=2, replica_groups=mesh['pp'=4,'xh'=4,'xl'=2,'zh'=4,'zl'=2,'tp'=4] {'tp'}, dimensions={0}, use_global_device_ids=true | all-gather | bytes 409600 | tf_op jit(solution)/shard_map/all_gather | solution.py:271
  102.6 0.0 collective-permute-done.5
  102.6 0.8 copy-done.3
  103.4 0.0 copy-done.5
  103.4 1.0 copy-done.4
  104.4 5.8 %shard_map.80 = (f32[160,128]{1,0:T(8,128)S(1)}, f32[128,2048]{1,0:T(8,128)S(1)}, f32[640,128]{1,0:T(8,128)S(1)}) custom-call(s32[1]{0:T(128)} %bitcast.tp_ref, f32[1,32]{1,0:T(1,128)S(1)} %copy-done.5, f32[4,160,128]{2,1,0:T(8,128)S(1)} %bitcast.26, f32[32,128]{1,0:T(8,128)S(1)} %shard_map.78.rate_ref, f32[32,128]{1,0:T(8,128)S(1)} %shard_map.79.bias_ref, ...), custom_call_target="tpu_custom_call" | custom-call | tf_op jit(solution)/shard_map/pallas_call | solution.py:273
  110.2 6.2 %all-gather.1 = f32[640,128]{1,0:T(8,128)S(1)} all-gather(f32[160,128]{1,0:T(8,128)S(1)} %get-tuple-element.5), channel_id=3, replica_groups=mesh['pp'=4,'xh'=4,'xl'=2,'zh'=4,'zl'=2,'tp'=4] {'tp'}, dimensions={0}, use_global_device_ids=true | all-gather | bytes 409600 | tf_op jit(solution)/shard_map/all_gather | solution.py:291
  116.4 1.1 shard_map.81.grad_ref
  117.5 4.3 %all-to-all-start.2 = ((bf16[4,160,128]{2,1,0:T(8,128)(2,1)}), bf16[4,160,128]{2,1,0:T(8,128)(2,1)}, u32[]{:S(2)}, u32[]{:S(2)}) async-start(bf16[4,160,128]{2,1,0:T(8,128)(2,1)} %shard_map.81.grad_ref), calls=%async_computation.2 | async-start | bytes 327680 | tf_op jit(solution)/shard_map/all_to_all | solution.py:298
  121.8 5.6 %all-to-all-done.2.grad_ref = bf16[4,160,128]{2,1,0:T(8,128)(2,1)} async-done(((bf16[4,160,128]{2,1,0:T(8,128)(2,1)}), bf16[4,160,128]{2,1,0:T(8,128)(2,1)}, u32[]{:S(2)}, u32[]{:S(2)}) %all-to-all-start.2) | async-done | bytes 163872 | tf_op jit(solution)/shard_map/all_to_all | solution.py:298
  127.4 0.9 copy-done.2
  128.4 3.0 %shard_map.83 = bf16[128,2560]{1,0:T(8,128)(2,1)} custom-call(s32[4]{0:T(128)S(1)} %iota_xor_fusion.who_ref, bf16[4,160,128]{2,1,0:T(8,128)(2,1)} %all-to-all-done.2.grad_ref, bf16[128,2048]{1,0:T(8,128)(2,1)S(1)} %bitcast.24, bf16[128,2048]{1,0:T(8,128)(2,1)S(1)} %collective-permute-done.x1_ref, bf16[128,2048]{1,0:T(8,128)(2,1)S(1)} %collective-permute-done.1.x2_ref, ...), custom_call_target="tpu_custom_call" | custom-call | tf_op jit(solution)/shard_map/pallas_call | solution.py:299
  131.4 10.5 %all-to-all-start.3 = ((bf16[16,8,2560]{2,1,0:T(8,128)(2,1)}), bf16[16,8,2560]{2,1,0:T(8,128)(2,1)}, u32[]{:S(2)}, u32[]{:S(2)}) async-start(bf16[16,8,2560]{2,1,0:T(8,128)(2,1)} %bitcast.10), calls=%async_computation.3 | async-start | bytes 1310720 | tf_op jit(solution)/shard_map/all_to_all | solution.py:306
  141.9 2.7 %collective-permute-start.8 = (bf16[128,2560]{1,0:T(8,128)(2,1)S(1)}, bf16[128,2560]{1,0:T(8,128)(2,1)S(1)}, u32[]{:S(2)}, u32[]{:S(2)}) collective-permute-start(bf16[128,2560]{1,0:T(8,128)(2,1)S(1)} %bitcast.16), channel_id=1, source_target_pairs={{0,36},{4,32},{32,4},{36,0},{1,37},{5,33},{33,5},{37,1},{2,38},{6,... | collective-permute-start | bytes 1966088 | tf_op jit(solution)/shard_map/ppermute | solution.py:223
  144.6 2.9 %collective-permute-start.7 = (bf16[128,2560]{1,0:T(8,128)(2,1)S(1)}, bf16[128,2560]{1,0:T(8,128)(2,1)S(1)}, u32[]{:S(2)}, u32[]{:S(2)}) collective-permute-start(bf16[128,2560]{1,0:T(8,128)(2,1)S(1)} %bitcast.17), channel_id=1, source_target_pairs={{0,32},{4,36},{32,0},{36,4},{1,33},{5,37},{33,1},{37,5},{2,34},{6,... | collective-permute-start | bytes 1966088 | tf_op jit(solution)/shard_map/ppermute | solution.py:223
  147.5 2.8 %collective-permute-start.6 = (bf16[128,2560]{1,0:T(8,128)(2,1)S(1)}, bf16[128,2560]{1,0:T(8,128)(2,1)S(1)}, u32[]{:S(2)}, u32[]{:S(2)}) collective-permute-start(bf16[128,2560]{1,0:T(8,128)(2,1)S(1)} %bitcast.18), channel_id=1, source_target_pairs={{0,4},{4,0},{32,36},{36,32},{1,5},{5,1},{33,37},{37,33},{2,6},{6,2... | collective-permute-start | bytes 1966088 | tf_op jit(solution)/shard_map/ppermute | solution.py:223
  150.3 23.6 %collective-permute-done.8.w3_ref = bf16[128,2560]{1,0:T(8,128)(2,1)S(1)} collective-permute-done((bf16[128,2560]{1,0:T(8,128)(2,1)S(1)}, bf16[128,2560]{1,0:T(8,128)(2,1)S(1)}, u32[]{:S(2)}, u32[]{:S(2)}) %collective-permute-start.8) | collective-permute-done | bytes 655392 | tf_op jit(solution)/shard_map/ppermute | solution.py:223
  173.9 13.8 %collective-permute-done.7.w2_ref = bf16[128,2560]{1,0:T(8,128)(2,1)S(1)} collective-permute-done((bf16[128,2560]{1,0:T(8,128)(2,1)S(1)}, bf16[128,2560]{1,0:T(8,128)(2,1)S(1)}, u32[]{:S(2)}, u32[]{:S(2)}) %collective-permute-start.7) | collective-permute-done | bytes 655392 | tf_op jit(solution)/shard_map/ppermute | solution.py:223
  187.7 0.3 collective-permute-done.6.w1_ref
  188.0 3.0 %shard_map.82 = bf16[128,2048]{1,0:T(8,128)(2,1)} custom-call(s32[4]{0:T(128)S(1)} %iota_xor_fusion.who_ref, bf16[4,160,128]{2,1,0:T(8,128)(2,1)} %shard_map.81.grad_ref, bf16[128,2560]{1,0:T(8,128)(2,1)S(1)} %bitcast.19, bf16[128,2560]{1,0:T(8,128)(2,1)S(1)} %collective-permute-done.6.w1_ref, bf16[128,2560]{1,0:T(8,128)(2,1)S(1)} %collective-permute-done.7.w2_ref, ...), custom_call_target="tpu_custom_call" | custom-call | tf_op jit(solution)/shard_map/pallas_call | solution.py:307
  191.0 0.0 all-to-all-done.3
  191.0 1.2 convert_reduce_fusion
  192.2 0.7 broadcast_in_dim.14
  (18 shorter events, 0.1 us)
Async XLA Ops:
  2.2 22.2 %copy-start = (bf16[1,128,2048]{2,1,0:T(8,128)(2,1)S(1)}, bf16[1,128,2048]{2,1,0:T(8,128)(2,1)}, u32[]{:S(2)}) copy-start(bf16[1,128,2048]{2,1,0:T(8,128)(2,1)} %param.6) | copy-start | bytes 1572868
  3.1 59.3 %all-to-all-start = ((bf16[16,8,2560]{2,1,0:T(8,128)(2,1)}), bf16[16,8,2560]{2,1,0:T(8,128)(2,1)S(1)}, u32[]{:S(2)}, u32[]{:S(2)}) async-start(bf16[16,8,2560]{2,1,0:T(8,128)(2,1)} %broadcast_in_dim.12), calls=%async_computation | async-start | bytes 1310720 | tf_op jit(solution)/shard_map/all_to_all | solution.py:253
  24.4 25.9 %collective-permute-start.1 = (bf16[128,2048]{1,0:T(8,128)(2,1)S(1)}, bf16[128,2048]{1,0:T(8,128)(2,1)S(1)}, u32[]{:S(2)}, u32[]{:S(2)}) collective-permute-start(bf16[128,2048]{1,0:T(8,128)(2,1)S(1)} %bitcast.20), channel_id=1, source_target_pairs={{0,32},{4,36},{32,0},{36,4},{1,33},{5,37},{33,1},{37,5},{2,34},{6,... | collective-permute-start | bytes 1572872 | tf_op jit(solution)/shard_map/ppermute | solution.py:223
  26.6 27.7 %collective-permute-start = (bf16[128,2048]{1,0:T(8,128)(2,1)S(1)}, bf16[128,2048]{1,0:T(8,128)(2,1)S(1)}, u32[]{:S(2)}, u32[]{:S(2)}) collective-permute-start(bf16[128,2048]{1,0:T(8,128)(2,1)S(1)} %bitcast.21), channel_id=1, source_target_pairs={{0,4},{4,0},{32,36},{36,32},{1,5},{5,1},{33,37},{37,33},{2,6},{6,2... | collective-permute-start | bytes 1572872 | tf_op jit(solution)/shard_map/ppermute | solution.py:223
  50.3 9.2 %collective-permute-start.3 = (bf16[128,1024]{1,0:T(8,128)(2,1)S(1)}, bf16[128,1024]{1,0:T(8,128)(2,1)S(1)}, u32[]{:S(2)}, u32[]{:S(2)}) collective-permute-start(bf16[128,1024]{1,0:T(8,128)(2,1)S(1)} %slice.27), channel_id=1, source_target_pairs={{0,4},{4,0},{32,36},{36,32},{1,5},{5,1},{33,37},{37,33},{2,6},{6,2... | collective-permute-start | bytes 786440 | tf_op jit(solution)/shard_map/ppermute | solution.py:223
  54.4 8.0 %collective-permute-start.2 = (bf16[128,1024]{1,0:T(8,128)(2,1)S(1)}, bf16[128,1024]{1,0:T(8,128)(2,1)S(1)}, u32[]{:S(2)}, u32[]{:S(2)}) collective-permute-start(bf16[128,1024]{1,0:T(8,128)(2,1)S(1)} %slice.26), channel_id=1, source_target_pairs={{0,32},{4,36},{32,0},{36,4},{1,33},{5,37},{33,1},{37,5},{2,34},{6,... | collective-permute-start | bytes 786440 | tf_op jit(solution)/shard_map/ppermute | solution.py:223
  62.4 2.0 %copy-start.1 = (bf16[128,1024]{1,0:T(8,128)(2,1)}, bf16[128,1024]{1,0:T(8,128)(2,1)S(1)}, u32[]{:S(2)}) copy-start(bf16[128,1024]{1,0:T(8,128)(2,1)S(1)} %collective-permute-done.2.xa_ref) | copy-start | bytes 786436
  64.4 17.2 %copy-start.6 = (f32[1,32]{1,0:T(1,128)S(1)}, f32[1,32]{1,0:T(1,128)}, u32[]{:S(2)}) copy-start(f32[1,32]{1,0:T(1,128)} %rate_ref.1) | copy-start | bytes 388
  64.4 17.3 %copy-start.7 = (f32[1,32]{1,0:T(1,128)S(1)}, f32[1,32]{1,0:T(1,128)}, u32[]{:S(2)}) copy-start(f32[1,32]{1,0:T(1,128)} %bias_ref.1) | copy-start | bytes 388
  64.4 39.0 %copy-start.5 = (f32[1,32]{1,0:T(1,128)S(1)}, f32[1,32]{1,0:T(1,128)}, u32[]{:S(2)}) copy-start(f32[1,32]{1,0:T(1,128)} %gain_ref.1) | copy-start | bytes 388
  64.4 12.8 %all-to-all-start.1 = ((f32[4,160,128]{2,1,0:T(8,128)}), f32[4,160,128]{2,1,0:T(8,128)S(1)}, u32[]{:S(2)}, u32[]{:S(2)}) async-start(f32[4,160,128]{2,1,0:T(8,128)} %shard_map.77), calls=%async_computation.1 | async-start | bytes 655360 | tf_op jit(solution)/shard_map/all_to_all | solution.py:265
  70.6 32.0 %collective-permute-start.5 = (bf16[1,128,2048]{2,1,0:T(8,128)(2,1)}, bf16[1,128,2048]{2,1,0:T(8,128)(2,1)S(1)}, u32[]{:S(2)}, u32[]{:S(2)}) collective-permute-start(bf16[1,128,2048]{2,1,0:T(8,128)(2,1)} %param.7), channel_id=1, source_target_pairs={{0,768},{256,0},{512,256},{768,512},{1,769},{257,1},{513,257},{769... | collective-permute-start | bytes 1572872 | tf_op jit(solution)/shard_map/ppermute | solution.py:247
  77.2 5.9 %collective-permute-start.4 = (f32[160,128]{1,0:T(8,128)S(1)}, f32[160,128]{1,0:T(8,128)S(1)}, u32[]{:S(2)}, u32[]{:S(2)}) collective-permute-start(f32[160,128]{1,0:T(8,128)S(1)} %reduce_sum.18), channel_id=1, source_target_pairs={{0,0},{1,4},{2,32},{3,36},{4,5},{5,1},{6,37},{7,33},{32,34},{33,38... | collective-permute-start | bytes 245768 | tf_op jit(solution)/shard_map/ppermute | solution.py:266
  102.6 0.8 copy-start.3
  103.4 1.0 copy-start.4
  117.5 9.9 %all-to-all-start.2 = ((bf16[4,160,128]{2,1,0:T(8,128)(2,1)}), bf16[4,160,128]{2,1,0:T(8,128)(2,1)}, u32[]{:S(2)}, u32[]{:S(2)}) async-start(bf16[4,160,128]{2,1,0:T(8,128)(2,1)} %shard_map.81.grad_ref), calls=%async_computation.2 | async-start | bytes 327680 | tf_op jit(solution)/shard_map/all_to_all | solution.py:298
  127.4 1.0 copy-start.2
  131.4 59.6 %all-to-all-start.3 = ((bf16[16,8,2560]{2,1,0:T(8,128)(2,1)}), bf16[16,8,2560]{2,1,0:T(8,128)(2,1)}, u32[]{:S(2)}, u32[]{:S(2)}) async-start(bf16[16,8,2560]{2,1,0:T(8,128)(2,1)} %bitcast.10), calls=%async_computation.3 | async-start | bytes 1310720 | tf_op jit(solution)/shard_map/all_to_all | solution.py:306
  141.9 32.0 %collective-permute-start.8 = (bf16[128,2560]{1,0:T(8,128)(2,1)S(1)}, bf16[128,2560]{1,0:T(8,128)(2,1)S(1)}, u32[]{:S(2)}, u32[]{:S(2)}) collective-permute-start(bf16[128,2560]{1,0:T(8,128)(2,1)S(1)} %bitcast.16), channel_id=1, source_target_pairs={{0,36},{4,32},{32,4},{36,0},{1,37},{5,33},{33,5},{37,1},{2,38},{6,... | collective-permute-start | bytes 1966088 | tf_op jit(solution)/shard_map/ppermute | solution.py:223
  144.6 43.1 %collective-permute-start.7 = (bf16[128,2560]{1,0:T(8,128)(2,1)S(1)}, bf16[128,2560]{1,0:T(8,128)(2,1)S(1)}, u32[]{:S(2)}, u32[]{:S(2)}) collective-permute-start(bf16[128,2560]{1,0:T(8,128)(2,1)S(1)} %bitcast.17), channel_id=1, source_target_pairs={{0,32},{4,36},{32,0},{36,4},{1,33},{5,37},{33,1},{37,5},{2,34},{6,... | collective-permute-start | bytes 1966088 | tf_op jit(solution)/shard_map/ppermute | solution.py:223
  147.5 40.5 %collective-permute-start.6 = (bf16[128,2560]{1,0:T(8,128)(2,1)S(1)}, bf16[128,2560]{1,0:T(8,128)(2,1)S(1)}, u32[]{:S(2)}, u32[]{:S(2)}) collective-permute-start(bf16[128,2560]{1,0:T(8,128)(2,1)S(1)} %bitcast.18), channel_id=1, source_target_pairs={{0,4},{4,0},{32,36},{36,32},{1,5},{5,1},{33,37},{37,33},{2,6},{6,2... | collective-permute-start | bytes 1966088 | tf_op jit(solution)/shard_map/ppermute | solution.py:223

commit v4 on v2

--- a/solution.py
+++ b/solution.py
@@ -15,7 +15,7 @@
 HIGHEST = lax.Precision.HIGHEST
 NT = (((1,), (1,)), ((), ()))
 NN = (((1,), (0,)), ((), ()))
-VMEM_LIMIT = 20 * 1024 * 1024
+VMEM_LIMIT = 8 * 1024 * 1024
 
 
 def dot(a, b, dims=NN, precision=None):
@@ -61,18 +61,20 @@
     return jnp.sum(jnp.where(at, jnp.broadcast_to(row, (n, n)), 0.0), axis=1, keepdims=True)
 
 
-def prepare_kernel(rate_ref, bias_ref, out_ref):
-    _, heads, t = out_ref.shape
-    out_ref[0] = jnp.broadcast_to(as_column(jnp.exp(rate_ref[...])), (heads, t))
-    out_ref[1] = jnp.broadcast_to(as_column(bias_ref[...]), (heads, t))
+def bias_kernel(bias_ref, out_ref):
+    out_ref[...] = jnp.broadcast_to(as_column(bias_ref[...]), out_ref.shape)
+
+
+def rate_kernel(rate_ref, out_ref):
+    out_ref[...] = jnp.broadcast_to(as_column(jnp.exp(rate_ref[...])), out_ref.shape)
 
 
 def core_kernel(
-    side, tp_ref, gain_ref, group_ref, head_ref, g_ref, x_ref,
+    side, tp_ref, gain_ref, group_ref, rate_ref, bias_ref, g_ref, x_ref,
     pack_ref, gx_ref, proj_ref,
     cum_ref, cols_ref, row_ref, col_ref, scores_ref,
 ):
-    heads = head_ref.shape[1]
+    heads = rate_ref.shape[0]
     t = g_ref.shape[0]
     near, rows, _ = group_ref.shape
     far = rows // 10
@@ -83,8 +85,8 @@
             last = 8 * far + 2 * f
             proj_ref[at + 8 : at + 10, :] = group_ref[m, last : last + 2, :]
     raw = proj_ref[pl.ds(pl.multiple_of(2 * STATE + tp_ref[0] * heads, heads), heads), :]
-    z = raw + head_ref[1]
-    rate = head_ref[0]
+    z = raw + bias_ref[...]
+    rate = rate_ref[...]
     step = jnp.maximum(z, 0.0) + jnp.log1p(jnp.exp(-jnp.abs(z)))
     first = lax.broadcasted_iota(jnp.int32, (t, t), 0)
     second = lax.broadcasted_iota(jnp.int32, (t, t), 1)
@@ -226,9 +228,8 @@
     who = lax.axis_index(NEAR) ^ jnp.arange(near, dtype=jnp.int32)
     xs = from_near(x)
     arrived = lax.ppermute(returned, "pp", [(i, (i - 1) % sections) for i in range(sections)])[0]
-    of_heads = call(
-        prepare_kernel, jax.ShapeDtypeStruct((2, heads, t), F32), inputs=2
-    )(log_rate, step_bias)
+    rates = call(rate_kernel, jax.ShapeDtypeStruct((heads, t), F32), inputs=1)(log_rate)
+    biases = call(bias_kernel, jax.ShapeDtypeStruct((heads, t), F32), inputs=1)(step_bias)
 
     w = proj_weight[0].T
     shard = jnp.concatenate([w[:8], w[8:].reshape(8, inner // 4)], axis=1)
@@ -266,8 +267,8 @@
             pltpu.VMEM((t, t), F32),
         ],
         smem=(0, 1),
-        inputs=6,
-    )(lax.axis_index("tp").reshape(1), skip_gain, proj, of_heads, arrived, x)
+        inputs=7,
+    )(lax.axis_index("tp").reshape(1), skip_gain, proj, rates, biases, arrived, x)
 
     packs = lax.all_gather(pack, "tp", axis=0)
     send = call(

time: 190 us -> 190 us (level)
  no operation moved by 1% of the time
where the time goes in v4:
time: 190 us; the launch traced here: 189 us
  waiting for transfers between devices  81.2 us (43%)
  starting transfers between devices  67.8 us (36%)
  blocking collectives  19.4 us (10%)
  Pallas kernels  14.7 us (8%)
  local copies, waits for them, and re-layouts  4.15 us (2%)
    ppermute x6, waiting for transfers between devices, from_near(): lax.ppermute(value, NEAR, [(m, m ^ r) for m in range(count)])  71.9 us
    all_to_all x1, starting transfers between devices, per_device(): lax.all_to_all(jnp.broadcast_to(shard[None], (far, 8, wide)), FAR, 0, 0)  20.5 us
    ppermute x6, starting transfers between devices, from_near(): lax.ppermute(value, NEAR, [(m, m ^ r) for m in range(count)])  17.4 us
    all_gather x1, blocking collectives, per_device(): proj = lax.all_gather(own, 'tp', axis=0)  13.2 us
    ppermute x1, starting transfers between devices, per_device(): lax.ppermute(share, NEAR + ('tp',), [(m * tps + k, (m ^ k) * tps + m) for...  10.1 us
    all_to_all x1, starting transfers between devices, per_device(): pieces = lax.all_to_all(contrib.reshape(far, 8, wide), FAR, 0, 0)  8.71 us
    all_gather x1, blocking collectives, per_device(): packs = lax.all_gather(pack, 'tp', axis=0)  6.19 us
    pallas_call x1, Pallas kernels, per_device(): call(functools.partial(core_kernel, side), (jax.ShapeDtypeStruct((t + hea...  5.81 us
  transfers between devices with their start and end apart: 12, of which 9 were waited for; matrix products, arithmetic and copies ran while one was open for 1% of the time, Pallas kernels for 2%

profile of v4, /device:TPU:65, one launch (start us, length us, event | category | flops | bytes accessed | tf_op | source)
XLA Modules:
  0.0 189.1 jit_solution(15878892505408554981)
XLA Ops:
  0.6 0.8 slice.17
  1.4 0.8 slice.16
  2.2 0.0 copy-start
  2.2 0.9 broadcast_in_dim.12
  3.1 20.5 %all-to-all-start = ((bf16[16,8,2560]{2,1,0:T(8,128)(2,1)}), bf16[16,8,2560]{2,1,0:T(8,128)(2,1)S(1)}, u32[]{:S(2)}, u32[]{:S(2)}) async-start(bf16[16,8,2560]{2,1,0:T(8,128)(2,1)} %broadcast_in_dim.12), calls=%async_computation | async-start | bytes 1310720 | tf_op jit(solution)/shard_map/all_to_all | solution.py:236
  23.6 0.0 copy-done
  23.6 4.0 %collective-permute-start.2 = (bf16[128,2048]{1,0:T(8,128)(2,1)S(1)}, bf16[128,2048]{1,0:T(8,128)(2,1)S(1)}, u32[]{:S(2)}, u32[]{:S(2)}) collective-permute-start(bf16[128,2048]{1,0:T(8,128)(2,1)S(1)} %bitcast.20), channel_id=1, source_target_pairs={{0,36},{4,32},{32,4},{36,0},{1,37},{5,33},{33,5},{37,1},{2,38},{6,... | collective-permute-start | bytes 1572872 | tf_op jit(solution)/shard_map/ppermute | solution.py:212
  27.6 3.1 %collective-permute-start.1 = (bf16[128,2048]{1,0:T(8,128)(2,1)S(1)}, bf16[128,2048]{1,0:T(8,128)(2,1)S(1)}, u32[]{:S(2)}, u32[]{:S(2)}) collective-permute-start(bf16[128,2048]{1,0:T(8,128)(2,1)S(1)} %bitcast.21), channel_id=1, source_target_pairs={{0,32},{4,36},{32,0},{36,4},{1,33},{5,37},{33,1},{37,5},{2,34},{6,... | collective-permute-start | bytes 1572872 | tf_op jit(solution)/shard_map/ppermute | solution.py:212
  30.7 1.9 %collective-permute-start = (bf16[128,2048]{1,0:T(8,128)(2,1)S(1)}, bf16[128,2048]{1,0:T(8,128)(2,1)S(1)}, u32[]{:S(2)}, u32[]{:S(2)}) collective-permute-start(bf16[128,2048]{1,0:T(8,128)(2,1)S(1)} %bitcast.22), channel_id=1, source_target_pairs={{0,4},{4,0},{32,36},{36,32},{1,5},{5,1},{33,37},{37,33},{2,6},{6,2... | collective-permute-start | bytes 1572872 | tf_op jit(solution)/shard_map/ppermute | solution.py:212
  32.6 22.7 %collective-permute-done.2.x3_ref = bf16[128,2048]{1,0:T(8,128)(2,1)S(1)} collective-permute-done((bf16[128,2048]{1,0:T(8,128)(2,1)S(1)}, bf16[128,2048]{1,0:T(8,128)(2,1)S(1)}, u32[]{:S(2)}, u32[]{:S(2)}) %collective-permute-start.2) | collective-permute-done | bytes 524320 | tf_op jit(solution)/shard_map/ppermute | solution.py:212
  55.3 10.2 %collective-permute-done.1.x2_ref = bf16[128,2048]{1,0:T(8,128)(2,1)S(1)} collective-permute-done((bf16[128,2048]{1,0:T(8,128)(2,1)S(1)}, bf16[128,2048]{1,0:T(8,128)(2,1)S(1)}, u32[]{:S(2)}, u32[]{:S(2)}) %collective-permute-start.1) | collective-permute-done | bytes 524320 | tf_op jit(solution)/shard_map/ppermute | solution.py:212
  65.5 1.0 collective-permute-done.x1_ref
  66.5 0.0 all-to-all-done
  66.5 2.0 %shard_map.77 = f32[4,160,128]{2,1,0:T(8,128)} custom-call(bf16[128,2560]{1,0:T(8,128)(2,1)S(1)} %bitcast.15, bf16[128,2048]{1,0:T(8,128)(2,1)S(1)} %bitcast.23, bf16[128,2048]{1,0:T(8,128)(2,1)S(1)} %collective-permute-done.x1_ref, bf16[128,2048]{1,0:T(8,128)(2,1)S(1)} %collective-permute-done.1.x2_ref, bf16[128,2048]{1,0:T(8,128)(2,1)S(1)} %collective-permute-done.2.x3_ref), custom_call_target="tpu_custom_call" | custom-call | tf_op jit(solution)/shard_map/pallas_call | solution.py:241
  68.5 0.0 copy-start.4
  68.5 4.9 %all-to-all-start.1 = ((f32[4,160,128]{2,1,0:T(8,128)}), f32[4,160,128]{2,1,0:T(8,128)}, u32[]{:S(2)}, u32[]{:S(2)}) async-start(f32[4,160,128]{2,1,0:T(8,128)} %shard_map.77), calls=%async_computation.1 | async-start | bytes 655360 | tf_op jit(solution)/shard_map/all_to_all | solution.py:247
  73.4 1.9 %collective-permute-start.4 = (bf16[1,128,2048]{2,1,0:T(8,128)(2,1)}, bf16[1,128,2048]{2,1,0:T(8,128)(2,1)S(1)}, u32[]{:S(2)}, u32[]{:S(2)}) collective-permute-start(bf16[1,128,2048]{2,1,0:T(8,128)(2,1)} %param.7), channel_id=1, source_target_pairs={{0,768},{256,0},{512,256},{768,512},{1,769},{257,1},{513,257},{769... | collective-permute-start | bytes 1572872 | tf_op jit(solution)/shard_map/ppermute | solution.py:230
  75.3 3.9 %all-to-all-done.1 = f32[4,160,128]{2,1,0:T(8,128)} async-done(((f32[4,160,128]{2,1,0:T(8,128)}), f32[4,160,128]{2,1,0:T(8,128)}, u32[]{:S(2)}, u32[]{:S(2)}) %all-to-all-start.1) | async-done | bytes 327712 | tf_op jit(solution)/shard_map/all_to_all | solution.py:247
  79.2 1.0 reduce_sum.18
  80.3 10.1 %collective-permute-start.3 = (f32[160,128]{1,0:T(8,128)S(1)}, f32[160,128]{1,0:T(8,128)S(1)}, u32[]{:S(2)}, u32[]{:S(2)}) collective-permute-start(f32[160,128]{1,0:T(8,128)S(1)} %reduce_sum.18), channel_id=1, source_target_pairs={{0,0},{1,4},{2,32},{3,36},{4,5},{5,1},{6,37},{7,33},{32,34},{33,38... | collective-permute-start | bytes 245768 | tf_op jit(solution)/shard_map/ppermute | solution.py:248
  90.3 0.0 copy-done.4
  90.4 0.1 shard_map.78.rate_ref
  90.4 0.0 copy-done.5
  90.4 0.1 shard_map.79.bias_ref
  90.5 1.3 collective-permute-done.3
  91.8 13.2 %all-gather = f32[640,128]{1,0:T(8,128)S(1)} all-gather(f32[160,128]{1,0:T(8,128)S(1)} %collective-permute-done.3), channel_id=2, replica_groups=mesh['pp'=4,'xh'=4,'xl'=2,'zh'=4,'zl'=2,'tp'=4] {'tp'}, dimensions={0}, use_global_device_ids=true | all-gather | bytes 409600 | tf_op jit(solution)/shard_map/all_gather | solution.py:253
  105.0 0.0 collective-permute-done.4
  105.0 0.0 copy-done.3
  105.0 5.8 %shard_map.80 = (f32[160,128]{1,0:T(8,128)S(1)}, f32[128,2048]{1,0:T(8,128)S(1)}, f32[640,128]{1,0:T(8,128)S(1)}) custom-call(s32[1]{0:T(128)} %bitcast.tp_ref, f32[1,32]{1,0:T(1,128)S(1)} %copy-done.3, f32[4,160,128]{2,1,0:T(8,128)S(1)} %bitcast.27, f32[32,128]{1,0:T(8,128)S(1)} %shard_map.78.rate_ref, f32[32,128]{1,0:T(8,128)S(1)} %shard_map.79.bias_ref, ...), custom_call_target="tpu_custom_call" | custom-call | tf_op jit(solution)/shard_map/pallas_call | solution.py:255
  110.8 0.0 copy-start.1
  110.8 1.0 copy-done.1
  111.8 6.2 %all-gather.1 = f32[640,128]{1,0:T(8,128)S(1)} all-gather(f32[160,128]{1,0:T(8,128)S(1)} %get-tuple-element.5), channel_id=3, replica_groups=mesh['pp'=4,'xh'=4,'xl'=2,'zh'=4,'zl'=2,'tp'=4] {'tp'}, dimensions={0}, use_global_device_ids=true | all-gather | bytes 409600 | tf_op jit(solution)/shard_map/all_gather | solution.py:273
  118.0 1.1 shard_map.81.grad_ref
  119.1 4.3 %all-to-all-start.2 = ((bf16[4,160,128]{2,1,0:T(8,128)(2,1)}), bf16[4,160,128]{2,1,0:T(8,128)(2,1)S(1)}, u32[]{:S(2)}, u32[]{:S(2)}) async-start(bf16[4,160,128]{2,1,0:T(8,128)(2,1)} %shard_map.81.grad_ref), calls=%async_computation.2 | async-start | bytes 327680 | tf_op jit(solution)/shard_map/all_to_all | solution.py:280
  123.4 4.0 %all-to-all-done.2.grad_ref = bf16[4,160,128]{2,1,0:T(8,128)(2,1)S(1)} async-done(((bf16[4,160,128]{2,1,0:T(8,128)(2,1)}), bf16[4,160,128]{2,1,0:T(8,128)(2,1)S(1)}, u32[]{:S(2)}, u32[]{:S(2)}) %all-to-all-start.2) | async-done | bytes 163872 | tf_op jit(solution)/shard_map/all_to_all | solution.py:280
  127.4 2.6 %shard_map.83 = bf16[128,2560]{1,0:T(8,128)(2,1)} custom-call(s32[4]{0:T(128)S(1)} %iota_xor_fusion.who_ref, bf16[4,160,128]{2,1,0:T(8,128)(2,1)S(1)} %all-to-all-done.2.grad_ref, bf16[128,2048]{1,0:T(8,128)(2,1)S(1)} %bitcast.25, bf16[128,2048]{1,0:T(8,128)(2,1)S(1)} %collective-permute-done.x1_ref, bf16[128,2048]{1,0:T(8,128)(2,1)S(1)} %collective-permute-done.1.x2_ref, ...), custom_call_target="tpu_custom_call" | custom-call | tf_op jit(solution)/shard_map/pallas_call | solution.py:281
  130.0 8.7 %all-to-all-start.3 = ((bf16[16,8,2560]{2,1,0:T(8,128)(2,1)}), bf16[16,8,2560]{2,1,0:T(8,128)(2,1)S(1)}, u32[]{:S(2)}, u32[]{:S(2)}) async-start(bf16[16,8,2560]{2,1,0:T(8,128)(2,1)} %bitcast.10), calls=%async_computation.3 | async-start | bytes 1310720 | tf_op jit(solution)/shard_map/all_to_all | solution.py:288
  138.8 2.9 %collective-permute-start.7 = (bf16[128,2560]{1,0:T(8,128)(2,1)S(1)}, bf16[128,2560]{1,0:T(8,128)(2,1)S(1)}, u32[]{:S(2)}, u32[]{:S(2)}) collective-permute-start(bf16[128,2560]{1,0:T(8,128)(2,1)S(1)} %bitcast.16), channel_id=1, source_target_pairs={{0,36},{4,32},{32,4},{36,0},{1,37},{5,33},{33,5},{37,1},{2,38},{6,... | collective-permute-start | bytes 1966088 | tf_op jit(solution)/shard_map/ppermute | solution.py:212
  141.6 2.8 %collective-permute-start.6 = (bf16[128,2560]{1,0:T(8,128)(2,1)S(1)}, bf16[128,2560]{1,0:T(8,128)(2,1)S(1)}, u32[]{:S(2)}, u32[]{:S(2)}) collective-permute-start(bf16[128,2560]{1,0:T(8,128)(2,1)S(1)} %bitcast.17), channel_id=1, source_target_pairs={{0,32},{4,36},{32,0},{36,4},{1,33},{5,37},{33,1},{37,5},{2,34},{6,... | collective-permute-start | bytes 1966088 | tf_op jit(solution)/shard_map/ppermute | solution.py:212
  144.4 2.7 %collective-permute-start.5 = (bf16[128,2560]{1,0:T(8,128)(2,1)S(1)}, bf16[128,2560]{1,0:T(8,128)(2,1)S(1)}, u32[]{:S(2)}, u32[]{:S(2)}) collective-permute-start(bf16[128,2560]{1,0:T(8,128)(2,1)S(1)} %bitcast.18), channel_id=1, source_target_pairs={{0,4},{4,0},{32,36},{36,32},{1,5},{5,1},{33,37},{37,33},{2,6},{6,2... | collective-permute-start | bytes 1966088 | tf_op jit(solution)/shard_map/ppermute | solution.py:212
  147.2 22.9 %collective-permute-done.7.w3_ref = bf16[128,2560]{1,0:T(8,128)(2,1)S(1)} collective-permute-done((bf16[128,2560]{1,0:T(8,128)(2,1)S(1)}, bf16[128,2560]{1,0:T(8,128)(2,1)S(1)}, u32[]{:S(2)}, u32[]{:S(2)}) %collective-permute-start.7) | collective-permute-done | bytes 655392 | tf_op jit(solution)/shard_map/ppermute | solution.py:212
  170.1 13.5 %collective-permute-done.6.w2_ref = bf16[128,2560]{1,0:T(8,128)(2,1)S(1)} collective-permute-done((bf16[128,2560]{1,0:T(8,128)(2,1)S(1)}, bf16[128,2560]{1,0:T(8,128)(2,1)S(1)}, u32[]{:S(2)}, u32[]{:S(2)}) %collective-permute-start.6) | collective-permute-done | bytes 655392 | tf_op jit(solution)/shard_map/ppermute | solution.py:212
  183.6 1.6 collective-permute-done.5.w1_ref
  185.2 0.0 copy-done.2
  185.2 3.0 %shard_map.82 = bf16[128,2048]{1,0:T(8,128)(2,1)} custom-call(s32[4]{0:T(128)S(1)} %iota_xor_fusion.who_ref, bf16[4,160,128]{2,1,0:T(8,128)(2,1)} %shard_map.81.grad_ref, bf16[128,2560]{1,0:T(8,128)(2,1)S(1)} %bitcast.19, bf16[128,2560]{1,0:T(8,128)(2,1)S(1)} %collective-permute-done.5.w1_ref, bf16[128,2560]{1,0:T(8,128)(2,1)S(1)} %collective-permute-done.6.w2_ref, ...), custom_call_target="tpu_custom_call" | custom-call | tf_op jit(solution)/shard_map/pallas_call | solution.py:289
  188.3 0.0 all-to-all-done.3
  188.3 0.1 convert_reduce_fusion
  188.4 0.7 broadcast_in_dim.14
  (10 shorter events, 0.1 us)
Async XLA Ops:
  2.2 21.4 %copy-start = (bf16[1,128,2048]{2,1,0:T(8,128)(2,1)S(1)}, bf16[1,128,2048]{2,1,0:T(8,128)(2,1)}, u32[]{:S(2)}) copy-start(bf16[1,128,2048]{2,1,0:T(8,128)(2,1)} %param.6) | copy-start | bytes 1572868
  3.1 63.4 %all-to-all-start = ((bf16[16,8,2560]{2,1,0:T(8,128)(2,1)}), bf16[16,8,2560]{2,1,0:T(8,128)(2,1)S(1)}, u32[]{:S(2)}, u32[]{:S(2)}) async-start(bf16[16,8,2560]{2,1,0:T(8,128)(2,1)} %broadcast_in_dim.12), calls=%async_computation | async-start | bytes 1310720 | tf_op jit(solution)/shard_map/all_to_all | solution.py:236
  23.6 31.7 %collective-permute-start.2 = (bf16[128,2048]{1,0:T(8,128)(2,1)S(1)}, bf16[128,2048]{1,0:T(8,128)(2,1)S(1)}, u32[]{:S(2)}, u32[]{:S(2)}) collective-permute-start(bf16[128,2048]{1,0:T(8,128)(2,1)S(1)} %bitcast.20), channel_id=1, source_target_pairs={{0,36},{4,32},{32,4},{36,0},{1,37},{5,33},{33,5},{37,1},{2,38},{6,... | collective-permute-start | bytes 1572872 | tf_op jit(solution)/shard_map/ppermute | solution.py:212
  27.6 37.9 %collective-permute-start.1 = (bf16[128,2048]{1,0:T(8,128)(2,1)S(1)}, bf16[128,2048]{1,0:T(8,128)(2,1)S(1)}, u32[]{:S(2)}, u32[]{:S(2)}) collective-permute-start(bf16[128,2048]{1,0:T(8,128)(2,1)S(1)} %bitcast.21), channel_id=1, source_target_pairs={{0,32},{4,36},{32,0},{36,4},{1,33},{5,37},{33,1},{37,5},{2,34},{6,... | collective-permute-start | bytes 1572872 | tf_op jit(solution)/shard_map/ppermute | solution.py:212
  30.7 35.8 %collective-permute-start = (bf16[128,2048]{1,0:T(8,128)(2,1)S(1)}, bf16[128,2048]{1,0:T(8,128)(2,1)S(1)}, u32[]{:S(2)}, u32[]{:S(2)}) collective-permute-start(bf16[128,2048]{1,0:T(8,128)(2,1)S(1)} %bitcast.22), channel_id=1, source_target_pairs={{0,4},{4,0},{32,36},{36,32},{1,5},{5,1},{33,37},{37,33},{2,6},{6,2... | collective-permute-start | bytes 1572872 | tf_op jit(solution)/shard_map/ppermute | solution.py:212
  68.5 21.8 %copy-start.4 = (f32[1,32]{1,0:T(1,128)S(1)}, f32[1,32]{1,0:T(1,128)}, u32[]{:S(2)}) copy-start(f32[1,32]{1,0:T(1,128)} %rate_ref.1) | copy-start | bytes 388
  68.5 21.9 %copy-start.5 = (f32[1,32]{1,0:T(1,128)S(1)}, f32[1,32]{1,0:T(1,128)}, u32[]{:S(2)}) copy-start(f32[1,32]{1,0:T(1,128)} %bias_ref.1) | copy-start | bytes 388
  68.5 36.5 %copy-start.3 = (f32[1,32]{1,0:T(1,128)S(1)}, f32[1,32]{1,0:T(1,128)}, u32[]{:S(2)}) copy-start(f32[1,32]{1,0:T(1,128)} %gain_ref.1) | copy-start | bytes 388
  68.5 10.7 %all-to-all-start.1 = ((f32[4,160,128]{2,1,0:T(8,128)}), f32[4,160,128]{2,1,0:T(8,128)}, u32[]{:S(2)}, u32[]{:S(2)}) async-start(f32[4,160,128]{2,1,0:T(8,128)} %shard_map.77), calls=%async_computation.1 | async-start | bytes 655360 | tf_op jit(solution)/shard_map/all_to_all | solution.py:247
  73.4 31.6 %collective-permute-start.4 = (bf16[1,128,2048]{2,1,0:T(8,128)(2,1)}, bf16[1,128,2048]{2,1,0:T(8,128)(2,1)S(1)}, u32[]{:S(2)}, u32[]{:S(2)}) collective-permute-start(bf16[1,128,2048]{2,1,0:T(8,128)(2,1)} %param.7), channel_id=1, source_target_pairs={{0,768},{256,0},{512,256},{768,512},{1,769},{257,1},{513,257},{769... | collective-permute-start | bytes 1572872 | tf_op jit(solution)/shard_map/ppermute | solution.py:230
  80.3 11.6 %collective-permute-start.3 = (f32[160,128]{1,0:T(8,128)S(1)}, f32[160,128]{1,0:T(8,128)S(1)}, u32[]{:S(2)}, u32[]{:S(2)}) collective-permute-start(f32[160,128]{1,0:T(8,128)S(1)} %reduce_sum.18), channel_id=1, source_target_pairs={{0,0},{1,4},{2,32},{3,36},{4,5},{5,1},{6,37},{7,33},{32,34},{33,38... | collective-permute-start | bytes 245768 | tf_op jit(solution)/shard_map/ppermute | solution.py:248
  110.8 1.0 copy-start.1
  119.1 8.3 %all-to-all-start.2 = ((bf16[4,160,128]{2,1,0:T(8,128)(2,1)}), bf16[4,160,128]{2,1,0:T(8,128)(2,1)S(1)}, u32[]{:S(2)}, u32[]{:S(2)}) async-start(bf16[4,160,128]{2,1,0:T(8,128)(2,1)} %shard_map.81.grad_ref), calls=%async_computation.2 | async-start | bytes 327680 | tf_op jit(solution)/shard_map/all_to_all | solution.py:280
  130.0 55.2 %copy-start.2 = (f32[128,2048]{1,0:T(8,128)S(1)}, f32[128,2048]{1,0:T(8,128)}, u32[]{:S(2)}) copy-start(f32[128,2048]{1,0:T(8,128)} %copy-done.1) | copy-start | bytes 3145732
  130.0 58.2 %all-to-all-start.3 = ((bf16[16,8,2560]{2,1,0:T(8,128)(2,1)}), bf16[16,8,2560]{2,1,0:T(8,128)(2,1)S(1)}, u32[]{:S(2)}, u32[]{:S(2)}) async-start(bf16[16,8,2560]{2,1,0:T(8,128)(2,1)} %bitcast.10), calls=%async_computation.3 | async-start | bytes 1310720 | tf_op jit(solution)/shard_map/all_to_all | solution.py:288
  138.8 31.3 %collective-permute-start.7 = (bf16[128,2560]{1,0:T(8,128)(2,1)S(1)}, bf16[128,2560]{1,0:T(8,128)(2,1)S(1)}, u32[]{:S(2)}, u32[]{:S(2)}) collective-permute-start(bf16[128,2560]{1,0:T(8,128)(2,1)S(1)} %bitcast.16), channel_id=1, source_target_pairs={{0,36},{4,32},{32,4},{36,0},{1,37},{5,33},{33,5},{37,1},{2,38},{6,... | collective-permute-start | bytes 1966088 | tf_op jit(solution)/shard_map/ppermute | solution.py:212
  141.6 42.0 %collective-permute-start.6 = (bf16[128,2560]{1,0:T(8,128)(2,1)S(1)}, bf16[128,2560]{1,0:T(8,128)(2,1)S(1)}, u32[]{:S(2)}, u32[]{:S(2)}) collective-permute-start(bf16[128,2560]{1,0:T(8,128)(2,1)S(1)} %bitcast.17), channel_id=1, source_target_pairs={{0,32},{4,36},{32,0},{36,4},{1,33},{5,37},{33,1},{37,5},{2,34},{6,... | collective-permute-start | bytes 1966088 | tf_op jit(solution)/shard_map/ppermute | solution.py:212
  144.4 40.8 %collective-permute-start.5 = (bf16[128,2560]{1,0:T(8,128)(2,1)S(1)}, bf16[128,2560]{1,0:T(8,128)(2,1)S(1)}, u32[]{:S(2)}, u32[]{:S(2)}) collective-permute-start(bf16[128,2560]{1,0:T(8,128)(2,1)S(1)} %bitcast.18), channel_id=1, source_target_pairs={{0,4},{4,0},{32,36},{36,32},{1,5},{5,1},{33,37},{37,33},{2,6},{6,2... | collective-permute-start | bytes 1966088 | tf_op jit(solution)/shard_map/ppermute | solution.py:212

commit v5 on v4

--- a/solution.py
+++ b/solution.py
@@ -206,11 +206,8 @@
 ROWS = ("xh", "xl", "zh", "zl")
 
 
-def from_near(value):
-    count = lax.axis_size(NEAR)
-    return [value] + [
-        lax.ppermute(value, NEAR, [(m, m ^ r) for m in range(count)]) for r in range(1, count)
-    ]
+def from_near(value, r):
+    return lax.ppermute(value, NEAR, [(m, m ^ r) for m in range(lax.axis_size(NEAR))])
 
 
 def per_device(saved_inputs, returned, proj_weight, log_rate, step_bias, skip_gain):
@@ -226,7 +223,7 @@
     rows = pcols // near
     wide = inner + 2 * inner // 8
     who = lax.axis_index(NEAR) ^ jnp.arange(near, dtype=jnp.int32)
-    xs = from_near(x)
+    xs = [x] + [from_near(x, r) for r in range(1, near)]
     arrived = lax.ppermute(returned, "pp", [(i, (i - 1) % sections) for i in range(sections)])[0]
     rates = call(rate_kernel, jax.ShapeDtypeStruct((heads, t), F32), inputs=1)(log_rate)
     biases = call(bias_kernel, jax.ShapeDtypeStruct((heads, t), F32), inputs=1)(step_bias)
@@ -236,7 +233,8 @@
     weight = lax.all_to_all(
         jnp.broadcast_to(shard[None], (far, 8, wide)), FAR, 0, 0
     ).reshape(far * 8, wide)
-    weights = from_near(weight)
+    diagonal = from_near(weight, 3)
+    weights = [weight, from_near(weight, 1), from_near(weight, 2), diagonal]
 
     partial = call(
         project_kernel,

time: 190 us -> 190 us (level)
  no operation moved by 1% of the time
where the time goes in v5:
time: 190 us; the launch traced here: 189 us
  waiting for transfers between devices  81.2 us (43%)
  starting transfers between devices  67.8 us (36%)
  blocking collectives  19.4 us (10%)
  Pallas kernels  14.7 us (8%)
  local copies, waits for them, and re-layouts  4.15 us (2%)
    ppermute x6, waiting for transfers between devices, from_near(): lax.ppermute(value, NEAR, [(m, m ^ r) for m in range(lax.axis_size(NEAR))])  71.9 us
    all_to_all x1, starting transfers between devices, per_device(): lax.all_to_all(jnp.broadcast_to(shard[None], (far, 8, wide)), FAR, 0, 0)  20.5 us
    ppermute x6, starting transfers between devices, from_near(): lax.ppermute(value, NEAR, [(m, m ^ r) for m in range(lax.axis_size(NEAR))])  17.4 us
    all_gather x1, blocking collectives, per_device(): proj = lax.all_gather(own, 'tp', axis=0)  13.2 us
    ppermute x1, starting transfers between devices, per_device(): lax.ppermute(share, NEAR + ('tp',), [(m * tps + k, (m ^ k) * tps + m) for...  10.1 us
    all_to_all x1, starting transfers between devices, per_device(): pieces = lax.all_to_all(contrib.reshape(far, 8, wide), FAR, 0, 0)  8.71 us
    all_gather x1, blocking collectives, per_device(): packs = lax.all_gather(pack, 'tp', axis=0)  6.19 us
    pallas_call x1, Pallas kernels, per_device(): call(functools.partial(core_kernel, side), (jax.ShapeDtypeStruct((t + hea...  5.81 us
  transfers between devices with their start and end apart: 12, of which 9 were waited for; matrix products, arithmetic and copies ran while one was open for 1% of the time, Pallas kernels for 2%

profile of v5, /device:TPU:65, one launch (start us, length us, event | category | flops | bytes accessed | tf_op | source)
XLA Modules:
  0.0 189.1 jit_solution(15878892505408554981)
XLA Ops:
  0.6 0.8 slice.17
  1.4 0.8 slice.16
  2.2 0.0 copy-start
  2.2 0.9 broadcast_in_dim.12
  3.1 20.5 %all-to-all-start = ((bf16[16,8,2560]{2,1,0:T(8,128)(2,1)}), bf16[16,8,2560]{2,1,0:T(8,128)(2,1)S(1)}, u32[]{:S(2)}, u32[]{:S(2)}) async-start(bf16[16,8,2560]{2,1,0:T(8,128)(2,1)} %broadcast_in_dim.12), calls=%async_computation | async-start | bytes 1310720 | tf_op jit(solution)/shard_map/all_to_all | solution.py:233
  23.6 0.0 copy-done
  23.6 4.0 %collective-permute-start.2 = (bf16[128,2048]{1,0:T(8,128)(2,1)S(1)}, bf16[128,2048]{1,0:T(8,128)(2,1)S(1)}, u32[]{:S(2)}, u32[]{:S(2)}) collective-permute-start(bf16[128,2048]{1,0:T(8,128)(2,1)S(1)} %bitcast.20), channel_id=1, source_target_pairs={{0,36},{4,32},{32,4},{36,0},{1,37},{5,33},{33,5},{37,1},{2,38},{6,... | collective-permute-start | bytes 1572872 | tf_op jit(solution)/shard_map/ppermute | solution.py:210
  27.6 3.1 %collective-permute-start.1 = (bf16[128,2048]{1,0:T(8,128)(2,1)S(1)}, bf16[128,2048]{1,0:T(8,128)(2,1)S(1)}, u32[]{:S(2)}, u32[]{:S(2)}) collective-permute-start(bf16[128,2048]{1,0:T(8,128)(2,1)S(1)} %bitcast.21), channel_id=1, source_target_pairs={{0,32},{4,36},{32,0},{36,4},{1,33},{5,37},{33,1},{37,5},{2,34},{6,... | collective-permute-start | bytes 1572872 | tf_op jit(solution)/shard_map/ppermute | solution.py:210
  30.7 1.9 %collective-permute-start = (bf16[128,2048]{1,0:T(8,128)(2,1)S(1)}, bf16[128,2048]{1,0:T(8,128)(2,1)S(1)}, u32[]{:S(2)}, u32[]{:S(2)}) collective-permute-start(bf16[128,2048]{1,0:T(8,128)(2,1)S(1)} %bitcast.22), channel_id=1, source_target_pairs={{0,4},{4,0},{32,36},{36,32},{1,5},{5,1},{33,37},{37,33},{2,6},{6,2... | collective-permute-start | bytes 1572872 | tf_op jit(solution)/shard_map/ppermute | solution.py:210
  32.6 22.7 %collective-permute-done.2.x3_ref = bf16[128,2048]{1,0:T(8,128)(2,1)S(1)} collective-permute-done((bf16[128,2048]{1,0:T(8,128)(2,1)S(1)}, bf16[128,2048]{1,0:T(8,128)(2,1)S(1)}, u32[]{:S(2)}, u32[]{:S(2)}) %collective-permute-start.2) | collective-permute-done | bytes 524320 | tf_op jit(solution)/shard_map/ppermute | solution.py:210
  55.3 10.2 %collective-permute-done.1.x2_ref = bf16[128,2048]{1,0:T(8,128)(2,1)S(1)} collective-permute-done((bf16[128,2048]{1,0:T(8,128)(2,1)S(1)}, bf16[128,2048]{1,0:T(8,128)(2,1)S(1)}, u32[]{:S(2)}, u32[]{:S(2)}) %collective-permute-start.1) | collective-permute-done | bytes 524320 | tf_op jit(solution)/shard_map/ppermute | solution.py:210
  65.5 1.0 collective-permute-done.x1_ref
  66.5 0.0 all-to-all-done
  66.5 2.0 %shard_map.77 = f32[4,160,128]{2,1,0:T(8,128)} custom-call(bf16[128,2560]{1,0:T(8,128)(2,1)S(1)} %bitcast.15, bf16[128,2048]{1,0:T(8,128)(2,1)S(1)} %bitcast.23, bf16[128,2048]{1,0:T(8,128)(2,1)S(1)} %collective-permute-done.x1_ref, bf16[128,2048]{1,0:T(8,128)(2,1)S(1)} %collective-permute-done.1.x2_ref, bf16[128,2048]{1,0:T(8,128)(2,1)S(1)} %collective-permute-done.2.x3_ref), custom_call_target="tpu_custom_call" | custom-call | tf_op jit(solution)/shard_map/pallas_call | solution.py:239
  68.5 0.0 copy-start.4
  68.5 4.9 %all-to-all-start.1 = ((f32[4,160,128]{2,1,0:T(8,128)}), f32[4,160,128]{2,1,0:T(8,128)}, u32[]{:S(2)}, u32[]{:S(2)}) async-start(f32[4,160,128]{2,1,0:T(8,128)} %shard_map.77), calls=%async_computation.1 | async-start | bytes 655360 | tf_op jit(solution)/shard_map/all_to_all | solution.py:245
  73.4 1.9 %collective-permute-start.4 = (bf16[1,128,2048]{2,1,0:T(8,128)(2,1)}, bf16[1,128,2048]{2,1,0:T(8,128)(2,1)S(1)}, u32[]{:S(2)}, u32[]{:S(2)}) collective-permute-start(bf16[1,128,2048]{2,1,0:T(8,128)(2,1)} %param.7), channel_id=1, source_target_pairs={{0,768},{256,0},{512,256},{768,512},{1,769},{257,1},{513,257},{769... | collective-permute-start | bytes 1572872 | tf_op jit(solution)/shard_map/ppermute | solution.py:227
  75.3 3.9 %all-to-all-done.1 = f32[4,160,128]{2,1,0:T(8,128)} async-done(((f32[4,160,128]{2,1,0:T(8,128)}), f32[4,160,128]{2,1,0:T(8,128)}, u32[]{:S(2)}, u32[]{:S(2)}) %all-to-all-start.1) | async-done | bytes 327712 | tf_op jit(solution)/shard_map/all_to_all | solution.py:245
  79.2 1.0 reduce_sum.18
  80.3 10.1 %collective-permute-start.3 = (f32[160,128]{1,0:T(8,128)S(1)}, f32[160,128]{1,0:T(8,128)S(1)}, u32[]{:S(2)}, u32[]{:S(2)}) collective-permute-start(f32[160,128]{1,0:T(8,128)S(1)} %reduce_sum.18), channel_id=1, source_target_pairs={{0,0},{1,4},{2,32},{3,36},{4,5},{5,1},{6,37},{7,33},{32,34},{33,38... | collective-permute-start | bytes 245768 | tf_op jit(solution)/shard_map/ppermute | solution.py:246
  90.3 0.0 copy-done.4
  90.4 0.1 shard_map.78.rate_ref
  90.4 0.0 copy-done.5
  90.4 0.1 shard_map.79.bias_ref
  90.5 1.3 collective-permute-done.3
  91.8 13.2 %all-gather = f32[640,128]{1,0:T(8,128)S(1)} all-gather(f32[160,128]{1,0:T(8,128)S(1)} %collective-permute-done.3), channel_id=2, replica_groups=mesh['pp'=4,'xh'=4,'xl'=2,'zh'=4,'zl'=2,'tp'=4] {'tp'}, dimensions={0}, use_global_device_ids=true | all-gather | bytes 409600 | tf_op jit(solution)/shard_map/all_gather | solution.py:251
  105.0 0.0 collective-permute-done.4
  105.0 0.0 copy-done.3
  105.0 5.8 %shard_map.80 = (f32[160,128]{1,0:T(8,128)S(1)}, f32[128,2048]{1,0:T(8,128)S(1)}, f32[640,128]{1,0:T(8,128)S(1)}) custom-call(s32[1]{0:T(128)} %bitcast.tp_ref, f32[1,32]{1,0:T(1,128)S(1)} %copy-done.3, f32[4,160,128]{2,1,0:T(8,128)S(1)} %bitcast.27, f32[32,128]{1,0:T(8,128)S(1)} %shard_map.78.rate_ref, f32[32,128]{1,0:T(8,128)S(1)} %shard_map.79.bias_ref, ...), custom_call_target="tpu_custom_call" | custom-call | tf_op jit(solution)/shard_map/pallas_call | solution.py:253
  110.8 0.0 copy-start.1
  110.8 1.0 copy-done.1
  111.8 6.2 %all-gather.1 = f32[640,128]{1,0:T(8,128)S(1)} all-gather(f32[160,128]{1,0:T(8,128)S(1)} %get-tuple-element.5), channel_id=3, replica_groups=mesh['pp'=4,'xh'=4,'xl'=2,'zh'=4,'zl'=2,'tp'=4] {'tp'}, dimensions={0}, use_global_device_ids=true | all-gather | bytes 409600 | tf_op jit(solution)/shard_map/all_gather | solution.py:271
  118.0 1.1 shard_map.81.grad_ref
  119.1 4.3 %all-to-all-start.2 = ((bf16[4,160,128]{2,1,0:T(8,128)(2,1)}), bf16[4,160,128]{2,1,0:T(8,128)(2,1)S(1)}, u32[]{:S(2)}, u32[]{:S(2)}) async-start(bf16[4,160,128]{2,1,0:T(8,128)(2,1)} %shard_map.81.grad_ref), calls=%async_computation.2 | async-start | bytes 327680 | tf_op jit(solution)/shard_map/all_to_all | solution.py:278
  123.4 4.0 %all-to-all-done.2.grad_ref = bf16[4,160,128]{2,1,0:T(8,128)(2,1)S(1)} async-done(((bf16[4,160,128]{2,1,0:T(8,128)(2,1)}), bf16[4,160,128]{2,1,0:T(8,128)(2,1)S(1)}, u32[]{:S(2)}, u32[]{:S(2)}) %all-to-all-start.2) | async-done | bytes 163872 | tf_op jit(solution)/shard_map/all_to_all | solution.py:278
  127.4 2.6 %shard_map.83 = bf16[128,2560]{1,0:T(8,128)(2,1)} custom-call(s32[4]{0:T(128)S(1)} %iota_xor_fusion.who_ref, bf16[4,160,128]{2,1,0:T(8,128)(2,1)S(1)} %all-to-all-done.2.grad_ref, bf16[128,2048]{1,0:T(8,128)(2,1)S(1)} %bitcast.25, bf16[128,2048]{1,0:T(8,128)(2,1)S(1)} %collective-permute-done.x1_ref, bf16[128,2048]{1,0:T(8,128)(2,1)S(1)} %collective-permute-done.1.x2_ref, ...), custom_call_target="tpu_custom_call" | custom-call | tf_op jit(solution)/shard_map/pallas_call | solution.py:279
  130.0 8.7 %all-to-all-start.3 = ((bf16[16,8,2560]{2,1,0:T(8,128)(2,1)}), bf16[16,8,2560]{2,1,0:T(8,128)(2,1)S(1)}, u32[]{:S(2)}, u32[]{:S(2)}) async-start(bf16[16,8,2560]{2,1,0:T(8,128)(2,1)} %bitcast.10), calls=%async_computation.3 | async-start | bytes 1310720 | tf_op jit(solution)/shard_map/all_to_all | solution.py:286
  138.8 2.9 %collective-permute-start.7 = (bf16[128,2560]{1,0:T(8,128)(2,1)S(1)}, bf16[128,2560]{1,0:T(8,128)(2,1)S(1)}, u32[]{:S(2)}, u32[]{:S(2)}) collective-permute-start(bf16[128,2560]{1,0:T(8,128)(2,1)S(1)} %bitcast.16), channel_id=1, source_target_pairs={{0,36},{4,32},{32,4},{36,0},{1,37},{5,33},{33,5},{37,1},{2,38},{6,... | collective-permute-start | bytes 1966088 | tf_op jit(solution)/shard_map/ppermute | solution.py:210
  141.6 2.8 %collective-permute-start.6 = (bf16[128,2560]{1,0:T(8,128)(2,1)S(1)}, bf16[128,2560]{1,0:T(8,128)(2,1)S(1)}, u32[]{:S(2)}, u32[]{:S(2)}) collective-permute-start(bf16[128,2560]{1,0:T(8,128)(2,1)S(1)} %bitcast.17), channel_id=1, source_target_pairs={{0,32},{4,36},{32,0},{36,4},{1,33},{5,37},{33,1},{37,5},{2,34},{6,... | collective-permute-start | bytes 1966088 | tf_op jit(solution)/shard_map/ppermute | solution.py:210
  144.4 2.7 %collective-permute-start.5 = (bf16[128,2560]{1,0:T(8,128)(2,1)S(1)}, bf16[128,2560]{1,0:T(8,128)(2,1)S(1)}, u32[]{:S(2)}, u32[]{:S(2)}) collective-permute-start(bf16[128,2560]{1,0:T(8,128)(2,1)S(1)} %bitcast.18), channel_id=1, source_target_pairs={{0,4},{4,0},{32,36},{36,32},{1,5},{5,1},{33,37},{37,33},{2,6},{6,2... | collective-permute-start | bytes 1966088 | tf_op jit(solution)/shard_map/ppermute | solution.py:210
  147.2 22.9 %collective-permute-done.7.w3_ref = bf16[128,2560]{1,0:T(8,128)(2,1)S(1)} collective-permute-done((bf16[128,2560]{1,0:T(8,128)(2,1)S(1)}, bf16[128,2560]{1,0:T(8,128)(2,1)S(1)}, u32[]{:S(2)}, u32[]{:S(2)}) %collective-permute-start.7) | collective-permute-done | bytes 655392 | tf_op jit(solution)/shard_map/ppermute | solution.py:210
  170.1 13.5 %collective-permute-done.6.w2_ref = bf16[128,2560]{1,0:T(8,128)(2,1)S(1)} collective-permute-done((bf16[128,2560]{1,0:T(8,128)(2,1)S(1)}, bf16[128,2560]{1,0:T(8,128)(2,1)S(1)}, u32[]{:S(2)}, u32[]{:S(2)}) %collective-permute-start.6) | collective-permute-done | bytes 655392 | tf_op jit(solution)/shard_map/ppermute | solution.py:210
  183.6 1.6 collective-permute-done.5.w1_ref
  185.2 0.0 copy-done.2
  185.2 3.0 %shard_map.82 = bf16[128,2048]{1,0:T(8,128)(2,1)} custom-call(s32[4]{0:T(128)S(1)} %iota_xor_fusion.who_ref, bf16[4,160,128]{2,1,0:T(8,128)(2,1)} %shard_map.81.grad_ref, bf16[128,2560]{1,0:T(8,128)(2,1)S(1)} %bitcast.19, bf16[128,2560]{1,0:T(8,128)(2,1)S(1)} %collective-permute-done.5.w1_ref, bf16[128,2560]{1,0:T(8,128)(2,1)S(1)} %collective-permute-done.6.w2_ref, ...), custom_call_target="tpu_custom_call" | custom-call | tf_op jit(solution)/shard_map/pallas_call | solution.py:287
  188.3 0.0 all-to-all-done.3
  188.3 0.1 convert_reduce_fusion
  188.4 0.7 broadcast_in_dim.14
  (10 shorter events, 0.1 us)
Async XLA Ops:
  2.2 21.4 %copy-start = (bf16[1,128,2048]{2,1,0:T(8,128)(2,1)S(1)}, bf16[1,128,2048]{2,1,0:T(8,128)(2,1)}, u32[]{:S(2)}) copy-start(bf16[1,128,2048]{2,1,0:T(8,128)(2,1)} %param.6) | copy-start | bytes 1572868
  3.1 63.4 %all-to-all-start = ((bf16[16,8,2560]{2,1,0:T(8,128)(2,1)}), bf16[16,8,2560]{2,1,0:T(8,128)(2,1)S(1)}, u32[]{:S(2)}, u32[]{:S(2)}) async-start(bf16[16,8,2560]{2,1,0:T(8,128)(2,1)} %broadcast_in_dim.12), calls=%async_computation | async-start | bytes 1310720 | tf_op jit(solution)/shard_map/all_to_all | solution.py:233
  23.6 31.7 %collective-permute-start.2 = (bf16[128,2048]{1,0:T(8,128)(2,1)S(1)}, bf16[128,2048]{1,0:T(8,128)(2,1)S(1)}, u32[]{:S(2)}, u32[]{:S(2)}) collective-permute-start(bf16[128,2048]{1,0:T(8,128)(2,1)S(1)} %bitcast.20), channel_id=1, source_target_pairs={{0,36},{4,32},{32,4},{36,0},{1,37},{5,33},{33,5},{37,1},{2,38},{6,... | collective-permute-start | bytes 1572872 | tf_op jit(solution)/shard_map/ppermute | solution.py:210
  27.6 37.9 %collective-permute-start.1 = (bf16[128,2048]{1,0:T(8,128)(2,1)S(1)}, bf16[128,2048]{1,0:T(8,128)(2,1)S(1)}, u32[]{:S(2)}, u32[]{:S(2)}) collective-permute-start(bf16[128,2048]{1,0:T(8,128)(2,1)S(1)} %bitcast.21), channel_id=1, source_target_pairs={{0,32},{4,36},{32,0},{36,4},{1,33},{5,37},{33,1},{37,5},{2,34},{6,... | collective-permute-start | bytes 1572872 | tf_op jit(solution)/shard_map/ppermute | solution.py:210
  30.7 35.8 %collective-permute-start = (bf16[128,2048]{1,0:T(8,128)(2,1)S(1)}, bf16[128,2048]{1,0:T(8,128)(2,1)S(1)}, u32[]{:S(2)}, u32[]{:S(2)}) collective-permute-start(bf16[128,2048]{1,0:T(8,128)(2,1)S(1)} %bitcast.22), channel_id=1, source_target_pairs={{0,4},{4,0},{32,36},{36,32},{1,5},{5,1},{33,37},{37,33},{2,6},{6,2... | collective-permute-start | bytes 1572872 | tf_op jit(solution)/shard_map/ppermute | solution.py:210
  68.5 21.8 %copy-start.4 = (f32[1,32]{1,0:T(1,128)S(1)}, f32[1,32]{1,0:T(1,128)}, u32[]{:S(2)}) copy-start(f32[1,32]{1,0:T(1,128)} %rate_ref.1) | copy-start | bytes 388
  68.5 21.9 %copy-start.5 = (f32[1,32]{1,0:T(1,128)S(1)}, f32[1,32]{1,0:T(1,128)}, u32[]{:S(2)}) copy-start(f32[1,32]{1,0:T(1,128)} %bias_ref.1) | copy-start | bytes 388
  68.5 36.5 %copy-start.3 = (f32[1,32]{1,0:T(1,128)S(1)}, f32[1,32]{1,0:T(1,128)}, u32[]{:S(2)}) copy-start(f32[1,32]{1,0:T(1,128)} %gain_ref.1) | copy-start | bytes 388
  68.5 10.7 %all-to-all-start.1 = ((f32[4,160,128]{2,1,0:T(8,128)}), f32[4,160,128]{2,1,0:T(8,128)}, u32[]{:S(2)}, u32[]{:S(2)}) async-start(f32[4,160,128]{2,1,0:T(8,128)} %shard_map.77), calls=%async_computation.1 | async-start | bytes 655360 | tf_op jit(solution)/shard_map/all_to_all | solution.py:245
  73.4 31.6 %collective-permute-start.4 = (bf16[1,128,2048]{2,1,0:T(8,128)(2,1)}, bf16[1,128,2048]{2,1,0:T(8,128)(2,1)S(1)}, u32[]{:S(2)}, u32[]{:S(2)}) collective-permute-start(bf16[1,128,2048]{2,1,0:T(8,128)(2,1)} %param.7), channel_id=1, source_target_pairs={{0,768},{256,0},{512,256},{768,512},{1,769},{257,1},{513,257},{769... | collective-permute-start | bytes 1572872 | tf_op jit(solution)/shard_map/ppermute | solution.py:227
  80.3 11.6 %collective-permute-start.3 = (f32[160,128]{1,0:T(8,128)S(1)}, f32[160,128]{1,0:T(8,128)S(1)}, u32[]{:S(2)}, u32[]{:S(2)}) collective-permute-start(f32[160,128]{1,0:T(8,128)S(1)} %reduce_sum.18), channel_id=1, source_target_pairs={{0,0},{1,4},{2,32},{3,36},{4,5},{5,1},{6,37},{7,33},{32,34},{33,38... | collective-permute-start | bytes 245768 | tf_op jit(solution)/shard_map/ppermute | solution.py:246
  110.8 1.0 copy-start.1
  119.1 8.3 %all-to-all-start.2 = ((bf16[4,160,128]{2,1,0:T(8,128)(2,1)}), bf16[4,160,128]{2,1,0:T(8,128)(2,1)S(1)}, u32[]{:S(2)}, u32[]{:S(2)}) async-start(bf16[4,160,128]{2,1,0:T(8,128)(2,1)} %shard_map.81.grad_ref), calls=%async_computation.2 | async-start | bytes 327680 | tf_op jit(solution)/shard_map/all_to_all | solution.py:278
  130.0 55.2 %copy-start.2 = (f32[128,2048]{1,0:T(8,128)S(1)}, f32[128,2048]{1,0:T(8,128)}, u32[]{:S(2)}) copy-start(f32[128,2048]{1,0:T(8,128)} %copy-done.1) | copy-start | bytes 3145732
  130.0 58.2 %all-to-all-start.3 = ((bf16[16,8,2560]{2,1,0:T(8,128)(2,1)}), bf16[16,8,2560]{2,1,0:T(8,128)(2,1)S(1)}, u32[]{:S(2)}, u32[]{:S(2)}) async-start(bf16[16,8,2560]{2,1,0:T(8,128)(2,1)} %bitcast.10), calls=%async_computation.3 | async-start | bytes 1310720 | tf_op jit(solution)/shard_map/all_to_all | solution.py:286
  138.8 31.3 %collective-permute-start.7 = (bf16[128,2560]{1,0:T(8,128)(2,1)S(1)}, bf16[128,2560]{1,0:T(8,128)(2,1)S(1)}, u32[]{:S(2)}, u32[]{:S(2)}) collective-permute-start(bf16[128,2560]{1,0:T(8,128)(2,1)S(1)} %bitcast.16), channel_id=1, source_target_pairs={{0,36},{4,32},{32,4},{36,0},{1,37},{5,33},{33,5},{37,1},{2,38},{6,... | collective-permute-start | bytes 1966088 | tf_op jit(solution)/shard_map/ppermute | solution.py:210
  141.6 42.0 %collective-permute-start.6 = (bf16[128,2560]{1,0:T(8,128)(2,1)S(1)}, bf16[128,2560]{1,0:T(8,128)(2,1)S(1)}, u32[]{:S(2)}, u32[]{:S(2)}) collective-permute-start(bf16[128,2560]{1,0:T(8,128)(2,1)S(1)} %bitcast.17), channel_id=1, source_target_pairs={{0,32},{4,36},{32,0},{36,4},{1,33},{5,37},{33,1},{37,5},{2,34},{6,... | collective-permute-start | bytes 1966088 | tf_op jit(solution)/shard_map/ppermute | solution.py:210
  144.4 40.8 %collective-permute-start.5 = (bf16[128,2560]{1,0:T(8,128)(2,1)S(1)}, bf16[128,2560]{1,0:T(8,128)(2,1)S(1)}, u32[]{:S(2)}, u32[]{:S(2)}) collective-permute-start(bf16[128,2560]{1,0:T(8,128)(2,1)S(1)} %bitcast.18), channel_id=1, source_target_pairs={{0,4},{4,0},{32,36},{36,32},{1,5},{5,1},{33,37},{37,33},{2,6},{6,2... | collective-permute-start | bytes 1966088 | tf_op jit(solution)/shard_map/ppermute | solution.py:210

commit v6 on v5

--- a/solution.py
+++ b/solution.py
@@ -39,6 +39,36 @@
 def natural(side, m, f):
     half = side // 2
     return 10 * ((2 * (f // half) + m // 2) * side + 2 * (f % half) + m % 2)
+
+
+def shard_kernel(w_ref, out_ref, row_ref):
+    copies, _, _ = out_ref.shape
+    inner = w_ref.shape[1]
+    quarter = inner // 4
+    w = w_ref[...].astype(F32)
+    row_ref[:, :inner] = w[:8, :]
+    for c in range(2):
+        for q in range(4):
+            row_ref[4 * c + q : 4 * c + q + 1, inner:] = w[
+                8 + c : 9 + c, q * quarter : (q + 1) * quarter
+            ]
+    row = row_ref[...].astype(BF16)
+    for i in range(copies):
+        out_ref[i] = row
+
+
+def total_kernel(piece_ref, out_ref):
+    count, _, wide = piece_ref.shape
+    blocks = wide // 160
+    inner = blocks * 128
+    total = piece_ref[0].astype(F32)
+    for i in range(1, count):
+        total = total + piece_ref[i].astype(F32)
+    for b in range(blocks):
+        out_ref[pl.ds(b, 8, blocks), :] = total[:, 128 * b : 128 * b + 128]
+    for b in range(blocks // 4):
+        at = inner + 128 * b
+        out_ref[pl.ds(8 * blocks + b, 8, blocks // 4), :] = total[:, at : at + 128]
 
 
 def project_kernel(w_ref, x0_ref, x1_ref, x2_ref, x3_ref, out_ref, tail_ref):
@@ -228,11 +258,13 @@
     rates = call(rate_kernel, jax.ShapeDtypeStruct((heads, t), F32), inputs=1)(log_rate)
     biases = call(bias_kernel, jax.ShapeDtypeStruct((heads, t), F32), inputs=1)(step_bias)
 
-    w = proj_weight[0].T
-    shard = jnp.concatenate([w[:8], w[8:].reshape(8, inner // 4)], axis=1)
-    weight = lax.all_to_all(
-        jnp.broadcast_to(shard[None], (far, 8, wide)), FAR, 0, 0
-    ).reshape(far * 8, wide)
+    spread_shard = call(
+        shard_kernel,
+        jax.ShapeDtypeStruct((far, 8, wide), BF16),
+        scratch=[pltpu.VMEM((8, wide), F32)],
+        inputs=1,
+    )(proj_weight[0].T)
+    weight = lax.all_to_all(spread_shard, FAR, 0, 0).reshape(far * 8, wide)
     diagonal = from_near(weight, 3)
     weights = [weight, from_near(weight, 1), from_near(weight, 2), diagonal]
 
@@ -291,9 +323,11 @@
         smem=(0,),
         inputs=7,
     )(who, send, *weights, gx)
-    total = pieces.astype(F32).sum(axis=0)
-    wgrad = jnp.concatenate([total[:, :inner], total[:, inner:].reshape(2, inner)], axis=0)
-    return (grad_inputs[None], wgrad.T[None])
+    wgrad = call(
+        total_kernel, jax.ShapeDtypeStruct((10 * inner // 128, 128), F32), inputs=1
+    )(pieces)
+    wgrad = wgrad.reshape(10, inner // 128, 128).transpose(1, 2, 0).reshape(inner, 10)
+    return (grad_inputs[None], wgrad[None])
 
 
 def solution(mesh):

time: 190 us -> 190 us (level)
    unnamed x12 -> x14, local copies, waits for them, and re-layouts: 1 us -> 3.7 us
where the time goes in v6:
time: 190 us; the launch traced here: 189 us
  waiting for transfers between devices  79.9 us (42%)
  starting transfers between devices  67.8 us (36%)
  blocking collectives  19.4 us (10%)
  Pallas kernels  16.4 us (9%)
  local copies, waits for them, and re-layouts  3.7 us (2%)
    ppermute x6, waiting for transfers between devices, from_near(): lax.ppermute(value, NEAR, [(m, m ^ r) for m in range(lax.axis_size(NEAR))])  71.9 us
    all_to_all x1, starting transfers between devices, per_device(): weight = lax.all_to_all(spread_shard, FAR, 0, 0).reshape(far * 8, wide)  20.6 us
    ppermute x6, starting transfers between devices, from_near(): lax.ppermute(value, NEAR, [(m, m ^ r) for m in range(lax.axis_size(NEAR))])  17.4 us
    all_gather x1, blocking collectives, per_device(): proj = lax.all_gather(own, 'tp', axis=0)  13.2 us
    ppermute x1, starting transfers between devices, per_device(): lax.ppermute(share, NEAR + ('tp',), [(m * tps + k, (m ^ k) * tps + m) for...  10.1 us
    all_to_all x1, starting transfers between devices, per_device(): pieces = lax.all_to_all(contrib.reshape(far, 8, wide), FAR, 0, 0)  8.71 us
    all_gather x1, blocking collectives, per_device(): packs = lax.all_gather(pack, 'tp', axis=0)  6.19 us
    pallas_call x1, Pallas kernels, per_device(): call(functools.partial(core_kernel, side), (jax.ShapeDtypeStruct((t + hea...  5.81 us
  transfers between devices with their start and end apart: 12, of which 9 were waited for; matrix products, arithmetic and copies ran while one was open for 1% of the time, Pallas kernels for 2%

profile of v6, /device:TPU:65, one launch (start us, length us, event | category | flops | bytes accessed | tf_op | source)
XLA Modules:
  0.0 189.0 jit_solution(2843352190747721687)
XLA Ops:
  0.6 0.0 copy-start.3
  0.6 0.8 copy-done.3
  1.5 0.9 shard_map.77
  2.4 0.0 copy-start
  2.4 20.6 %all-to-all-start = ((bf16[16,8,2560]{2,1,0:T(8,128)(2,1)}), bf16[16,8,2560]{2,1,0:T(8,128)(2,1)S(1)}, u32[]{:S(2)}, u32[]{:S(2)}) async-start(bf16[16,8,2560]{2,1,0:T(8,128)(2,1)} %shard_map.77), calls=%async_computation | async-start | bytes 1310720 | tf_op jit(solution)/shard_map/all_to_all | solution.py:267
  23.0 0.0 copy-done
  23.0 4.0 %collective-permute-start.2 = (bf16[128,2048]{1,0:T(8,128)(2,1)S(1)}, bf16[128,2048]{1,0:T(8,128)(2,1)S(1)}, u32[]{:S(2)}, u32[]{:S(2)}) collective-permute-start(bf16[128,2048]{1,0:T(8,128)(2,1)S(1)} %bitcast.21), channel_id=1, source_target_pairs={{0,36},{4,32},{32,4},{36,0},{1,37},{5,33},{33,5},{37,1},{2,38},{6,... | collective-permute-start | bytes 1572872 | tf_op jit(solution)/shard_map/ppermute | solution.py:240
  27.1 3.1 %collective-permute-start.1 = (bf16[128,2048]{1,0:T(8,128)(2,1)S(1)}, bf16[128,2048]{1,0:T(8,128)(2,1)S(1)}, u32[]{:S(2)}, u32[]{:S(2)}) collective-permute-start(bf16[128,2048]{1,0:T(8,128)(2,1)S(1)} %bitcast.22), channel_id=1, source_target_pairs={{0,32},{4,36},{32,0},{36,4},{1,33},{5,37},{33,1},{37,5},{2,34},{6,... | collective-permute-start | bytes 1572872 | tf_op jit(solution)/shard_map/ppermute | solution.py:240
  30.2 1.9 %collective-permute-start = (bf16[128,2048]{1,0:T(8,128)(2,1)S(1)}, bf16[128,2048]{1,0:T(8,128)(2,1)S(1)}, u32[]{:S(2)}, u32[]{:S(2)}) collective-permute-start(bf16[128,2048]{1,0:T(8,128)(2,1)S(1)} %bitcast.23), channel_id=1, source_target_pairs={{0,4},{4,0},{32,36},{36,32},{1,5},{5,1},{33,37},{37,33},{2,6},{6,2... | collective-permute-start | bytes 1572872 | tf_op jit(solution)/shard_map/ppermute | solution.py:240
  32.1 22.7 %collective-permute-done.2.x3_ref = bf16[128,2048]{1,0:T(8,128)(2,1)S(1)} collective-permute-done((bf16[128,2048]{1,0:T(8,128)(2,1)S(1)}, bf16[128,2048]{1,0:T(8,128)(2,1)S(1)}, u32[]{:S(2)}, u32[]{:S(2)}) %collective-permute-start.2) | collective-permute-done | bytes 524320 | tf_op jit(solution)/shard_map/ppermute | solution.py:240
  54.8 10.2 %collective-permute-done.1.x2_ref = bf16[128,2048]{1,0:T(8,128)(2,1)S(1)} collective-permute-done((bf16[128,2048]{1,0:T(8,128)(2,1)S(1)}, bf16[128,2048]{1,0:T(8,128)(2,1)S(1)}, u32[]{:S(2)}, u32[]{:S(2)}) %collective-permute-start.1) | collective-permute-done | bytes 524320 | tf_op jit(solution)/shard_map/ppermute | solution.py:240
  65.0 1.0 collective-permute-done.x1_ref
  66.0 0.0 all-to-all-done
  66.0 2.0 %shard_map.78 = f32[4,160,128]{2,1,0:T(8,128)} custom-call(bf16[128,2560]{1,0:T(8,128)(2,1)S(1)} %bitcast.16, bf16[128,2048]{1,0:T(8,128)(2,1)S(1)} %bitcast.24, bf16[128,2048]{1,0:T(8,128)(2,1)S(1)} %collective-permute-done.x1_ref, bf16[128,2048]{1,0:T(8,128)(2,1)S(1)} %collective-permute-done.1.x2_ref, bf16[128,2048]{1,0:T(8,128)(2,1)S(1)} %collective-permute-done.2.x3_ref), custom_call_target="tpu_custom_call" | custom-call | tf_op jit(solution)/shard_map/pallas_call | solution.py:271
  68.0 4.7 %all-to-all-start.1 = ((f32[4,160,128]{2,1,0:T(8,128)}), f32[4,160,128]{2,1,0:T(8,128)}, u32[]{:S(2)}, u32[]{:S(2)}) async-start(f32[4,160,128]{2,1,0:T(8,128)} %shard_map.78), calls=%async_computation.1 | async-start | bytes 655360 | tf_op jit(solution)/shard_map/all_to_all | solution.py:277
  72.7 1.9 %collective-permute-start.4 = (bf16[1,128,2048]{2,1,0:T(8,128)(2,1)}, bf16[1,128,2048]{2,1,0:T(8,128)(2,1)S(1)}, u32[]{:S(2)}, u32[]{:S(2)}) collective-permute-start(bf16[1,128,2048]{2,1,0:T(8,128)(2,1)} %param.7), channel_id=1, source_target_pairs={{0,768},{256,0},{512,256},{768,512},{1,769},{257,1},{513,257},{769... | collective-permute-start | bytes 1572872 | tf_op jit(solution)/shard_map/ppermute | solution.py:257
  74.6 3.9 %all-to-all-done.1 = f32[4,160,128]{2,1,0:T(8,128)} async-done(((f32[4,160,128]{2,1,0:T(8,128)}), f32[4,160,128]{2,1,0:T(8,128)}, u32[]{:S(2)}, u32[]{:S(2)}) %all-to-all-start.1) | async-done | bytes 327712 | tf_op jit(solution)/shard_map/all_to_all | solution.py:277
  78.6 1.0 reduce_sum.9
  79.6 10.1 %collective-permute-start.3 = (f32[160,128]{1,0:T(8,128)S(1)}, f32[160,128]{1,0:T(8,128)S(1)}, u32[]{:S(2)}, u32[]{:S(2)}) collective-permute-start(f32[160,128]{1,0:T(8,128)S(1)} %reduce_sum.9), channel_id=1, source_target_pairs={{0,0},{1,4},{2,32},{3,36},{4,5},{5,1},{6,37},{7,33},{32,34},{33,38... | collective-permute-start | bytes 245768 | tf_op jit(solution)/shard_map/ppermute | solution.py:278
  89.7 0.0 copy-start.5
  89.7 0.6 copy-done.5
  90.3 0.0 copy-start.6
  90.3 0.1 shard_map.79.rate_ref
  90.4 0.6 copy-done.6
  91.0 0.1 shard_map.80.bias_ref
  91.1 0.1 collective-permute-done.3
  91.1 13.2 %all-gather = f32[640,128]{1,0:T(8,128)S(1)} all-gather(f32[160,128]{1,0:T(8,128)S(1)} %collective-permute-done.3), channel_id=2, replica_groups=mesh['pp'=4,'xh'=4,'xl'=2,'zh'=4,'zl'=2,'tp'=4] {'tp'}, dimensions={0}, use_global_device_ids=true | all-gather | bytes 409600 | tf_op jit(solution)/shard_map/all_gather | solution.py:283
  104.3 0.0 collective-permute-done.4
  104.3 0.7 copy-done.4
  105.0 5.8 %shard_map.81 = (f32[160,128]{1,0:T(8,128)S(1)}, f32[128,2048]{1,0:T(8,128)S(1)}, f32[640,128]{1,0:T(8,128)S(1)}) custom-call(s32[1]{0:T(128)} %bitcast.tp_ref, f32[1,32]{1,0:T(1,128)S(1)} %copy-done.4, f32[4,160,128]{2,1,0:T(8,128)S(1)} %bitcast.28, f32[32,128]{1,0:T(8,128)S(1)} %shard_map.79.rate_ref, f32[32,128]{1,0:T(8,128)S(1)} %shard_map.80.bias_ref, ...), custom_call_target="tpu_custom_call" | custom-call | tf_op jit(solution)/shard_map/pallas_call | solution.py:285
  110.8 0.0 copy-start.1
  110.8 1.0 copy-done.1
  111.8 6.2 %all-gather.1 = f32[640,128]{1,0:T(8,128)S(1)} all-gather(f32[160,128]{1,0:T(8,128)S(1)} %get-tuple-element.5), channel_id=3, replica_groups=mesh['pp'=4,'xh'=4,'xl'=2,'zh'=4,'zl'=2,'tp'=4] {'tp'}, dimensions={0}, use_global_device_ids=true | all-gather | bytes 409600 | tf_op jit(solution)/shard_map/all_gather | solution.py:303
  118.0 1.1 shard_map.82.grad_ref
  119.1 4.3 %all-to-all-start.2 = ((bf16[4,160,128]{2,1,0:T(8,128)(2,1)}), bf16[4,160,128]{2,1,0:T(8,128)(2,1)S(1)}, u32[]{:S(2)}, u32[]{:S(2)}) async-start(bf16[4,160,128]{2,1,0:T(8,128)(2,1)} %shard_map.82.grad_ref), calls=%async_computation.2 | async-start | bytes 327680 | tf_op jit(solution)/shard_map/all_to_all | solution.py:310
  123.4 4.0 %all-to-all-done.2.grad_ref = bf16[4,160,128]{2,1,0:T(8,128)(2,1)S(1)} async-done(((bf16[4,160,128]{2,1,0:T(8,128)(2,1)}), bf16[4,160,128]{2,1,0:T(8,128)(2,1)S(1)}, u32[]{:S(2)}, u32[]{:S(2)}) %all-to-all-start.2) | async-done | bytes 163872 | tf_op jit(solution)/shard_map/all_to_all | solution.py:310
  127.4 2.7 %shard_map.84 = bf16[128,2560]{1,0:T(8,128)(2,1)} custom-call(s32[4]{0:T(128)S(1)} %iota_xor_fusion.who_ref, bf16[4,160,128]{2,1,0:T(8,128)(2,1)S(1)} %all-to-all-done.2.grad_ref, bf16[128,2048]{1,0:T(8,128)(2,1)S(1)} %bitcast.26, bf16[128,2048]{1,0:T(8,128)(2,1)S(1)} %collective-permute-done.x1_ref, bf16[128,2048]{1,0:T(8,128)(2,1)S(1)} %collective-permute-done.1.x2_ref, ...), custom_call_target="tpu_custom_call" | custom-call | tf_op jit(solution)/shard_map/pallas_call | solution.py:311
  130.0 8.7 %all-to-all-start.3 = ((bf16[16,8,2560]{2,1,0:T(8,128)(2,1)}), bf16[16,8,2560]{2,1,0:T(8,128)(2,1)S(1)}, u32[]{:S(2)}, u32[]{:S(2)}) async-start(bf16[16,8,2560]{2,1,0:T(8,128)(2,1)} %bitcast.9), calls=%async_computation.3 | async-start | bytes 1310720 | tf_op jit(solution)/shard_map/all_to_all | solution.py:318
  138.7 2.9 %collective-permute-start.7 = (bf16[128,2560]{1,0:T(8,128)(2,1)S(1)}, bf16[128,2560]{1,0:T(8,128)(2,1)S(1)}, u32[]{:S(2)}, u32[]{:S(2)}) collective-permute-start(bf16[128,2560]{1,0:T(8,128)(2,1)S(1)} %bitcast.17), channel_id=1, source_target_pairs={{0,36},{4,32},{32,4},{36,0},{1,37},{5,33},{33,5},{37,1},{2,38},{6,... | collective-permute-start | bytes 1966088 | tf_op jit(solution)/shard_map/ppermute | solution.py:240
  141.6 2.8 %collective-permute-start.6 = (bf16[128,2560]{1,0:T(8,128)(2,1)S(1)}, bf16[128,2560]{1,0:T(8,128)(2,1)S(1)}, u32[]{:S(2)}, u32[]{:S(2)}) collective-permute-start(bf16[128,2560]{1,0:T(8,128)(2,1)S(1)} %bitcast.18), channel_id=1, source_target_pairs={{0,32},{4,36},{32,0},{36,4},{1,33},{5,37},{33,1},{37,5},{2,34},{6,... | collective-permute-start | bytes 1966088 | tf_op jit(solution)/shard_map/ppermute | solution.py:240
  144.4 2.7 %collective-permute-start.5 = (bf16[128,2560]{1,0:T(8,128)(2,1)S(1)}, bf16[128,2560]{1,0:T(8,128)(2,1)S(1)}, u32[]{:S(2)}, u32[]{:S(2)}) collective-permute-start(bf16[128,2560]{1,0:T(8,128)(2,1)S(1)} %bitcast.19), channel_id=1, source_target_pairs={{0,4},{4,0},{32,36},{36,32},{1,5},{5,1},{33,37},{37,33},{2,6},{6,2... | collective-permute-start | bytes 1966088 | tf_op jit(solution)/shard_map/ppermute | solution.py:240
  147.1 22.9 %collective-permute-done.7.w3_ref = bf16[128,2560]{1,0:T(8,128)(2,1)S(1)} collective-permute-done((bf16[128,2560]{1,0:T(8,128)(2,1)S(1)}, bf16[128,2560]{1,0:T(8,128)(2,1)S(1)}, u32[]{:S(2)}, u32[]{:S(2)}) %collective-permute-start.7) | collective-permute-done | bytes 655392 | tf_op jit(solution)/shard_map/ppermute | solution.py:240
  170.0 13.5 %collective-permute-done.6.w2_ref = bf16[128,2560]{1,0:T(8,128)(2,1)S(1)} collective-permute-done((bf16[128,2560]{1,0:T(8,128)(2,1)S(1)}, bf16[128,2560]{1,0:T(8,128)(2,1)S(1)}, u32[]{:S(2)}, u32[]{:S(2)}) %collective-permute-start.6) | collective-permute-done | bytes 655392 | tf_op jit(solution)/shard_map/ppermute | solution.py:240
  183.6 1.6 collective-permute-done.5.w1_ref
  185.2 0.0 copy-done.2
  185.2 3.0 %shard_map.83 = bf16[128,2048]{1,0:T(8,128)(2,1)} custom-call(s32[4]{0:T(128)S(1)} %iota_xor_fusion.who_ref, bf16[4,160,128]{2,1,0:T(8,128)(2,1)} %shard_map.82.grad_ref, bf16[128,2560]{1,0:T(8,128)(2,1)S(1)} %bitcast.20, bf16[128,2560]{1,0:T(8,128)(2,1)S(1)} %collective-permute-done.5.w1_ref, bf16[128,2560]{1,0:T(8,128)(2,1)S(1)} %collective-permute-done.6.w2_ref, ...), custom_call_target="tpu_custom_call" | custom-call | tf_op jit(solution)/shard_map/pallas_call | solution.py:319
  188.2 0.0 all-to-all-done.3.piece_ref
  188.2 0.7 shard_map.85
  (3 shorter events, 0.0 us)
Async XLA Ops:
  0.6 0.8 copy-start.3
  2.4 20.6 %copy-start = (bf16[1,128,2048]{2,1,0:T(8,128)(2,1)S(1)}, bf16[1,128,2048]{2,1,0:T(8,128)(2,1)}, u32[]{:S(2)}) copy-start(bf16[1,128,2048]{2,1,0:T(8,128)(2,1)} %param.6) | copy-start | bytes 1572868
  2.4 63.6 %all-to-all-start = ((bf16[16,8,2560]{2,1,0:T(8,128)(2,1)}), bf16[16,8,2560]{2,1,0:T(8,128)(2,1)S(1)}, u32[]{:S(2)}, u32[]{:S(2)}) async-start(bf16[16,8,2560]{2,1,0:T(8,128)(2,1)} %shard_map.77), calls=%async_computation | async-start | bytes 1310720 | tf_op jit(solution)/shard_map/all_to_all | solution.py:267
  23.0 31.7 %collective-permute-start.2 = (bf16[128,2048]{1,0:T(8,128)(2,1)S(1)}, bf16[128,2048]{1,0:T(8,128)(2,1)S(1)}, u32[]{:S(2)}, u32[]{:S(2)}) collective-permute-start(bf16[128,2048]{1,0:T(8,128)(2,1)S(1)} %bitcast.21), channel_id=1, source_target_pairs={{0,36},{4,32},{32,4},{36,0},{1,37},{5,33},{33,5},{37,1},{2,38},{6,... | collective-permute-start | bytes 1572872 | tf_op jit(solution)/shard_map/ppermute | solution.py:240
  27.1 37.9 %collective-permute-start.1 = (bf16[128,2048]{1,0:T(8,128)(2,1)S(1)}, bf16[128,2048]{1,0:T(8,128)(2,1)S(1)}, u32[]{:S(2)}, u32[]{:S(2)}) collective-permute-start(bf16[128,2048]{1,0:T(8,128)(2,1)S(1)} %bitcast.22), channel_id=1, source_target_pairs={{0,32},{4,36},{32,0},{36,4},{1,33},{5,37},{33,1},{37,5},{2,34},{6,... | collective-permute-start | bytes 1572872 | tf_op jit(solution)/shard_map/ppermute | solution.py:240
  30.2 35.8 %collective-permute-start = (bf16[128,2048]{1,0:T(8,128)(2,1)S(1)}, bf16[128,2048]{1,0:T(8,128)(2,1)S(1)}, u32[]{:S(2)}, u32[]{:S(2)}) collective-permute-start(bf16[128,2048]{1,0:T(8,128)(2,1)S(1)} %bitcast.23), channel_id=1, source_target_pairs={{0,4},{4,0},{32,36},{36,32},{1,5},{5,1},{33,37},{37,33},{2,6},{6,2... | collective-permute-start | bytes 1572872 | tf_op jit(solution)/shard_map/ppermute | solution.py:240
  68.0 10.6 %all-to-all-start.1 = ((f32[4,160,128]{2,1,0:T(8,128)}), f32[4,160,128]{2,1,0:T(8,128)}, u32[]{:S(2)}, u32[]{:S(2)}) async-start(f32[4,160,128]{2,1,0:T(8,128)} %shard_map.78), calls=%async_computation.1 | async-start | bytes 655360 | tf_op jit(solution)/shard_map/all_to_all | solution.py:277
  72.7 31.6 %collective-permute-start.4 = (bf16[1,128,2048]{2,1,0:T(8,128)(2,1)}, bf16[1,128,2048]{2,1,0:T(8,128)(2,1)S(1)}, u32[]{:S(2)}, u32[]{:S(2)}) collective-permute-start(bf16[1,128,2048]{2,1,0:T(8,128)(2,1)} %param.7), channel_id=1, source_target_pairs={{0,768},{256,0},{512,256},{768,512},{1,769},{257,1},{513,257},{769... | collective-permute-start | bytes 1572872 | tf_op jit(solution)/shard_map/ppermute | solution.py:257
  79.6 11.6 %collective-permute-start.3 = (f32[160,128]{1,0:T(8,128)S(1)}, f32[160,128]{1,0:T(8,128)S(1)}, u32[]{:S(2)}, u32[]{:S(2)}) collective-permute-start(f32[160,128]{1,0:T(8,128)S(1)} %reduce_sum.9), channel_id=1, source_target_pairs={{0,0},{1,4},{2,32},{3,36},{4,5},{5,1},{6,37},{7,33},{32,34},{33,38... | collective-permute-start | bytes 245768 | tf_op jit(solution)/shard_map/ppermute | solution.py:278
  89.7 0.7 copy-start.5
  90.3 0.7 copy-start.6
  104.3 0.7 copy-start.4
  110.8 1.0 copy-start.1
  119.1 8.3 %all-to-all-start.2 = ((bf16[4,160,128]{2,1,0:T(8,128)(2,1)}), bf16[4,160,128]{2,1,0:T(8,128)(2,1)S(1)}, u32[]{:S(2)}, u32[]{:S(2)}) async-start(bf16[4,160,128]{2,1,0:T(8,128)(2,1)} %shard_map.82.grad_ref), calls=%async_computation.2 | async-start | bytes 327680 | tf_op jit(solution)/shard_map/all_to_all | solution.py:310
  130.0 55.2 %copy-start.2 = (f32[128,2048]{1,0:T(8,128)S(1)}, f32[128,2048]{1,0:T(8,128)}, u32[]{:S(2)}) copy-start(f32[128,2048]{1,0:T(8,128)} %copy-done.1) | copy-start | bytes 3145732
  130.0 58.2 %all-to-all-start.3 = ((bf16[16,8,2560]{2,1,0:T(8,128)(2,1)}), bf16[16,8,2560]{2,1,0:T(8,128)(2,1)S(1)}, u32[]{:S(2)}, u32[]{:S(2)}) async-start(bf16[16,8,2560]{2,1,0:T(8,128)(2,1)} %bitcast.9), calls=%async_computation.3 | async-start | bytes 1310720 | tf_op jit(solution)/shard_map/all_to_all | solution.py:318
  138.7 31.3 %collective-permute-start.7 = (bf16[128,2560]{1,0:T(8,128)(2,1)S(1)}, bf16[128,2560]{1,0:T(8,128)(2,1)S(1)}, u32[]{:S(2)}, u32[]{:S(2)}) collective-permute-start(bf16[128,2560]{1,0:T(8,128)(2,1)S(1)} %bitcast.17), channel_id=1, source_target_pairs={{0,36},{4,32},{32,4},{36,0},{1,37},{5,33},{33,5},{37,1},{2,38},{6,... | collective-permute-start | bytes 1966088 | tf_op jit(solution)/shard_map/ppermute | solution.py:240
  141.6 42.0 %collective-permute-start.6 = (bf16[128,2560]{1,0:T(8,128)(2,1)S(1)}, bf16[128,2560]{1,0:T(8,128)(2,1)S(1)}, u32[]{:S(2)}, u32[]{:S(2)}) collective-permute-start(bf16[128,2560]{1,0:T(8,128)(2,1)S(1)} %bitcast.18), channel_id=1, source_target_pairs={{0,32},{4,36},{32,0},{36,4},{1,33},{5,37},{33,1},{37,5},{2,34},{6,... | collective-permute-start | bytes 1966088 | tf_op jit(solution)/shard_map/ppermute | solution.py:240
  144.4 40.8 %collective-permute-start.5 = (bf16[128,2560]{1,0:T(8,128)(2,1)S(1)}, bf16[128,2560]{1,0:T(8,128)(2,1)S(1)}, u32[]{:S(2)}, u32[]{:S(2)}) collective-permute-start(bf16[128,2560]{1,0:T(8,128)(2,1)S(1)} %bitcast.19), channel_id=1, source_target_pairs={{0,4},{4,0},{32,36},{36,32},{1,5},{5,1},{33,37},{37,33},{2,6},{6,2... | collective-permute-start | bytes 1966088 | tf_op jit(solution)/shard_map/ppermute | solution.py:240

commit v7 on v6

--- a/solution.py
+++ b/solution.py
@@ -71,18 +71,18 @@
         out_ref[pl.ds(8 * blocks + b, 8, blocks // 4), :] = total[:, at : at + 128]
 
 
-def project_kernel(w_ref, x0_ref, x1_ref, x2_ref, x3_ref, out_ref, tail_ref):
+def project_kernel(who_ref, w_ref, x0_ref, x1_ref, x2_ref, x3_ref, out_ref, tail_ref):
     far = w_ref.shape[0] // 8
     inner = x0_ref.shape[1]
     quarter = inner // 4
     for r, x_ref in enumerate((x0_ref, x1_ref, x2_ref, x3_ref)):
-        out_ref[r, : 8 * far, :] = dot(w_ref[:, :inner], x_ref[...], NT)
+        out_ref[who_ref[r], : 8 * far, :] = dot(w_ref[:, :inner], x_ref[...], NT)
         tail = None
         for q in range(4):
             tail_ref[r, q] = dot(w_ref[:, inner:], x_ref[:, q * quarter : (q + 1) * quarter], NT)
             part = tail_ref[r, q, pl.ds(q, 2 * far, 4), :]
             tail = part if tail is None else tail + part
-        out_ref[r, 8 * far :, :] = tail
+        out_ref[who_ref[r], 8 * far :, :] = tail
 
 
 def as_column(row):
@@ -91,20 +91,23 @@
     return jnp.sum(jnp.where(at, jnp.broadcast_to(row, (n, n)), 0.0), axis=1, keepdims=True)
 
 
-def bias_kernel(bias_ref, out_ref):
-    out_ref[...] = jnp.broadcast_to(as_column(bias_ref[...]), out_ref.shape)
-
-
-def rate_kernel(rate_ref, out_ref):
-    out_ref[...] = jnp.broadcast_to(as_column(jnp.exp(rate_ref[...])), out_ref.shape)
+def rate_kernel(rate_ref, bias_ref, gain_ref, out_ref, lanes_ref):
+    _, heads, t = out_ref.shape
+    out_ref[0] = jnp.broadcast_to(as_column(jnp.exp(rate_ref[...])), (heads, t))
+    out_ref[1] = jnp.broadcast_to(as_column(bias_ref[...]), (heads, t))
+    left = lax.broadcasted_iota(jnp.int32, (1, 2 * HEAD_DIM), 1) < HEAD_DIM
+    for k in range(heads // 2):
+        lanes_ref[:, 2 * HEAD_DIM * k : 2 * HEAD_DIM * (k + 1)] = jnp.where(
+            left, gain_ref[:, 2 * k : 2 * k + 1], gain_ref[:, 2 * k + 1 : 2 * k + 2]
+        )
 
 
 def core_kernel(
-    side, tp_ref, gain_ref, group_ref, rate_ref, bias_ref, g_ref, x_ref,
+    side, tp_ref, gain_ref, group_ref, head_ref, g_ref, x_ref,
     pack_ref, gx_ref, proj_ref,
     cum_ref, cols_ref, row_ref, col_ref, scores_ref,
 ):
-    heads = rate_ref.shape[0]
+    heads = head_ref.shape[1]
     t = g_ref.shape[0]
     near, rows, _ = group_ref.shape
     far = rows // 10
@@ -115,8 +118,8 @@
             last = 8 * far + 2 * f
             proj_ref[at + 8 : at + 10, :] = group_ref[m, last : last + 2, :]
     raw = proj_ref[pl.ds(pl.multiple_of(2 * STATE + tp_ref[0] * heads, heads), heads), :]
-    z = raw + bias_ref[...]
-    rate = rate_ref[...]
+    z = raw + head_ref[1]
+    rate = head_ref[0]
     step = jnp.maximum(z, 0.0) + jnp.log1p(jnp.exp(-jnp.abs(z)))
     first = lax.broadcasted_iota(jnp.int32, (t, t), 0)
     second = lax.broadcasted_iota(jnp.int32, (t, t), 1)
@@ -155,7 +158,7 @@
             row_ref[pl.ds(h, 1), :] = jnp.sum(stepped * scores_ref[...], axis=0, keepdims=True)
             moved += dot((decay * scores_ref[...]).astype(BF16), gs[a], NN)
         step_both = jnp.where(left, cols[:, heads : heads + 1], cols[:, heads + 1 : heads + 2])
-        gain = jnp.where(left, gain_ref[0, 2 * k], gain_ref[0, 2 * k + 1])
+        gain = gain_ref[:, lanes]
         up = g.astype(F32)
         gx_ref[:, lanes] = up + (moved * step_both + gain * up)
         cols_ref[...] = pltpu.roll(cols, t - 2, 1)
@@ -248,15 +251,20 @@
     near = lax.axis_size(NEAR)
     far = lax.axis_size(FAR)
     side = lax.axis_size(("xh", "xl"))
-    tps = lax.axis_size("tp")
     pcols = proj_weight.shape[2] * near * far
     rows = pcols // near
     wide = inner + 2 * inner // 8
     who = lax.axis_index(NEAR) ^ jnp.arange(near, dtype=jnp.int32)
     xs = [x] + [from_near(x, r) for r in range(1, near)]
     arrived = lax.ppermute(returned, "pp", [(i, (i - 1) % sections) for i in range(sections)])[0]
-    rates = call(rate_kernel, jax.ShapeDtypeStruct((heads, t), F32), inputs=1)(log_rate)
-    biases = call(bias_kernel, jax.ShapeDtypeStruct((heads, t), F32), inputs=1)(step_bias)
+    of_heads, gains = call(
+        rate_kernel,
+        (
+            jax.ShapeDtypeStruct((2, heads, t), F32),
+            jax.ShapeDtypeStruct((1, inner), F32),
+        ),
+        inputs=3,
+    )(log_rate, step_bias, skip_gain)
 
     spread_shard = call(
         shard_kernel,
@@ -265,21 +273,17 @@
         inputs=1,
     )(proj_weight[0].T)
     weight = lax.all_to_all(spread_shard, FAR, 0, 0).reshape(far * 8, wide)
-    diagonal = from_near(weight, 3)
-    weights = [weight, from_near(weight, 1), from_near(weight, 2), diagonal]
+    weights = [weight] + [from_near(weight, r) for r in range(1, near)]
 
     partial = call(
         project_kernel,
         jax.ShapeDtypeStruct((near, rows, t), F32),
         scratch=[pltpu.VMEM((near, 4, far * 8, t), F32)],
-        inputs=5,
-    )(weight, *xs)
-    share = lax.all_to_all(partial, "tp", 0, 0).sum(axis=0)
-    own = lax.ppermute(
-        share,
-        NEAR + ("tp",),
-        [(m * tps + k, (m ^ k) * tps + m) for m in range(near) for k in range(tps)],
-    )
+        smem=(0,),
+        inputs=6,
+    )(who, weight, *xs)
+    partial = lax.all_to_all(partial, NEAR, 0, 0)
+    own = lax.all_to_all(partial, "tp", 0, 0).sum(axis=0)
     proj = lax.all_gather(own, "tp", axis=0)
 
     pack, gx, proj = call(
@@ -296,9 +300,9 @@
             pltpu.VMEM((t, t), F32),
             pltpu.VMEM((t, t), F32),
         ],
-        smem=(0, 1),
-        inputs=7,
-    )(lax.axis_index("tp").reshape(1), skip_gain, proj, rates, biases, arrived, x)
+        smem=(0,),
+        inputs=6,
+    )(lax.axis_index("tp").reshape(1), gains, proj, of_heads, arrived, x)
 
     packs = lax.all_gather(pack, "tp", axis=0)
     send = call(

time: 190 us -> 196 us (1.032)
  the two profiles are of different devices: /device:TPU:65 before, /device:TPU:1 now
where the time goes in v7:
time: 196 us; the launch traced here: 195 us
  waiting for transfers between devices  72.3 us (37%)
  starting transfers between devices  59.4 us (30%)
  blocking collectives  45.6 us (23%)
  Pallas kernels  14.6 us (7%)
    ppermute x6, waiting for transfers between devices, from_near(): lax.ppermute(value, NEAR, [(m, m ^ r) for m in range(lax.axis_size(NEAR))])  72.3 us
    all_gather x1, blocking collectives, per_device(): proj = lax.all_gather(own, 'tp', axis=0)  23.5 us
    all_to_all x1, starting transfers between devices, per_device(): weight = lax.all_to_all(spread_shard, FAR, 0, 0).reshape(far * 8, wide)  21.5 us
    ppermute x6, starting transfers between devices, from_near(): lax.ppermute(value, NEAR, [(m, m ^ r) for m in range(lax.axis_size(NEAR))])  17.4 us
    all_to_all x1, blocking collectives, per_device(): partial = lax.all_to_all(partial, NEAR, 0, 0)  8.7 us
    all_to_all x1, starting transfers between devices, per_device(): pieces = lax.all_to_all(contrib.reshape(far, 8, wide), FAR, 0, 0)  8.04 us
    all_to_all x1, blocking collectives, per_device(): grads = lax.all_to_all(send, NEAR, 0, 0)  7.13 us
    ppermute x1, starting transfers between devices, per_device(): lax.ppermute(returned, 'pp', [(i, (i - 1) % sections) for i in range(sect...  6.55 us
  transfers between devices with their start and end apart: 10, of which 6 were waited for; matrix products, arithmetic and copies ran while one was open for 1% of the time, Pallas kernels for 1%

profile of v7, /device:TPU:1, one launch (start us, length us, event | category | flops | bytes accessed | tf_op | source)
XLA Modules:
  0.0 195.2 jit_solution(18297564142752673366)
XLA Ops:
  0.6 0.0 copy-start.3
  0.6 0.8 copy-done.3
  1.5 0.9 shard_map.78
  2.4 0.0 copy-start
  2.4 21.5 %all-to-all-start = ((bf16[16,8,2560]{2,1,0:T(8,128)(2,1)}), bf16[16,8,2560]{2,1,0:T(8,128)(2,1)S(1)}, u32[]{:S(2)}, u32[]{:S(2)}) async-start(bf16[16,8,2560]{2,1,0:T(8,128)(2,1)} %shard_map.78), calls=%async_computation | async-start | bytes 1310720 | tf_op jit(solution)/shard_map/all_to_all | solution.py:275
  23.8 0.0 copy-done
  23.9 4.0 %collective-permute-start.2 = (bf16[128,2048]{1,0:T(8,128)(2,1)S(1)}, bf16[128,2048]{1,0:T(8,128)(2,1)S(1)}, u32[]{:S(2)}, u32[]{:S(2)}) collective-permute-start(bf16[128,2048]{1,0:T(8,128)(2,1)S(1)} %bitcast.21), channel_id=1, source_target_pairs={{0,36},{4,32},{32,4},{36,0},{1,37},{5,33},{33,5},{37,1},{2,38},{6,... | collective-permute-start | bytes 1572872 | tf_op jit(solution)/shard_map/ppermute | solution.py:243
  27.9 3.1 %collective-permute-start.1 = (bf16[128,2048]{1,0:T(8,128)(2,1)S(1)}, bf16[128,2048]{1,0:T(8,128)(2,1)S(1)}, u32[]{:S(2)}, u32[]{:S(2)}) collective-permute-start(bf16[128,2048]{1,0:T(8,128)(2,1)S(1)} %bitcast.22), channel_id=1, source_target_pairs={{0,32},{4,36},{32,0},{36,4},{1,33},{5,37},{33,1},{37,5},{2,34},{6,... | collective-permute-start | bytes 1572872 | tf_op jit(solution)/shard_map/ppermute | solution.py:243
  31.0 1.9 collective-permute-start
  32.9 22.7 %collective-permute-done.2.x3_ref = bf16[128,2048]{1,0:T(8,128)(2,1)S(1)} collective-permute-done((bf16[128,2048]{1,0:T(8,128)(2,1)S(1)}, bf16[128,2048]{1,0:T(8,128)(2,1)S(1)}, u32[]{:S(2)}, u32[]{:S(2)}) %collective-permute-start.2) | collective-permute-done | bytes 524320 | tf_op jit(solution)/shard_map/ppermute | solution.py:243
  55.6 10.2 %collective-permute-done.1.x2_ref = bf16[128,2048]{1,0:T(8,128)(2,1)S(1)} collective-permute-done((bf16[128,2048]{1,0:T(8,128)(2,1)S(1)}, bf16[128,2048]{1,0:T(8,128)(2,1)S(1)}, u32[]{:S(2)}, u32[]{:S(2)}) %collective-permute-start.1) | collective-permute-done | bytes 524320 | tf_op jit(solution)/shard_map/ppermute | solution.py:243
  65.8 1.0 collective-permute-done.x1_ref
  66.8 0.0 all-to-all-done
  66.8 1.8 shard_map.79
  68.6 8.7 %all_to_all.25 = f32[4,160,128]{2,1,0:T(8,128)} all-to-all(f32[4,160,128]{2,1,0:T(8,128)S(1)} %shard_map.79), channel_id=1, replica_groups=mesh['pp'=4,'xh'=4,'xl'=2,'zh'=4,'zl'=2,'tp'=4] {'xl','zl'}, dimensions={0} | all-to-all | bytes 655360 | tf_op jit(solution)/shard_map/all_to_all | solution.py:285
  77.3 6.0 %all-to-all-start.2 = ((f32[4,160,128]{2,1,0:T(8,128)}), f32[4,160,128]{2,1,0:T(8,128)}, u32[]{:S(2)}, u32[]{:S(2)}) async-start(f32[4,160,128]{2,1,0:T(8,128)} %all_to_all.25), calls=%async_computation.2 | async-start | bytes 655360 | tf_op jit(solution)/shard_map/all_to_all | solution.py:286
  83.3 6.6 %collective-permute-start.3 = (bf16[1,128,2048]{2,1,0:T(8,128)(2,1)}, bf16[1,128,2048]{2,1,0:T(8,128)(2,1)S(1)}, u32[]{:S(2)}, u32[]{:S(2)}) collective-permute-start(bf16[1,128,2048]{2,1,0:T(8,128)(2,1)} %param.7), channel_id=1, source_target_pairs={{0,768},{256,0},{512,256},{768,512},{1,769},{257,1},{513,257},{769... | collective-permute-start | bytes 1572872 | tf_op jit(solution)/shard_map/ppermute | solution.py:259
  89.8 0.0 copy-start.4
  89.8 0.0 copy-start.5
  89.8 0.0 copy-start.6
  89.9 0.6 copy-done.4
  90.5 0.0 copy-done.5
  90.5 0.0 copy-done.6
  90.5 0.2 shard_map.77
  90.7 0.0 all-to-all-done.2
  90.7 1.0 reduce_sum.9
  91.7 23.5 %all-gather = f32[640,128]{1,0:T(8,128)S(1)} all-gather(f32[160,128]{1,0:T(8,128)S(1)} %reduce_sum.9), channel_id=2, replica_groups=mesh['pp'=4,'xh'=4,'xl'=2,'zh'=4,'zl'=2,'tp'=4] {'tp'}, dimensions={0}, use_global_device_ids=true | all-gather | bytes 409600 | tf_op jit(solution)/shard_map/all_gather | solution.py:287
  115.2 0.0 collective-permute-done.3
  115.2 5.3 %shard_map.80 = (f32[160,128]{1,0:T(8,128)S(1)}, f32[128,2048]{1,0:T(8,128)S(1)}, f32[640,128]{1,0:T(8,128)S(1)}) custom-call(s32[1]{0:T(128)} %bitcast.tp_ref, f32[1,2048]{1,0:T(1,128)S(1)} %get-tuple-element.7.gain_ref, f32[4,160,128]{2,1,0:T(8,128)S(1)} %bitcast.27, f32[2,32,128]{2,1,0:T(8,128)S(1)} %get-tuple-element.8.head_ref, ...), custom_call_target="tpu_custom_call" | custom-call | tf_op jit(solution)/shard_map/pallas_call | solution.py:289
  120.5 0.0 copy-start.1
  120.5 6.2 %all-gather.1 = f32[640,128]{1,0:T(8,128)S(1)} all-gather(f32[160,128]{1,0:T(8,128)S(1)} %get-tuple-element.9), channel_id=3, replica_groups=mesh['pp'=4,'xh'=4,'xl'=2,'zh'=4,'zl'=2,'tp'=4] {'tp'}, dimensions={0}, use_global_device_ids=true | all-gather | bytes 409600 | tf_op jit(solution)/shard_map/all_gather | solution.py:307
  126.7 0.4 shard_map.81.grad_ref
  127.1 0.0 copy-done.1
  127.2 7.1 %all_to_all.26.grad_ref = bf16[4,160,128]{2,1,0:T(8,128)(2,1)S(1)} all-to-all(bf16[4,160,128]{2,1,0:T(8,128)(2,1)S(1)} %shard_map.81.grad_ref), channel_id=1, replica_groups=mesh['pp'=4,'xh'=4,'xl'=2,'zh'=4,'zl'=2,'tp'=4] {'xl','zl'}, dimensions={0} | all-to-all | bytes 327680 | tf_op jit(solution)/shard_map/all_to_all | solution.py:314
  134.3 2.7 %shard_map.83 = bf16[128,2560]{1,0:T(8,128)(2,1)} custom-call(s32[4]{0:T(128)S(1)} %iota_xor_fusion.who_ref, bf16[4,160,128]{2,1,0:T(8,128)(2,1)S(1)} %all_to_all.26.grad_ref, bf16[128,2048]{1,0:T(8,128)(2,1)S(1)} %bitcast.26, bf16[128,2048]{1,0:T(8,128)(2,1)S(1)} %collective-permute-done.x1_ref, bf16[128,2048]{1,0:T(8,128)(2,1)S(1)} %collective-permute-done.1.x2_ref, ...), custom_call_target="tpu_custom_call" | custom-call | tf_op jit(solution)/shard_map/pallas_call | solution.py:315
  136.9 0.0 copy-start.2
  136.9 8.0 %all-to-all-start.4 = ((bf16[16,8,2560]{2,1,0:T(8,128)(2,1)}), bf16[16,8,2560]{2,1,0:T(8,128)(2,1)S(1)}, u32[]{:S(2)}, u32[]{:S(2)}) async-start(bf16[16,8,2560]{2,1,0:T(8,128)(2,1)} %bitcast.9), calls=%async_computation.4 | async-start | bytes 1310720 | tf_op jit(solution)/shard_map/all_to_all | solution.py:322
  145.0 2.4 %collective-permute-start.6 = (bf16[128,2560]{1,0:T(8,128)(2,1)S(1)}, bf16[128,2560]{1,0:T(8,128)(2,1)S(1)}, u32[]{:S(2)}, u32[]{:S(2)}) collective-permute-start(bf16[128,2560]{1,0:T(8,128)(2,1)S(1)} %bitcast.17), channel_id=1, source_target_pairs={{0,36},{4,32},{32,4},{36,0},{1,37},{5,33},{33,5},{37,1},{2,38},{6,... | collective-permute-start | bytes 1966088 | tf_op jit(solution)/shard_map/ppermute | solution.py:243
  147.4 3.1 %collective-permute-start.5 = (bf16[128,2560]{1,0:T(8,128)(2,1)S(1)}, bf16[128,2560]{1,0:T(8,128)(2,1)S(1)}, u32[]{:S(2)}, u32[]{:S(2)}) collective-permute-start(bf16[128,2560]{1,0:T(8,128)(2,1)S(1)} %bitcast.18), channel_id=1, source_target_pairs={{0,32},{4,36},{32,0},{36,4},{1,33},{5,37},{33,1},{37,5},{2,34},{6,... | collective-permute-start | bytes 1966088 | tf_op jit(solution)/shard_map/ppermute | solution.py:243
  150.5 2.9 %collective-permute-start.4 = (bf16[128,2560]{1,0:T(8,128)(2,1)S(1)}, bf16[128,2560]{1,0:T(8,128)(2,1)S(1)}, u32[]{:S(2)}, u32[]{:S(2)}) collective-permute-start(bf16[128,2560]{1,0:T(8,128)(2,1)S(1)} %bitcast.19), channel_id=1, source_target_pairs={{0,4},{4,0},{32,36},{36,32},{1,5},{5,1},{33,37},{37,33},{2,6},{6,2... | collective-permute-start | bytes 1966088 | tf_op jit(solution)/shard_map/ppermute | solution.py:243
  153.4 23.8 %collective-permute-done.6.w3_ref = bf16[128,2560]{1,0:T(8,128)(2,1)S(1)} collective-permute-done((bf16[128,2560]{1,0:T(8,128)(2,1)S(1)}, bf16[128,2560]{1,0:T(8,128)(2,1)S(1)}, u32[]{:S(2)}, u32[]{:S(2)}) %collective-permute-start.6) | collective-permute-done | bytes 655392 | tf_op jit(solution)/shard_map/ppermute | solution.py:243
  177.2 13.6 %collective-permute-done.5.w2_ref = bf16[128,2560]{1,0:T(8,128)(2,1)S(1)} collective-permute-done((bf16[128,2560]{1,0:T(8,128)(2,1)S(1)}, bf16[128,2560]{1,0:T(8,128)(2,1)S(1)}, u32[]{:S(2)}, u32[]{:S(2)}) %collective-permute-start.5) | collective-permute-done | bytes 655392 | tf_op jit(solution)/shard_map/ppermute | solution.py:243
  190.8 1.0 collective-permute-done.4.w1_ref
  191.8 0.0 copy-done.2
  191.8 2.7 %shard_map.82 = bf16[128,2048]{1,0:T(8,128)(2,1)} custom-call(s32[4]{0:T(128)S(1)} %iota_xor_fusion.who_ref, bf16[4,160,128]{2,1,0:T(8,128)(2,1)S(1)} %shard_map.81.grad_ref, bf16[128,2560]{1,0:T(8,128)(2,1)S(1)} %bitcast.20, bf16[128,2560]{1,0:T(8,128)(2,1)S(1)} %collective-permute-done.4.w1_ref, bf16[128,2560]{1,0:T(8,128)(2,1)S(1)} %collective-permute-done.5.w2_ref, ...), custom_call_target="tpu_custom_call" | custom-call | tf_op jit(solution)/shard_map/pallas_call | solution.py:323
  194.5 0.0 all-to-all-done.4.piece_ref
  194.5 0.7 shard_map.84
  (1 shorter events, 0.0 us)
Async XLA Ops:
  0.6 0.8 copy-start.3
  2.4 21.5 %copy-start = (bf16[1,128,2048]{2,1,0:T(8,128)(2,1)S(1)}, bf16[1,128,2048]{2,1,0:T(8,128)(2,1)}, u32[]{:S(2)}) copy-start(bf16[1,128,2048]{2,1,0:T(8,128)(2,1)} %param.6) | copy-start | bytes 1572868
  2.4 64.4 %all-to-all-start = ((bf16[16,8,2560]{2,1,0:T(8,128)(2,1)}), bf16[16,8,2560]{2,1,0:T(8,128)(2,1)S(1)}, u32[]{:S(2)}, u32[]{:S(2)}) async-start(bf16[16,8,2560]{2,1,0:T(8,128)(2,1)} %shard_map.78), calls=%async_computation | async-start | bytes 1310720 | tf_op jit(solution)/shard_map/all_to_all | solution.py:275
  23.9 31.7 %collective-permute-start.2 = (bf16[128,2048]{1,0:T(8,128)(2,1)S(1)}, bf16[128,2048]{1,0:T(8,128)(2,1)S(1)}, u32[]{:S(2)}, u32[]{:S(2)}) collective-permute-start(bf16[128,2048]{1,0:T(8,128)(2,1)S(1)} %bitcast.21), channel_id=1, source_target_pairs={{0,36},{4,32},{32,4},{36,0},{1,37},{5,33},{33,5},{37,1},{2,38},{6,... | collective-permute-start | bytes 1572872 | tf_op jit(solution)/shard_map/ppermute | solution.py:243
  27.9 37.9 %collective-permute-start.1 = (bf16[128,2048]{1,0:T(8,128)(2,1)S(1)}, bf16[128,2048]{1,0:T(8,128)(2,1)S(1)}, u32[]{:S(2)}, u32[]{:S(2)}) collective-permute-start(bf16[128,2048]{1,0:T(8,128)(2,1)S(1)} %bitcast.22), channel_id=1, source_target_pairs={{0,32},{4,36},{32,0},{36,4},{1,33},{5,37},{33,1},{37,5},{2,34},{6,... | collective-permute-start | bytes 1572872 | tf_op jit(solution)/shard_map/ppermute | solution.py:243
  31.0 35.8 %collective-permute-start = (bf16[128,2048]{1,0:T(8,128)(2,1)S(1)}, bf16[128,2048]{1,0:T(8,128)(2,1)S(1)}, u32[]{:S(2)}, u32[]{:S(2)}) collective-permute-start(bf16[128,2048]{1,0:T(8,128)(2,1)S(1)} %bitcast.23), channel_id=1, source_target_pairs={{0,4},{4,0},{32,36},{36,32},{1,5},{5,1},{33,37},{37,33},{2,6},{6,2... | collective-permute-start | bytes 1572872 | tf_op jit(solution)/shard_map/ppermute | solution.py:243
  77.3 13.4 %all-to-all-start.2 = ((f32[4,160,128]{2,1,0:T(8,128)}), f32[4,160,128]{2,1,0:T(8,128)}, u32[]{:S(2)}, u32[]{:S(2)}) async-start(f32[4,160,128]{2,1,0:T(8,128)} %all_to_all.25), calls=%async_computation.2 | async-start | bytes 655360 | tf_op jit(solution)/shard_map/all_to_all | solution.py:286
  83.3 32.0 %collective-permute-start.3 = (bf16[1,128,2048]{2,1,0:T(8,128)(2,1)}, bf16[1,128,2048]{2,1,0:T(8,128)(2,1)S(1)}, u32[]{:S(2)}, u32[]{:S(2)}) collective-permute-start(bf16[1,128,2048]{2,1,0:T(8,128)(2,1)} %param.7), channel_id=1, source_target_pairs={{0,768},{256,0},{512,256},{768,512},{1,769},{257,1},{513,257},{769... | collective-permute-start | bytes 1572872 | tf_op jit(solution)/shard_map/ppermute | solution.py:259
  89.8 0.7 copy-start.4
  89.8 0.7 copy-start.5
  89.8 0.7 copy-start.6
  120.5 6.6 %copy-start.1 = (f32[128,2048]{1,0:T(8,128)}, f32[128,2048]{1,0:T(8,128)S(1)}, u32[]{:S(2)}) copy-start(f32[128,2048]{1,0:T(8,128)S(1)} %get-tuple-element.11.gx_ref) | copy-start | bytes 3145732
  136.9 54.9 %copy-start.2 = (f32[128,2048]{1,0:T(8,128)S(1)}, f32[128,2048]{1,0:T(8,128)}, u32[]{:S(2)}) copy-start(f32[128,2048]{1,0:T(8,128)} %copy-done.1) | copy-start | bytes 3145732
  136.9 57.5 %all-to-all-start.4 = ((bf16[16,8,2560]{2,1,0:T(8,128)(2,1)}), bf16[16,8,2560]{2,1,0:T(8,128)(2,1)S(1)}, u32[]{:S(2)}, u32[]{:S(2)}) async-start(bf16[16,8,2560]{2,1,0:T(8,128)(2,1)} %bitcast.9), calls=%async_computation.4 | async-start | bytes 1310720 | tf_op jit(solution)/shard_map/all_to_all | solution.py:322
  145.0 32.2 %collective-permute-start.6 = (bf16[128,2560]{1,0:T(8,128)(2,1)S(1)}, bf16[128,2560]{1,0:T(8,128)(2,1)S(1)}, u32[]{:S(2)}, u32[]{:S(2)}) collective-permute-start(bf16[128,2560]{1,0:T(8,128)(2,1)S(1)} %bitcast.17), channel_id=1, source_target_pairs={{0,36},{4,32},{32,4},{36,0},{1,37},{5,33},{33,5},{37,1},{2,38},{6,... | collective-permute-start | bytes 1966088 | tf_op jit(solution)/shard_map/ppermute | solution.py:243
  147.4 43.4 %collective-permute-start.5 = (bf16[128,2560]{1,0:T(8,128)(2,1)S(1)}, bf16[128,2560]{1,0:T(8,128)(2,1)S(1)}, u32[]{:S(2)}, u32[]{:S(2)}) collective-permute-start(bf16[128,2560]{1,0:T(8,128)(2,1)S(1)} %bitcast.18), channel_id=1, source_target_pairs={{0,32},{4,36},{32,0},{36,4},{1,33},{5,37},{33,1},{37,5},{2,34},{6,... | collective-permute-start | bytes 1966088 | tf_op jit(solution)/shard_map/ppermute | solution.py:243
  150.5 41.3 %collective-permute-start.4 = (bf16[128,2560]{1,0:T(8,128)(2,1)S(1)}, bf16[128,2560]{1,0:T(8,128)(2,1)S(1)}, u32[]{:S(2)}, u32[]{:S(2)}) collective-permute-start(bf16[128,2560]{1,0:T(8,128)(2,1)S(1)} %bitcast.19), channel_id=1, source_target_pairs={{0,4},{4,0},{32,36},{36,32},{1,5},{5,1},{33,37},{37,33},{2,6},{6,2... | collective-permute-start | bytes 1966088 | tf_op jit(solution)/shard_map/ppermute | solution.py:243

commit v8 on v7

--- a/solution.py
+++ b/solution.py
@@ -91,10 +91,14 @@
     return jnp.sum(jnp.where(at, jnp.broadcast_to(row, (n, n)), 0.0), axis=1, keepdims=True)
 
 
-def rate_kernel(rate_ref, bias_ref, gain_ref, out_ref, lanes_ref):
+def rate_kernel(rate_ref, bias_ref, out_ref):
     _, heads, t = out_ref.shape
     out_ref[0] = jnp.broadcast_to(as_column(jnp.exp(rate_ref[...])), (heads, t))
     out_ref[1] = jnp.broadcast_to(as_column(bias_ref[...]), (heads, t))
+
+
+def gain_kernel(gain_ref, lanes_ref):
+    heads = gain_ref.shape[1]
     left = lax.broadcasted_iota(jnp.int32, (1, 2 * HEAD_DIM), 1) < HEAD_DIM
     for k in range(heads // 2):
         lanes_ref[:, 2 * HEAD_DIM * k : 2 * HEAD_DIM * (k + 1)] = jnp.where(
@@ -257,14 +261,10 @@
     who = lax.axis_index(NEAR) ^ jnp.arange(near, dtype=jnp.int32)
     xs = [x] + [from_near(x, r) for r in range(1, near)]
     arrived = lax.ppermute(returned, "pp", [(i, (i - 1) % sections) for i in range(sections)])[0]
-    of_heads, gains = call(
-        rate_kernel,
-        (
-            jax.ShapeDtypeStruct((2, heads, t), F32),
-            jax.ShapeDtypeStruct((1, inner), F32),
-        ),
-        inputs=3,
-    )(log_rate, step_bias, skip_gain)
+    of_heads = call(
+        rate_kernel, jax.ShapeDtypeStruct((2, heads, t), F32), inputs=2
+    )(log_rate, step_bias)
+    gains = call(gain_kernel, jax.ShapeDtypeStruct((1, inner), F32), inputs=1)(skip_gain)
 
     spread_shard = call(
         shard_kernel,
@@ -273,7 +273,8 @@
         inputs=1,
     )(proj_weight[0].T)
     weight = lax.all_to_all(spread_shard, FAR, 0, 0).reshape(far * 8, wide)
-    weights = [weight] + [from_near(weight, r) for r in range(1, near)]
+    diagonal = from_near(weight, 3)
+    weights = [weight, from_near(weight, 1), from_near(weight, 2), diagonal]
 
     partial = call(
         project_kernel,

time: 196 us -> 196 us (level)
  no operation moved by 1% of the time
where the time goes in v8:
time: 196 us; the launch traced here: 195 us
  waiting for transfers between devices  72.3 us (37%)
  starting transfers between devices  59.4 us (30%)
  blocking collectives  45 us (23%)
  Pallas kernels  14.7 us (8%)
  local copies, waits for them, and re-layouts  2.05 us (1%)
    ppermute x6, waiting for transfers between devices, from_near(): lax.ppermute(value, NEAR, [(m, m ^ r) for m in range(lax.axis_size(NEAR))])  72.3 us
    all_gather x1, blocking collectives, per_device(): proj = lax.all_gather(own, 'tp', axis=0)  23 us
    all_to_all x1, starting transfers between devices, per_device(): weight = lax.all_to_all(spread_shard, FAR, 0, 0).reshape(far * 8, wide)  21.5 us
    ppermute x6, starting transfers between devices, from_near(): lax.ppermute(value, NEAR, [(m, m ^ r) for m in range(lax.axis_size(NEAR))])  17.4 us
    all_to_all x1, blocking collectives, per_device(): partial = lax.all_to_all(partial, NEAR, 0, 0)  8.71 us
    all_to_all x1, starting transfers between devices, per_device(): pieces = lax.all_to_all(contrib.reshape(far, 8, wide), FAR, 0, 0)  8.04 us
    all_to_all x1, blocking collectives, per_device(): grads = lax.all_to_all(send, NEAR, 0, 0)  7.13 us
    ppermute x1, starting transfers between devices, per_device(): lax.ppermute(returned, 'pp', [(i, (i - 1) % sections) for i in range(sect...  6.56 us
  transfers between devices with their start and end apart: 10, of which 6 were waited for; matrix products, arithmetic and copies ran while one was open for 1% of the time, Pallas kernels for 1%

profile of v8, /device:TPU:1, one launch (start us, length us, event | category | flops | bytes accessed | tf_op | source)
XLA Modules:
  0.0 195.2 jit_solution(7813854722633045235)
XLA Ops:
  0.6 0.0 copy-start.3
  0.6 0.8 copy-done.3
  1.5 0.9 shard_map.78
  2.4 0.0 copy-start
  2.4 21.5 %all-to-all-start = ((bf16[16,8,2560]{2,1,0:T(8,128)(2,1)}), bf16[16,8,2560]{2,1,0:T(8,128)(2,1)S(1)}, u32[]{:S(2)}, u32[]{:S(2)}) async-start(bf16[16,8,2560]{2,1,0:T(8,128)(2,1)} %shard_map.78), calls=%async_computation | async-start | bytes 1310720 | tf_op jit(solution)/shard_map/all_to_all | solution.py:275
  23.8 0.0 copy-done
  23.8 4.0 %collective-permute-start.2 = (bf16[128,2048]{1,0:T(8,128)(2,1)S(1)}, bf16[128,2048]{1,0:T(8,128)(2,1)S(1)}, u32[]{:S(2)}, u32[]{:S(2)}) collective-permute-start(bf16[128,2048]{1,0:T(8,128)(2,1)S(1)} %bitcast.21), channel_id=1, source_target_pairs={{0,36},{4,32},{32,4},{36,0},{1,37},{5,33},{33,5},{37,1},{2,38},{6,... | collective-permute-start | bytes 1572872 | tf_op jit(solution)/shard_map/ppermute | solution.py:247
  27.9 3.1 %collective-permute-start.1 = (bf16[128,2048]{1,0:T(8,128)(2,1)S(1)}, bf16[128,2048]{1,0:T(8,128)(2,1)S(1)}, u32[]{:S(2)}, u32[]{:S(2)}) collective-permute-start(bf16[128,2048]{1,0:T(8,128)(2,1)S(1)} %bitcast.22), channel_id=1, source_target_pairs={{0,32},{4,36},{32,0},{36,4},{1,33},{5,37},{33,1},{37,5},{2,34},{6,... | collective-permute-start | bytes 1572872 | tf_op jit(solution)/shard_map/ppermute | solution.py:247
  31.0 1.9 collective-permute-start
  32.9 22.7 %collective-permute-done.2.x3_ref = bf16[128,2048]{1,0:T(8,128)(2,1)S(1)} collective-permute-done((bf16[128,2048]{1,0:T(8,128)(2,1)S(1)}, bf16[128,2048]{1,0:T(8,128)(2,1)S(1)}, u32[]{:S(2)}, u32[]{:S(2)}) %collective-permute-start.2) | collective-permute-done | bytes 524320 | tf_op jit(solution)/shard_map/ppermute | solution.py:247
  55.6 10.2 %collective-permute-done.1.x2_ref = bf16[128,2048]{1,0:T(8,128)(2,1)S(1)} collective-permute-done((bf16[128,2048]{1,0:T(8,128)(2,1)S(1)}, bf16[128,2048]{1,0:T(8,128)(2,1)S(1)}, u32[]{:S(2)}, u32[]{:S(2)}) %collective-permute-start.1) | collective-permute-done | bytes 524320 | tf_op jit(solution)/shard_map/ppermute | solution.py:247
  65.8 1.0 collective-permute-done.x1_ref
  66.7 0.0 all-to-all-done
  66.7 1.8 shard_map.79
  68.6 8.7 %all_to_all.25 = f32[4,160,128]{2,1,0:T(8,128)} all-to-all(f32[4,160,128]{2,1,0:T(8,128)S(1)} %shard_map.79), channel_id=1, replica_groups=mesh['pp'=4,'xh'=4,'xl'=2,'zh'=4,'zl'=2,'tp'=4] {'xl','zl'}, dimensions={0} | all-to-all | bytes 655360 | tf_op jit(solution)/shard_map/all_to_all | solution.py:286
  77.3 6.0 %all-to-all-start.2 = ((f32[4,160,128]{2,1,0:T(8,128)}), f32[4,160,128]{2,1,0:T(8,128)}, u32[]{:S(2)}, u32[]{:S(2)}) async-start(f32[4,160,128]{2,1,0:T(8,128)} %all_to_all.25), calls=%async_computation.2 | async-start | bytes 655360 | tf_op jit(solution)/shard_map/all_to_all | solution.py:287
  83.3 6.6 %collective-permute-start.3 = (bf16[1,128,2048]{2,1,0:T(8,128)(2,1)}, bf16[1,128,2048]{2,1,0:T(8,128)(2,1)S(1)}, u32[]{:S(2)}, u32[]{:S(2)}) collective-permute-start(bf16[1,128,2048]{2,1,0:T(8,128)(2,1)} %param.7), channel_id=1, source_target_pairs={{0,768},{256,0},{512,256},{768,512},{1,769},{257,1},{513,257},{769... | collective-permute-start | bytes 1572872 | tf_op jit(solution)/shard_map/ppermute | solution.py:263
  89.8 0.0 copy-start.6
  89.8 0.6 copy-done.6
  90.5 0.0 copy-start.4
  90.5 0.0 copy-start.5
  90.5 0.1 shard_map.77.gain_ref
  90.6 0.5 copy-done.4
  91.2 0.0 copy-done.5
  91.2 0.1 shard_map.80.head_ref
  91.3 0.0 all-to-all-done.2
  91.3 1.0 reduce_sum.9
  92.3 23.0 %all-gather = f32[640,128]{1,0:T(8,128)S(1)} all-gather(f32[160,128]{1,0:T(8,128)S(1)} %reduce_sum.9), channel_id=2, replica_groups=mesh['pp'=4,'xh'=4,'xl'=2,'zh'=4,'zl'=2,'tp'=4] {'tp'}, dimensions={0}, use_global_device_ids=true | all-gather | bytes 409600 | tf_op jit(solution)/shard_map/all_gather | solution.py:288
  115.2 0.0 collective-permute-done.3
  115.2 5.3 %shard_map.81 = (f32[160,128]{1,0:T(8,128)S(1)}, f32[128,2048]{1,0:T(8,128)S(1)}, f32[640,128]{1,0:T(8,128)S(1)}) custom-call(s32[1]{0:T(128)} %bitcast.tp_ref, f32[1,2048]{1,0:T(1,128)S(1)} %shard_map.77.gain_ref, f32[4,160,128]{2,1,0:T(8,128)S(1)} %bitcast.27, f32[2,32,128]{2,1,0:T(8,128)S(1)} %shard_map.80.head_ref, bf16[128,2048]{1,0:T(8,128)(2,1)S(1)} %bitcast.29, ...), custom_call_target="tpu_custom_call" | custom-call | tf_op jit(solution)/shard_map/pallas_call | solution.py:290
  120.5 0.0 copy-start.1
  120.5 6.2 %all-gather.1 = f32[640,128]{1,0:T(8,128)S(1)} all-gather(f32[160,128]{1,0:T(8,128)S(1)} %get-tuple-element.5), channel_id=3, replica_groups=mesh['pp'=4,'xh'=4,'xl'=2,'zh'=4,'zl'=2,'tp'=4] {'tp'}, dimensions={0}, use_global_device_ids=true | all-gather | bytes 409600 | tf_op jit(solution)/shard_map/all_gather | solution.py:308
  126.8 0.4 shard_map.82.grad_ref
  127.2 0.0 copy-done.1
  127.2 7.1 %all_to_all.26.grad_ref = bf16[4,160,128]{2,1,0:T(8,128)(2,1)S(1)} all-to-all(bf16[4,160,128]{2,1,0:T(8,128)(2,1)S(1)} %shard_map.82.grad_ref), channel_id=1, replica_groups=mesh['pp'=4,'xh'=4,'xl'=2,'zh'=4,'zl'=2,'tp'=4] {'xl','zl'}, dimensions={0} | all-to-all | bytes 327680 | tf_op jit(solution)/shard_map/all_to_all | solution.py:315
  134.3 2.7 %shard_map.84 = bf16[128,2560]{1,0:T(8,128)(2,1)} custom-call(s32[4]{0:T(128)S(1)} %iota_xor_fusion.who_ref, bf16[4,160,128]{2,1,0:T(8,128)(2,1)S(1)} %all_to_all.26.grad_ref, bf16[128,2048]{1,0:T(8,128)(2,1)S(1)} %bitcast.26, bf16[128,2048]{1,0:T(8,128)(2,1)S(1)} %collective-permute-done.x1_ref, bf16[128,2048]{1,0:T(8,128)(2,1)S(1)} %collective-permute-done.1.x2_ref, ...), custom_call_target="tpu_custom_call" | custom-call | tf_op jit(solution)/shard_map/pallas_call | solution.py:316
  137.0 0.0 copy-start.2
  137.0 8.0 %all-to-all-start.4 = ((bf16[16,8,2560]{2,1,0:T(8,128)(2,1)}), bf16[16,8,2560]{2,1,0:T(8,128)(2,1)S(1)}, u32[]{:S(2)}, u32[]{:S(2)}) async-start(bf16[16,8,2560]{2,1,0:T(8,128)(2,1)} %bitcast.9), calls=%async_computation.4 | async-start | bytes 1310720 | tf_op jit(solution)/shard_map/all_to_all | solution.py:323
  145.0 2.4 %collective-permute-start.6 = (bf16[128,2560]{1,0:T(8,128)(2,1)S(1)}, bf16[128,2560]{1,0:T(8,128)(2,1)S(1)}, u32[]{:S(2)}, u32[]{:S(2)}) collective-permute-start(bf16[128,2560]{1,0:T(8,128)(2,1)S(1)} %bitcast.17), channel_id=1, source_target_pairs={{0,36},{4,32},{32,4},{36,0},{1,37},{5,33},{33,5},{37,1},{2,38},{6,... | collective-permute-start | bytes 1966088 | tf_op jit(solution)/shard_map/ppermute | solution.py:247
  147.4 3.1 %collective-permute-start.5 = (bf16[128,2560]{1,0:T(8,128)(2,1)S(1)}, bf16[128,2560]{1,0:T(8,128)(2,1)S(1)}, u32[]{:S(2)}, u32[]{:S(2)}) collective-permute-start(bf16[128,2560]{1,0:T(8,128)(2,1)S(1)} %bitcast.18), channel_id=1, source_target_pairs={{0,32},{4,36},{32,0},{36,4},{1,33},{5,37},{33,1},{37,5},{2,34},{6,... | collective-permute-start | bytes 1966088 | tf_op jit(solution)/shard_map/ppermute | solution.py:247
  150.5 2.9 %collective-permute-start.4 = (bf16[128,2560]{1,0:T(8,128)(2,1)S(1)}, bf16[128,2560]{1,0:T(8,128)(2,1)S(1)}, u32[]{:S(2)}, u32[]{:S(2)}) collective-permute-start(bf16[128,2560]{1,0:T(8,128)(2,1)S(1)} %bitcast.19), channel_id=1, source_target_pairs={{0,4},{4,0},{32,36},{36,32},{1,5},{5,1},{33,37},{37,33},{2,6},{6,2... | collective-permute-start | bytes 1966088 | tf_op jit(solution)/shard_map/ppermute | solution.py:247
  153.4 23.8 %collective-permute-done.6.w3_ref = bf16[128,2560]{1,0:T(8,128)(2,1)S(1)} collective-permute-done((bf16[128,2560]{1,0:T(8,128)(2,1)S(1)}, bf16[128,2560]{1,0:T(8,128)(2,1)S(1)}, u32[]{:S(2)}, u32[]{:S(2)}) %collective-permute-start.6) | collective-permute-done | bytes 655392 | tf_op jit(solution)/shard_map/ppermute | solution.py:247
  177.2 13.6 %collective-permute-done.5.w2_ref = bf16[128,2560]{1,0:T(8,128)(2,1)S(1)} collective-permute-done((bf16[128,2560]{1,0:T(8,128)(2,1)S(1)}, bf16[128,2560]{1,0:T(8,128)(2,1)S(1)}, u32[]{:S(2)}, u32[]{:S(2)}) %collective-permute-start.5) | collective-permute-done | bytes 655392 | tf_op jit(solution)/shard_map/ppermute | solution.py:247
  190.8 1.0 collective-permute-done.4.w1_ref
  191.8 0.0 copy-done.2
  191.8 2.7 %shard_map.83 = bf16[128,2048]{1,0:T(8,128)(2,1)} custom-call(s32[4]{0:T(128)S(1)} %iota_xor_fusion.who_ref, bf16[4,160,128]{2,1,0:T(8,128)(2,1)S(1)} %shard_map.82.grad_ref, bf16[128,2560]{1,0:T(8,128)(2,1)S(1)} %bitcast.20, bf16[128,2560]{1,0:T(8,128)(2,1)S(1)} %collective-permute-done.4.w1_ref, bf16[128,2560]{1,0:T(8,128)(2,1)S(1)} %collective-permute-done.5.w2_ref, ...), custom_call_target="tpu_custom_call" | custom-call | tf_op jit(solution)/shard_map/pallas_call | solution.py:324
  194.5 0.0 all-to-all-done.4.piece_ref
  194.5 0.7 shard_map.85
  (1 shorter events, 0.0 us)
Async XLA Ops:
  0.6 0.8 copy-start.3
  2.4 21.5 %copy-start = (bf16[1,128,2048]{2,1,0:T(8,128)(2,1)S(1)}, bf16[1,128,2048]{2,1,0:T(8,128)(2,1)}, u32[]{:S(2)}) copy-start(bf16[1,128,2048]{2,1,0:T(8,128)(2,1)} %param.6) | copy-start | bytes 1572868
  2.4 64.4 %all-to-all-start = ((bf16[16,8,2560]{2,1,0:T(8,128)(2,1)}), bf16[16,8,2560]{2,1,0:T(8,128)(2,1)S(1)}, u32[]{:S(2)}, u32[]{:S(2)}) async-start(bf16[16,8,2560]{2,1,0:T(8,128)(2,1)} %shard_map.78), calls=%async_computation | async-start | bytes 1310720 | tf_op jit(solution)/shard_map/all_to_all | solution.py:275
  23.8 31.7 %collective-permute-start.2 = (bf16[128,2048]{1,0:T(8,128)(2,1)S(1)}, bf16[128,2048]{1,0:T(8,128)(2,1)S(1)}, u32[]{:S(2)}, u32[]{:S(2)}) collective-permute-start(bf16[128,2048]{1,0:T(8,128)(2,1)S(1)} %bitcast.21), channel_id=1, source_target_pairs={{0,36},{4,32},{32,4},{36,0},{1,37},{5,33},{33,5},{37,1},{2,38},{6,... | collective-permute-start | bytes 1572872 | tf_op jit(solution)/shard_map/ppermute | solution.py:247
  27.9 37.9 %collective-permute-start.1 = (bf16[128,2048]{1,0:T(8,128)(2,1)S(1)}, bf16[128,2048]{1,0:T(8,128)(2,1)S(1)}, u32[]{:S(2)}, u32[]{:S(2)}) collective-permute-start(bf16[128,2048]{1,0:T(8,128)(2,1)S(1)} %bitcast.22), channel_id=1, source_target_pairs={{0,32},{4,36},{32,0},{36,4},{1,33},{5,37},{33,1},{37,5},{2,34},{6,... | collective-permute-start | bytes 1572872 | tf_op jit(solution)/shard_map/ppermute | solution.py:247
  31.0 35.8 %collective-permute-start = (bf16[128,2048]{1,0:T(8,128)(2,1)S(1)}, bf16[128,2048]{1,0:T(8,128)(2,1)S(1)}, u32[]{:S(2)}, u32[]{:S(2)}) collective-permute-start(bf16[128,2048]{1,0:T(8,128)(2,1)S(1)} %bitcast.23), channel_id=1, source_target_pairs={{0,4},{4,0},{32,36},{36,32},{1,5},{5,1},{33,37},{37,33},{2,6},{6,2... | collective-permute-start | bytes 1572872 | tf_op jit(solution)/shard_map/ppermute | solution.py:247
  77.3 14.0 %all-to-all-start.2 = ((f32[4,160,128]{2,1,0:T(8,128)}), f32[4,160,128]{2,1,0:T(8,128)}, u32[]{:S(2)}, u32[]{:S(2)}) async-start(f32[4,160,128]{2,1,0:T(8,128)} %all_to_all.25), calls=%async_computation.2 | async-start | bytes 655360 | tf_op jit(solution)/shard_map/all_to_all | solution.py:287
  83.3 32.0 %collective-permute-start.3 = (bf16[1,128,2048]{2,1,0:T(8,128)(2,1)}, bf16[1,128,2048]{2,1,0:T(8,128)(2,1)S(1)}, u32[]{:S(2)}, u32[]{:S(2)}) collective-permute-start(bf16[1,128,2048]{2,1,0:T(8,128)(2,1)} %param.7), channel_id=1, source_target_pairs={{0,768},{256,0},{512,256},{768,512},{1,769},{257,1},{513,257},{769... | collective-permute-start | bytes 1572872 | tf_op jit(solution)/shard_map/ppermute | solution.py:263
  89.8 0.7 copy-start.6
  90.5 0.7 copy-start.4
  90.5 0.7 copy-start.5
  120.5 6.6 %copy-start.1 = (f32[128,2048]{1,0:T(8,128)}, f32[128,2048]{1,0:T(8,128)S(1)}, u32[]{:S(2)}) copy-start(f32[128,2048]{1,0:T(8,128)S(1)} %get-tuple-element.7.gx_ref) | copy-start | bytes 3145732
  137.0 54.9 %copy-start.2 = (f32[128,2048]{1,0:T(8,128)S(1)}, f32[128,2048]{1,0:T(8,128)}, u32[]{:S(2)}) copy-start(f32[128,2048]{1,0:T(8,128)} %copy-done.1) | copy-start | bytes 3145732
  137.0 57.5 %all-to-all-start.4 = ((bf16[16,8,2560]{2,1,0:T(8,128)(2,1)}), bf16[16,8,2560]{2,1,0:T(8,128)(2,1)S(1)}, u32[]{:S(2)}, u32[]{:S(2)}) async-start(bf16[16,8,2560]{2,1,0:T(8,128)(2,1)} %bitcast.9), calls=%async_computation.4 | async-start | bytes 1310720 | tf_op jit(solution)/shard_map/all_to_all | solution.py:323
  145.0 32.2 %collective-permute-start.6 = (bf16[128,2560]{1,0:T(8,128)(2,1)S(1)}, bf16[128,2560]{1,0:T(8,128)(2,1)S(1)}, u32[]{:S(2)}, u32[]{:S(2)}) collective-permute-start(bf16[128,2560]{1,0:T(8,128)(2,1)S(1)} %bitcast.17), channel_id=1, source_target_pairs={{0,36},{4,32},{32,4},{36,0},{1,37},{5,33},{33,5},{37,1},{2,38},{6,... | collective-permute-start | bytes 1966088 | tf_op jit(solution)/shard_map/ppermute | solution.py:247
  147.4 43.4 %collective-permute-start.5 = (bf16[128,2560]{1,0:T(8,128)(2,1)S(1)}, bf16[128,2560]{1,0:T(8,128)(2,1)S(1)}, u32[]{:S(2)}, u32[]{:S(2)}) collective-permute-start(bf16[128,2560]{1,0:T(8,128)(2,1)S(1)} %bitcast.18), channel_id=1, source_target_pairs={{0,32},{4,36},{32,0},{36,4},{1,33},{5,37},{33,1},{37,5},{2,34},{6,... | collective-permute-start | bytes 1966088 | tf_op jit(solution)/shard_map/ppermute | solution.py:247
  150.5 41.3 %collective-permute-start.4 = (bf16[128,2560]{1,0:T(8,128)(2,1)S(1)}, bf16[128,2560]{1,0:T(8,128)(2,1)S(1)}, u32[]{:S(2)}, u32[]{:S(2)}) collective-permute-start(bf16[128,2560]{1,0:T(8,128)(2,1)S(1)} %bitcast.19), channel_id=1, source_target_pairs={{0,4},{4,0},{32,36},{36,32},{1,5},{5,1},{33,37},{37,33},{2,6},{6,2... | collective-permute-start | bytes 1966088 | tf_op jit(solution)/shard_map/ppermute | solution.py:247
